TPU v7x, 256 devices: a whole 4x4x8 slice. The times are simulated.
256 devices in a mesh: leaf: 64 (over z, y, core), off: 4 (over x).
Axes of the slice: x: 4, y: 4, z: 8, core: 2. Of those that a mesh axis runs over, the one named last changes fastest.
Arguments:
- multipoles: bfloat16 [65536, 488], P('leaf'), may hold values from -6 to 6
- kernels: bfloat16 [40, 488, 488], P('off'), may hold values from -0.0390625 to 0.0390625
- transfer: bfloat16 [8, 488, 488], replicated, may hold values from -0.09375 to 0.09375
- leaf_target: int32 [64, 40, 1024], P('leaf', 'off'), may hold values from 0 to 1023, as said below
- leaf_source: int32 [64, 40, 1024], P('leaf', 'off'), may hold values from 0 to 1407
- leaf_count: int32 [64, 40], P('leaf', 'off'), may hold values from 512 to 1024
- coarse_target: int32 [64, 40, 128], P('leaf', 'off'), may hold values from 0 to 127, as said below
- coarse_source: int32 [64, 40, 128], P('leaf', 'off'), may hold values from 0 to 223
- coarse_count: int32 [64, 40], P('leaf', 'off'), may hold values from 64 to 128
- ghost_send: int32 [64, 6, 64], P('leaf'), may hold values from 0 to 1343, as said below
- coarse_send: int32 [64, 6, 16], P('leaf'), may hold values from 0 to 207, as said below
Outputs:
- expansions: float32 [65536, 488], P(('leaf', 'off'))
Inputs may be any that keep to these rules, and one draw needn't show every extreme that they name: Per partition and class, leaf_target is a permutation of 0 to 1023. Per partition and class, coarse_target is a permutation of 0 to 127. `ghost_send`: in round b every index is below 1024 + b * 64. `coarse_send`: in round b every index is below 128 + b * 16.
All inputs are finite; a program needn't handle non-finite values.
Results may differ from a plain program's by a relative error of at most 0.0009.
Values may be sent and summed in bfloat16 or wider, within the bound.
A program may use at most 64 MiB of HBM per device.

v0:
```python
import functools

import jax
import jax.numpy as jnp
from jax import lax
from jax.experimental import pallas as pl
from jax.experimental.pallas import tpu as pltpu
from jax.sharding import PartitionSpec as P


def partner(block, axis, apart):
    count = lax.axis_size(axis)
    route = []
    for low in range(count):
        high = low | 1 << apart
        if high != low and high < count:
            route += [(low, high), (high, low)]
    return lax.ppermute(block, axis, route)


def invert_kernel(target_ref, payload_ref, out_ref):
    pairs = target_ref.shape[1]
    columns = jnp.transpose(target_ref[...])
    spots = lax.broadcasted_iota(jnp.int32, (pairs, pairs), 1)
    for c in range(payload_ref.shape[0]):
        hot = (columns[:, c:c + 1] == spots).astype(payload_ref.dtype)
        parts = jnp.dot(payload_ref[c], hot, preferred_element_type=jnp.float32)
        out_ref[c:c + 1, :] = (parts[0:1] * 64.0 + parts[1:2]).astype(jnp.int32)


def slot_table(target, source, pair_count, pad_row):
    classes, pairs = target.shape
    pair = lax.broadcasted_iota(jnp.int32, target.shape, 1)
    payload = jnp.where(pair < pair_count[:, None], source, pad_row)
    split = jnp.stack([payload // 64, payload % 64], axis=1).astype(jnp.bfloat16)
    split = jnp.pad(split, ((0, 0), (0, 6), (0, 0)))
    target = jnp.pad(target, ((0, 16 - classes), (0, 0)), constant_values=-1)
    return pl.pallas_call(
        invert_kernel,
        out_shape=jax.ShapeDtypeStruct((classes, pairs), jnp.int32),
        compiler_params=pltpu.CompilerParams(vmem_limit_bytes=48 * 1024 * 1024),
        cost_estimate=pl.CostEstimate(
            flops=2 * 8 * classes * pairs * pairs, bytes_accessed=24 * classes * pairs, transcendentals=0
        ),
    )(target, split)


def translate_kernel(spread, devices, slot_ref, buf_ref, k_ref, *rest):
    *rest, column_ref = rest
    if spread:
        high_ref, low_ref, t_ref, out_ref = rest
        nt = (((1,), (1,)), ((), ()))
        octants = t_ref.shape[0]
        span = high_ref.shape[0] // devices
        for h in range(octants):
            term = lax.dot_general(
                high_ref[...], t_ref[h], nt, preferred_element_type=jnp.float32
            ) + lax.dot_general(low_ref[...], t_ref[h], nt, preferred_element_type=jnp.float32)
            for d in range(devices):
                at = (d * octants + h) * span
                out_ref[at:at + span, :] = term[d * span:(d + 1) * span]
    else:
        (out_ref,) = rest
        out_ref[...] = jnp.zeros(out_ref.shape, out_ref.dtype)
    rows = buf_ref.shape[0]
    tile = out_ref.shape[0]
    columns = jnp.transpose(slot_ref[...])
    for c in range(k_ref.shape[0]):
        column_ref[c] = columns[:, c:c + 1]

    def one_class(c, carry):
        hot = (column_ref[c] == lax.broadcasted_iota(jnp.int32, (tile, rows), 1)).astype(
            buf_ref.dtype
        )
        picked = jnp.dot(hot, buf_ref[...], preferred_element_type=jnp.float32)
        out_ref[...] += jnp.dot(
            picked.astype(k_ref.dtype), k_ref[c], preferred_element_type=jnp.float32
        )
        return carry

    lax.fori_loop(0, k_ref.shape[0], one_class, 0)


def translate(slot, buffer, kernels, chunk, tile, spread=None, devices=1):
    classes = kernels.shape[0]
    rows, width = buffer.shape
    in_specs = [
        pl.BlockSpec((slot.shape[0], tile), lambda g: (0, chunk)),
        pl.BlockSpec((rows, width), lambda g: (0, 0)),
        pl.BlockSpec((classes, width, width), lambda g: (0, 0, 0)),
    ]
    operands = [slot, buffer, kernels]
    if spread is not None:
        high, low, transfer = spread
        octants = tile // high.shape[0]
        in_specs += [
            pl.BlockSpec(high.shape, lambda g: (0, 0)),
            pl.BlockSpec(low.shape, lambda g: (0, 0)),
            pl.BlockSpec((octants, width, width), lambda g: (chunk, 0, 0)),
        ]
        operands += [high, low, transfer]
    flops = 2 * classes * tile * width * (rows + width)
    return pl.pallas_call(
        functools.partial(translate_kernel, spread is not None, devices),
        grid=(1,),
        in_specs=in_specs,
        out_specs=pl.BlockSpec((tile, width), lambda g: (0, 0)),
        out_shape=jax.ShapeDtypeStruct((tile, width), jnp.float32),
        scratch_shapes=[pltpu.VMEM((slot.shape[0], tile, 1), jnp.int32)],
        compiler_params=pltpu.CompilerParams(vmem_limit_bytes=48 * 1024 * 1024),
        cost_estimate=pl.CostEstimate(
            flops=flops, bytes_accessed=2 * kernels.size + 2 * buffer.size, transcendentals=0
        ),
    )(*operands)


def on_device(
    multipoles,
    kernels,
    transfer,
    leaf_target,
    leaf_source,
    leaf_count,
    coarse_target,
    coarse_source,
    coarse_count,
    ghost_send,
    coarse_send,
):
    width = multipoles.shape[1]
    rounds = lax.axis_size("leaf").bit_length() - 1
    boxes = multipoles.shape[0]
    parents = boxes // 8
    classes = kernels.shape[0]
    leaf_ghost = ghost_send.shape[2]
    coarse_ghost = coarse_send.shape[2]
    leaf_rows = boxes + rounds * leaf_ghost
    coarse_rows = parents + rounds * coarse_ghost

    parent = jnp.dot(
        multipoles.reshape(-1, 8 * width),
        transfer.reshape(8 * width, width),
        preferred_element_type=jnp.float32,
    ).astype(jnp.bfloat16)

    coarse_slot = slot_table(coarse_target[0], coarse_source[0], coarse_count[0], coarse_rows)
    chunks = 4
    devices = lax.axis_size("off")
    span = parents // devices
    per = 8 // chunks
    coarse_slot = jnp.pad(coarse_slot, ((0, 16 - classes), (0, 0)), constant_values=coarse_rows)

    buffer = jnp.zeros((leaf_rows, width), multipoles.dtype)
    buffer = lax.dynamic_update_slice(buffer, multipoles, (0, 0))
    coarse_buffer = jnp.zeros((coarse_rows, width), parent.dtype)
    coarse_buffer = lax.dynamic_update_slice(coarse_buffer, parent, (0, 0))
    group = -(-classes // (rounds - 1))
    groups = [(low, min(low + group, classes)) for low in range(0, classes, group)]
    slot_parts = []
    for bit_index in range(rounds):
        outgoing = jnp.concatenate(
            [buffer[ghost_send[0, bit_index]], coarse_buffer[coarse_send[0, bit_index]]], axis=0
        )
        if bit_index < len(groups):
            low, high = groups[bit_index]
            tables, outgoing = lax.optimization_barrier(
                ((leaf_target[0, low:high], leaf_source[0, low:high], leaf_count[0, low:high]), outgoing)
            )
        arrived = partner(outgoing, "leaf", bit_index)
        if bit_index < len(groups):
            part, arrived = lax.optimization_barrier((slot_table(*tables, leaf_rows), arrived))
            slot_parts.append(part)
        buffer = lax.dynamic_update_slice(
            buffer, arrived[:leaf_ghost], (boxes + bit_index * leaf_ghost, 0)
        )
        coarse_buffer = lax.dynamic_update_slice(
            coarse_buffer, arrived[leaf_ghost:], (parents + bit_index * coarse_ghost, 0)
        )

    leaf_slot = jnp.concatenate(slot_parts, axis=0)
    leaf_slot = leaf_slot.reshape(classes, devices, span, chunks, per)
    leaf_slot = leaf_slot.transpose(0, 3, 1, 4, 2).reshape(classes, boxes)
    leaf_slot = jnp.pad(leaf_slot, ((0, 16 - classes), (0, 0)), constant_values=leaf_rows)
    coarse_local = 0.5 * translate(coarse_slot, coarse_buffer, kernels, 0, parents)
    coarse_high = coarse_local.astype(jnp.bfloat16)
    coarse_low = (coarse_local - coarse_high.astype(jnp.float32)).astype(jnp.bfloat16)
    tile = boxes // chunks
    block = tile // devices
    me = lax.axis_index("off")
    mine = []
    for chunk in range(chunks):
        slot_in = leaf_slot
        if chunk >= 2:
            slot_in, _ = lax.optimization_barrier((leaf_slot, mine[chunk - 2]))
        partial_sum = translate(
            slot_in, buffer, kernels, chunk, tile, (coarse_high, coarse_low, transfer), devices
        )
        total = lax.dynamic_slice_in_dim(partial_sum, me * block, block, 0)
        for shift in range(1, devices):
            theirs = lax.rem(me + shift, devices)
            sent = lax.dynamic_slice_in_dim(partial_sum, theirs * block, block, 0)
            route = [(k, (k + shift) % devices) for k in range(devices)]
            total = total + lax.ppermute(sent, "off", route)
        mine.append(total)
    mine = jnp.stack(mine).reshape(8, span, width)
    return mine.transpose(1, 0, 2).reshape(-1, width)


def solution(mesh):
    in_specs = (
        P("leaf", None),
        P("off", None, None),
        P(),
        P("leaf", "off", None),
        P("leaf", "off", None),
        P("leaf", "off"),
        P("leaf", "off", None),
        P("leaf", "off", None),
        P("leaf", "off"),
        P("leaf", None, None),
        P("leaf", None, None),
    )
    out_specs = P(("leaf", "off"), None)
    return jax.shard_map(
        on_device, mesh=mesh, in_specs=in_specs, out_specs=out_specs, check_vma=False
    )
```

profile of v0, /device:TPU:16, one launch (start us, length us, event | category | flops | bytes accessed | tf_op | source)
XLA Modules:
  0.0 130.1 jit_solution(15836766045786682147)
XLA Ops:
  0.0 0.7 fusion.51
  0.7 1.5 %copy.277 = bf16[1024,488]{1,0:T(8,128)(2,1)S(1)} copy(bf16[1024,488]{0,1:T(8,128)(2,1)} %param.11) | data formatting | bytes 1998848 | tf_op args[0]
  2.2 1.8 %reshape.502 = bf16[128,3904]{1,0:T(8,128)(2,1)S(1)} reshape(bf16[1024,488]{1,0:T(8,128)(2,1)S(1)} %copy.277) | data formatting | bytes 1998848 | tf_op jit(solution)/shard_map/reshape | solution.py:141
  4.0 3.8 %convolution_convert_fusion = bf16[128,488]{0,1:T(8,128)(2,1)S(1)} fusion(bf16[128,3904]{1,0:T(8,128)(2,1)S(1)} %reshape.502, bf16[3904,488]{1,0:T(8,128)(2,1)} %bitcast.124), kind=kOutput, calls=%fused_computation.12 | convolution fusion | flops 487781376 | bytes 4934656 | tf_op jit(solution)/shard_map/dot_general | solution.py:140
  8.9 0.6 gather_fusion.1
  9.5 0.7 gather_fusion
  10.8 0.9 shard_map.109
  11.9 0.7 gather_fusion.2
  12.6 0.6 gather_fusion.3
  13.4 1.4 %collective-permute-start.1 = (bf16[80,488]{1,0:T(8,128)(2,1)S(1)}, bf16[80,488]{1,0:T(8,128)(2,1)S(1)}, u32[]{:S(2)}, u32[]{:S(2)}) collective-permute-start(bf16[80,488]{1,0:T(8,128)(2,1)S(1)} %pad_maximum_fusion.2), channel_id=1, source_target_pairs={{0,8},{8,0},{4,12},{12,4},{16,24},{24,16},{20,28},{28,20},{32,40},... | collective-permute-start | bytes 234248 | tf_op jit(solution)/shard_map/ppermute | solution.py:18
  14.8 0.9 shard_map.110
  15.7 2.6 %collective-permute-done.1 = bf16[80,488]{1,0:T(8,128)(2,1)S(1)} collective-permute-done((bf16[80,488]{1,0:T(8,128)(2,1)S(1)}, bf16[80,488]{1,0:T(8,128)(2,1)S(1)}, u32[]{:S(2)}, u32[]{:S(2)}) %collective-permute-start.1) | collective-permute-done | bytes 78112 | tf_op jit(solution)/shard_map/ppermute | solution.py:18
  18.3 0.7 gather_fusion.4
  19.0 0.6 gather_fusion.5
  19.8 2.2 %collective-permute-start.2 = (bf16[80,488]{1,0:T(8,128)(2,1)S(1)}, bf16[80,488]{1,0:T(8,128)(2,1)S(1)}, u32[]{:S(2)}, u32[]{:S(2)}) collective-permute-start(bf16[80,488]{1,0:T(8,128)(2,1)S(1)} %pad_maximum_fusion.3), channel_id=1, source_target_pairs={{0,16},{16,0},{4,20},{20,4},{8,24},{24,8},{12,28},{28,12},{32,48},... | collective-permute-start | bytes 234248 | tf_op jit(solution)/shard_map/ppermute | solution.py:18
  21.9 0.9 shard_map.111
  22.9 2.9 %collective-permute-done.2 = bf16[80,488]{1,0:T(8,128)(2,1)S(1)} collective-permute-done((bf16[80,488]{1,0:T(8,128)(2,1)S(1)}, bf16[80,488]{1,0:T(8,128)(2,1)S(1)}, u32[]{:S(2)}, u32[]{:S(2)}) %collective-permute-start.2) | collective-permute-done | bytes 78112 | tf_op jit(solution)/shard_map/ppermute | solution.py:18
  25.8 0.7 gather_fusion.6
  26.5 0.6 gather_fusion.7
  27.3 2.0 %collective-permute-start.3 = (bf16[80,488]{1,0:T(8,128)(2,1)S(1)}, bf16[80,488]{1,0:T(8,128)(2,1)S(1)}, u32[]{:S(2)}, u32[]{:S(2)}) collective-permute-start(bf16[80,488]{1,0:T(8,128)(2,1)S(1)} %pad_maximum_fusion.4), channel_id=1, source_target_pairs={{0,32},{32,0},{4,36},{36,4},{8,40},{40,8},{12,44},{44,12},{16,48},... | collective-permute-start | bytes 234248 | tf_op jit(solution)/shard_map/ppermute | solution.py:18
  29.3 0.9 shard_map.112
  30.2 1.6 %collective-permute-done.3 = bf16[80,488]{1,0:T(8,128)(2,1)S(1)} collective-permute-done((bf16[80,488]{1,0:T(8,128)(2,1)S(1)}, bf16[80,488]{1,0:T(8,128)(2,1)S(1)}, u32[]{:S(2)}, u32[]{:S(2)}) %collective-permute-start.3) | collective-permute-done | bytes 78112 | tf_op jit(solution)/shard_map/ppermute | solution.py:18
  31.8 0.7 gather_fusion.8
  32.5 0.6 gather_fusion.9
  33.3 3.5 %collective-permute-start.4 = (bf16[80,488]{1,0:T(8,128)(2,1)S(1)}, bf16[80,488]{1,0:T(8,128)(2,1)S(1)}, u32[]{:S(2)}, u32[]{:S(2)}) collective-permute-start(bf16[80,488]{1,0:T(8,128)(2,1)S(1)} %pad_maximum_fusion.5), channel_id=1, source_target_pairs={{0,64},{64,0},{4,68},{68,4},{8,72},{72,8},{12,76},{76,12},{16,80},... | collective-permute-start | bytes 234248 | tf_op jit(solution)/shard_map/ppermute | solution.py:18
  36.8 0.9 shard_map.113
  37.8 1.5 %collective-permute-done.4 = bf16[80,488]{1,0:T(8,128)(2,1)S(1)} collective-permute-done((bf16[80,488]{1,0:T(8,128)(2,1)S(1)}, bf16[80,488]{1,0:T(8,128)(2,1)S(1)}, u32[]{:S(2)}, u32[]{:S(2)}) %collective-permute-start.4) | collective-permute-done | bytes 78112 | tf_op jit(solution)/shard_map/ppermute | solution.py:18
  39.2 0.6 gather_fusion.11
  39.8 0.7 gather_fusion.10
  40.6 7.8 %collective-permute-start.5 = (bf16[80,488]{1,0:T(8,128)(2,1)S(1)}, bf16[80,488]{1,0:T(8,128)(2,1)S(1)}, u32[]{:S(2)}, u32[]{:S(2)}) collective-permute-start(bf16[80,488]{1,0:T(8,128)(2,1)S(1)} %pad_maximum_fusion.6), channel_id=1, source_target_pairs={{0,128},{128,0},{4,132},{132,4},{8,136},{136,8},{12,140},{140,12},... | collective-permute-start | bytes 234248 | tf_op jit(solution)/shard_map/ppermute | solution.py:18
  49.9 0.9 collective-permute-done.5
  50.8 2.4 %copy-done = bf16[10,488,488]{2,1,0:T(8,128)(2,1)S(1)} copy-done((bf16[10,488,488]{2,1,0:T(8,128)(2,1)S(1)}, bf16[10,488,488]{2,1,0:T(8,128)(2,1)}, u32[]{:S(2)}) %copy-start) | copy-done | bytes 4762904
  53.2 4.3 %shard_map.115 = f32[128,488]{1,0:T(8,128)S(1)} custom-call(s32[16,128]{1,0:T(8,128)S(1)} %pad.62.slot_ref, bf16[224,488]{1,0:T(8,128)(2,1)S(1)} %slice_dynamic-update-slice_fusion.6.buf_ref, bf16[10,488,488]{2,1,0:T(8,128)(2,1)S(1)} %copy-done), custom_call_target="tpu_custom_call" | custom-call | flops 889487360 | bytes 4981504 | tf_op jit(solution)/shard_map/pallas_call | solution.py:103
  57.6 12.1 %shard_map.116 = f32[256,488]{1,0:T(8,128)S(1)} custom-call(s32[16,1024]{1,0:T(8,128)S(1)} %pad.59.slot_ref, bf16[1408,488]{1,0:T(8,128)(2,1)S(1)} %slice_dynamic-update-slice_fusion.buf_ref, bf16[10,488,488]{2,1,0:T(8,128)(2,1)} %k_ref.9, bf16[128,488]{1,0:T(8,128)(2,1)S(1)} %get-tuple-element.84.rest_0_, bf16[128,488]{1,0:T(8,128)(2,1)S(1)} %get-tuple-element.83.rest_1_, ...), custom_call_target="tpu_custom_call" | custom-call | flops 4737269760 | bytes 6137088 | tf_op jit(solution)/shard_map/pallas_call | solution.py:103
  69.7 1.6 %collective-permute-start.6 = (f32[64,488]{1,0:T(8,128)S(1)}, f32[64,488]{1,0:T(8,128)S(1)}, u32[]{:S(2)}, u32[]{:S(2)}) collective-permute-start(f32[64,488]{1,0:T(8,128)S(1)} %get-tuple-element.74), channel_id=1, source_target_pairs={{0,1},{1,2},{2,3},{3,0},{4,5},{5,6},{6,7},{7,4},{8,9},{9,10},{10,1... | collective-permute-start | bytes 374792 | tf_op jit(solution)/shard_map/ppermute | solution.py:203
  71.2 2.7 %collective-permute-start.7 = (f32[64,488]{1,0:T(8,128)S(1)}, f32[64,488]{1,0:T(8,128)S(1)}, u32[]{:S(2)}, u32[]{:S(2)}) collective-permute-start(f32[64,488]{1,0:T(8,128)S(1)} %get-tuple-element.76), channel_id=1, source_target_pairs={{0,2},{1,3},{2,0},{3,1},{4,6},{5,7},{6,4},{7,5},{8,10},{9,11},{10,... | collective-permute-start | bytes 374792 | tf_op jit(solution)/shard_map/ppermute | solution.py:203
  74.0 1.4 %collective-permute-start.8 = (f32[64,488]{1,0:T(8,128)S(1)}, f32[64,488]{1,0:T(8,128)S(1)}, u32[]{:S(2)}, u32[]{:S(2)}) collective-permute-start(f32[64,488]{1,0:T(8,128)S(1)} %get-tuple-element.75), channel_id=1, source_target_pairs={{0,3},{1,0},{2,1},{3,2},{4,7},{5,4},{6,5},{7,6},{8,11},{9,8},{10,9... | collective-permute-start | bytes 374792 | tf_op jit(solution)/shard_map/ppermute | solution.py:203
  75.4 12.1 %shard_map.117 = f32[256,488]{1,0:T(8,128)S(1)} custom-call(s32[16,1024]{1,0:T(8,128)S(1)} %pad.59.slot_ref, bf16[1408,488]{1,0:T(8,128)(2,1)S(1)} %slice_dynamic-update-slice_fusion.buf_ref, bf16[10,488,488]{2,1,0:T(8,128)(2,1)} %k_ref.9, bf16[128,488]{1,0:T(8,128)(2,1)S(1)} %get-tuple-element.84.rest_0_, bf16[128,488]{1,0:T(8,128)(2,1)S(1)} %get-tuple-element.83.rest_1_, ...), custom_call_target="tpu_custom_call" | custom-call | flops 4737269760 | bytes 6137088 | tf_op jit(solution)/shard_map/pallas_call | solution.py:103
  87.5 0.6 collective-permute-start.10
  88.1 2.8 %collective-permute-start.11 = (f32[64,488]{1,0:T(8,128)S(1)}, f32[64,488]{1,0:T(8,128)S(1)}, u32[]{:S(2)}, u32[]{:S(2)}) collective-permute-start(f32[64,488]{1,0:T(8,128)S(1)} %get-tuple-element.81), channel_id=1, source_target_pairs={{0,3},{1,0},{2,1},{3,2},{4,7},{5,4},{6,5},{7,6},{8,11},{9,8},{10,9... | collective-permute-start | bytes 374792 | tf_op jit(solution)/shard_map/ppermute | solution.py:203
  90.9 12.1 %shard_map.118 = f32[256,488]{1,0:T(8,128)S(1)} custom-call(s32[16,1024]{1,0:T(8,128)S(1)} %pad.59.slot_ref, bf16[1408,488]{1,0:T(8,128)(2,1)S(1)} %slice_dynamic-update-slice_fusion.buf_ref, bf16[10,488,488]{2,1,0:T(8,128)(2,1)} %k_ref.9, bf16[128,488]{1,0:T(8,128)(2,1)S(1)} %get-tuple-element.84.rest_0_, bf16[128,488]{1,0:T(8,128)(2,1)S(1)} %get-tuple-element.83.rest_1_, ...), custom_call_target="tpu_custom_call" | custom-call | flops 4737269760 | bytes 6137088 | tf_op jit(solution)/shard_map/pallas_call | solution.py:103
  103.3 4.5 %collective-permute-start.13 = (f32[64,488]{1,0:T(8,128)S(1)}, f32[64,488]{1,0:T(8,128)S(1)}, u32[]{:S(2)}, u32[]{:S(2)}) collective-permute-start(f32[64,488]{1,0:T(8,128)S(1)} %get-tuple-element.73), channel_id=1, source_target_pairs={{0,2},{1,3},{2,0},{3,1},{4,6},{5,7},{6,4},{7,5},{8,10},{9,11},{10,... | collective-permute-start | bytes 374792 | tf_op jit(solution)/shard_map/ppermute | solution.py:203
  108.1 12.1 %shard_map.119 = f32[256,488]{1,0:T(8,128)S(1)} custom-call(s32[16,1024]{1,0:T(8,128)S(1)} %pad.59.slot_ref, bf16[1408,488]{1,0:T(8,128)(2,1)S(1)} %slice_dynamic-update-slice_fusion.buf_ref, bf16[10,488,488]{2,1,0:T(8,128)(2,1)} %k_ref.9, bf16[128,488]{1,0:T(8,128)(2,1)S(1)} %get-tuple-element.84.rest_0_, bf16[128,488]{1,0:T(8,128)(2,1)S(1)} %get-tuple-element.83.rest_1_, ...), custom_call_target="tpu_custom_call" | custom-call | flops 4737269760 | bytes 6137088 | tf_op jit(solution)/shard_map/pallas_call | solution.py:103
  120.2 1.9 %collective-permute-start.15 = (f32[64,488]{1,0:T(8,128)S(1)}, f32[64,488]{1,0:T(8,128)S(1)}, u32[]{:S(2)}, u32[]{:S(2)}) collective-permute-start(f32[64,488]{1,0:T(8,128)S(1)} %get-tuple-element.77), channel_id=1, source_target_pairs={{0,1},{1,2},{2,3},{3,0},{4,5},{5,6},{6,7},{7,4},{8,9},{9,10},{10,1... | collective-permute-start | bytes 374792 | tf_op jit(solution)/shard_map/ppermute | solution.py:203
  122.1 2.8 %collective-permute-start.17 = (f32[64,488]{1,0:T(8,128)S(1)}, f32[64,488]{1,0:T(8,128)S(1)}, u32[]{:S(2)}, u32[]{:S(2)}) collective-permute-start(f32[64,488]{1,0:T(8,128)S(1)} %get-tuple-element.78), channel_id=1, source_target_pairs={{0,3},{1,0},{2,1},{3,2},{4,7},{5,4},{6,5},{7,6},{8,11},{9,8},{10,9... | collective-permute-start | bytes 374792 | tf_op jit(solution)/shard_map/ppermute | solution.py:203
  124.9 1.6 %collective-permute-done.15 = f32[64,488]{1,0:T(8,128)S(1)} collective-permute-done((f32[64,488]{1,0:T(8,128)S(1)}, f32[64,488]{1,0:T(8,128)S(1)}, u32[]{:S(2)}, u32[]{:S(2)}) %collective-permute-start.15) | collective-permute-done | bytes 124960 | tf_op jit(solution)/shard_map/ppermute | solution.py:203
  126.4 2.1 %collective-permute-done.16 = f32[64,488]{1,0:T(8,128)S(1)} collective-permute-done((f32[64,488]{1,0:T(8,128)S(1)}, f32[64,488]{1,0:T(8,128)S(1)}, u32[]{:S(2)}, u32[]{:S(2)}) %collective-permute-start.16) | collective-permute-done | bytes 124960 | tf_op jit(solution)/shard_map/ppermute | solution.py:203
  129.1 1.0 copy.300
  (116 shorter events, 5.1 us)
Async XLA Ops:
  8.0 0.7 copy-start.6
  8.0 0.8 copy-start.1
  8.0 0.8 copy-start.2
  8.1 0.8 copy-start.3
  8.2 2.3 %copy-start.4 = (s32[1,10,128]{2,0,1:T(1,128)S(1)}, s32[1,10,128]{2,0,1:T(1,128)}, u32[]{:S(2)}) copy-start(s32[1,10,128]{2,0,1:T(1,128)} %param.18) | copy-start | bytes 15364
  8.2 2.3 %copy-start.7 = (s32[1,10]{1,0:T(1,128)S(1)}, s32[1,10]{1,0:T(1,128)}, u32[]{:S(2)}) copy-start(s32[1,10]{1,0:T(1,128)} %param.19) | copy-start | bytes 124
  8.2 2.5 %copy-start.5 = (s32[1,10,128]{2,0,1:T(1,128)S(1)}, s32[1,10,128]{2,0,1:T(1,128)}, u32[]{:S(2)}) copy-start(s32[1,10,128]{2,0,1:T(1,128)} %param.17) | copy-start | bytes 15364
  10.3 1.6 %collective-permute-start = (bf16[80,488]{1,0:T(8,128)(2,1)S(1)}, bf16[80,488]{1,0:T(8,128)(2,1)S(1)}, u32[]{:S(2)}, u32[]{:S(2)}) collective-permute-start(bf16[80,488]{1,0:T(8,128)(2,1)S(1)} %pad_maximum_fusion.1), channel_id=1, source_target_pairs={{0,4},{4,0},{8,12},{12,8},{16,20},{20,16},{24,28},{28,24},{32,36},... | collective-permute-start | bytes 234248 | tf_op jit(solution)/shard_map/ppermute | solution.py:18
  13.4 4.9 %collective-permute-start.1 = (bf16[80,488]{1,0:T(8,128)(2,1)S(1)}, bf16[80,488]{1,0:T(8,128)(2,1)S(1)}, u32[]{:S(2)}, u32[]{:S(2)}) collective-permute-start(bf16[80,488]{1,0:T(8,128)(2,1)S(1)} %pad_maximum_fusion.2), channel_id=1, source_target_pairs={{0,8},{8,0},{4,12},{12,4},{16,24},{24,16},{20,28},{28,20},{32,40},... | collective-permute-start | bytes 234248 | tf_op jit(solution)/shard_map/ppermute | solution.py:18
  19.8 6.0 %collective-permute-start.2 = (bf16[80,488]{1,0:T(8,128)(2,1)S(1)}, bf16[80,488]{1,0:T(8,128)(2,1)S(1)}, u32[]{:S(2)}, u32[]{:S(2)}) collective-permute-start(bf16[80,488]{1,0:T(8,128)(2,1)S(1)} %pad_maximum_fusion.3), channel_id=1, source_target_pairs={{0,16},{16,0},{4,20},{20,4},{8,24},{24,8},{12,28},{28,12},{32,48},... | collective-permute-start | bytes 234248 | tf_op jit(solution)/shard_map/ppermute | solution.py:18
  27.3 4.5 %collective-permute-start.3 = (bf16[80,488]{1,0:T(8,128)(2,1)S(1)}, bf16[80,488]{1,0:T(8,128)(2,1)S(1)}, u32[]{:S(2)}, u32[]{:S(2)}) collective-permute-start(bf16[80,488]{1,0:T(8,128)(2,1)S(1)} %pad_maximum_fusion.4), channel_id=1, source_target_pairs={{0,32},{32,0},{4,36},{36,4},{8,40},{40,8},{12,44},{44,12},{16,48},... | collective-permute-start | bytes 234248 | tf_op jit(solution)/shard_map/ppermute | solution.py:18
  33.3 6.0 %collective-permute-start.4 = (bf16[80,488]{1,0:T(8,128)(2,1)S(1)}, bf16[80,488]{1,0:T(8,128)(2,1)S(1)}, u32[]{:S(2)}, u32[]{:S(2)}) collective-permute-start(bf16[80,488]{1,0:T(8,128)(2,1)S(1)} %pad_maximum_fusion.5), channel_id=1, source_target_pairs={{0,64},{64,0},{4,68},{68,4},{8,72},{72,8},{12,76},{76,12},{16,80},... | collective-permute-start | bytes 234248 | tf_op jit(solution)/shard_map/ppermute | solution.py:18
  40.6 10.2 %collective-permute-start.5 = (bf16[80,488]{1,0:T(8,128)(2,1)S(1)}, bf16[80,488]{1,0:T(8,128)(2,1)S(1)}, u32[]{:S(2)}, u32[]{:S(2)}) collective-permute-start(bf16[80,488]{1,0:T(8,128)(2,1)S(1)} %pad_maximum_fusion.6), channel_id=1, source_target_pairs={{0,128},{128,0},{4,132},{132,4},{8,136},{136,8},{12,140},{140,12},... | collective-permute-start | bytes 234248 | tf_op jit(solution)/shard_map/ppermute | solution.py:18
  50.8 2.4 %copy-start = (bf16[10,488,488]{2,1,0:T(8,128)(2,1)S(1)}, bf16[10,488,488]{2,1,0:T(8,128)(2,1)}, u32[]{:S(2)}) copy-start(bf16[10,488,488]{2,1,0:T(8,128)(2,1)} %k_ref.9) | copy-start | bytes 14288644
  69.7 21.2 %collective-permute-start.6 = (f32[64,488]{1,0:T(8,128)S(1)}, f32[64,488]{1,0:T(8,128)S(1)}, u32[]{:S(2)}, u32[]{:S(2)}) collective-permute-start(f32[64,488]{1,0:T(8,128)S(1)} %get-tuple-element.74), channel_id=1, source_target_pairs={{0,1},{1,2},{2,3},{3,0},{4,5},{5,6},{6,7},{7,4},{8,9},{9,10},{10,1... | collective-permute-start | bytes 374792 | tf_op jit(solution)/shard_map/ppermute | solution.py:203
  71.2 19.6 %collective-permute-start.7 = (f32[64,488]{1,0:T(8,128)S(1)}, f32[64,488]{1,0:T(8,128)S(1)}, u32[]{:S(2)}, u32[]{:S(2)}) collective-permute-start(f32[64,488]{1,0:T(8,128)S(1)} %get-tuple-element.76), channel_id=1, source_target_pairs={{0,2},{1,3},{2,0},{3,1},{4,6},{5,7},{6,4},{7,5},{8,10},{9,11},{10,... | collective-permute-start | bytes 374792 | tf_op jit(solution)/shard_map/ppermute | solution.py:203
  74.0 16.9 %collective-permute-start.8 = (f32[64,488]{1,0:T(8,128)S(1)}, f32[64,488]{1,0:T(8,128)S(1)}, u32[]{:S(2)}, u32[]{:S(2)}) collective-permute-start(f32[64,488]{1,0:T(8,128)S(1)} %get-tuple-element.75), channel_id=1, source_target_pairs={{0,3},{1,0},{2,1},{3,2},{4,7},{5,4},{6,5},{7,6},{8,11},{9,8},{10,9... | collective-permute-start | bytes 374792 | tf_op jit(solution)/shard_map/ppermute | solution.py:203
  87.5 20.3 %collective-permute-start.10 = (f32[64,488]{1,0:T(8,128)S(1)}, f32[64,488]{1,0:T(8,128)S(1)}, u32[]{:S(2)}, u32[]{:S(2)}) collective-permute-start(f32[64,488]{1,0:T(8,128)S(1)} %get-tuple-element.82), channel_id=1, source_target_pairs={{0,2},{1,3},{2,0},{3,1},{4,6},{5,7},{6,4},{7,5},{8,10},{9,11},{10,... | collective-permute-start | bytes 374792 | tf_op jit(solution)/shard_map/ppermute | solution.py:203
  88.1 19.9 %collective-permute-start.11 = (f32[64,488]{1,0:T(8,128)S(1)}, f32[64,488]{1,0:T(8,128)S(1)}, u32[]{:S(2)}, u32[]{:S(2)}) collective-permute-start(f32[64,488]{1,0:T(8,128)S(1)} %get-tuple-element.81), channel_id=1, source_target_pairs={{0,3},{1,0},{2,1},{3,2},{4,7},{5,4},{6,5},{7,6},{8,11},{9,8},{10,9... | collective-permute-start | bytes 374792 | tf_op jit(solution)/shard_map/ppermute | solution.py:203
  90.9 17.2 %collective-permute-start.9 = (f32[64,488]{1,0:T(8,128)S(1)}, f32[64,488]{1,0:T(8,128)S(1)}, u32[]{:S(2)}, u32[]{:S(2)}) collective-permute-start(f32[64,488]{1,0:T(8,128)S(1)} %get-tuple-element.80), channel_id=1, source_target_pairs={{0,1},{1,2},{2,3},{3,0},{4,5},{5,6},{6,7},{7,4},{8,9},{9,10},{10,1... | collective-permute-start | bytes 374792 | tf_op jit(solution)/shard_map/ppermute | solution.py:203
  103.0 19.0 %collective-permute-start.12 = (f32[64,488]{1,0:T(8,128)S(1)}, f32[64,488]{1,0:T(8,128)S(1)}, u32[]{:S(2)}, u32[]{:S(2)}) collective-permute-start(f32[64,488]{1,0:T(8,128)S(1)} %get-tuple-element.71), channel_id=1, source_target_pairs={{0,1},{1,2},{2,3},{3,0},{4,5},{5,6},{6,7},{7,4},{8,9},{9,10},{10,1... | collective-permute-start | bytes 374792 | tf_op jit(solution)/shard_map/ppermute | solution.py:203
  103.3 21.5 %collective-permute-start.13 = (f32[64,488]{1,0:T(8,128)S(1)}, f32[64,488]{1,0:T(8,128)S(1)}, u32[]{:S(2)}, u32[]{:S(2)}) collective-permute-start(f32[64,488]{1,0:T(8,128)S(1)} %get-tuple-element.73), channel_id=1, source_target_pairs={{0,2},{1,3},{2,0},{3,1},{4,6},{5,7},{6,4},{7,5},{8,10},{9,11},{10,... | collective-permute-start | bytes 374792 | tf_op jit(solution)/shard_map/ppermute | solution.py:203
  107.8 17.0 %collective-permute-start.14 = (f32[64,488]{1,0:T(8,128)S(1)}, f32[64,488]{1,0:T(8,128)S(1)}, u32[]{:S(2)}, u32[]{:S(2)}) collective-permute-start(f32[64,488]{1,0:T(8,128)S(1)} %get-tuple-element.72), channel_id=1, source_target_pairs={{0,3},{1,0},{2,1},{3,2},{4,7},{5,4},{6,5},{7,6},{8,11},{9,8},{10,9... | collective-permute-start | bytes 374792 | tf_op jit(solution)/shard_map/ppermute | solution.py:203
  120.2 6.3 %collective-permute-start.15 = (f32[64,488]{1,0:T(8,128)S(1)}, f32[64,488]{1,0:T(8,128)S(1)}, u32[]{:S(2)}, u32[]{:S(2)}) collective-permute-start(f32[64,488]{1,0:T(8,128)S(1)} %get-tuple-element.77), channel_id=1, source_target_pairs={{0,1},{1,2},{2,3},{3,0},{4,5},{5,6},{6,7},{7,4},{8,9},{9,10},{10,1... | collective-permute-start | bytes 374792 | tf_op jit(solution)/shard_map/ppermute | solution.py:203
  122.1 6.5 %collective-permute-start.16 = (f32[64,488]{1,0:T(8,128)S(1)}, f32[64,488]{1,0:T(8,128)S(1)}, u32[]{:S(2)}, u32[]{:S(2)}) collective-permute-start(f32[64,488]{1,0:T(8,128)S(1)} %get-tuple-element.79), channel_id=1, source_target_pairs={{0,2},{1,3},{2,0},{3,1},{4,6},{5,7},{6,4},{7,5},{8,10},{9,11},{10,... | collective-permute-start | bytes 374792 | tf_op jit(solution)/shard_map/ppermute | solution.py:203
  122.1 6.6 %collective-permute-start.17 = (f32[64,488]{1,0:T(8,128)S(1)}, f32[64,488]{1,0:T(8,128)S(1)}, u32[]{:S(2)}, u32[]{:S(2)}) collective-permute-start(f32[64,488]{1,0:T(8,128)S(1)} %get-tuple-element.78), channel_id=1, source_target_pairs={{0,3},{1,0},{2,1},{3,2},{4,7},{5,4},{6,5},{7,6},{8,11},{9,8},{10,9... | collective-permute-start | bytes 374792 | tf_op jit(solution)/shard_map/ppermute | solution.py:203
where the time goes:
time: 130 us
  Pallas kernels  57.7 us (44%)
  starting transfers between devices  35.7 us (27%)
  local copies, waits for them, and re-layouts  17 us (13%)
  waiting for transfers between devices  13.2 us (10%)
  matrix products  3.83 us (3%)
  other arithmetic  1.88 us (1%)
    pallas_call x5, Pallas kernels, translate(): pl.pallas_call(functools.partial(translate_kernel, spread is not None, de...  52.5 us
    ppermute x12, starting transfers between devices, on_device(): total = total + lax.ppermute(sent, 'off', route)  18.7 us
    ppermute x6, starting transfers between devices, partner(): return lax.ppermute(block, axis, route)  17 us
    ppermute x6, waiting for transfers between devices, partner(): return lax.ppermute(block, axis, route)  9.37 us
    pallas_call x6, Pallas kernels, slot_table(): pl.pallas_call(invert_kernel, out_shape=jax.ShapeDtypeStruct((classes, pa...  5.2 us
    unnamed x20, local copies, waits for them, and re-layouts  4.49 us
    gather x6, local copies, waits for them, and re-layouts, on_device(): buffer[ghost_send[0, bit_index]]  4.21 us
    ppermute x12, waiting for transfers between devices, on_device(): total = total + lax.ppermute(sent, 'off', route)  3.85 us
  transfers between devices with their start and end apart: 18, of which 8 were waited for; matrix products, arithmetic and copies ran while one was open for 1% of the time, Pallas kernels for 32%

commit v1 on v0

--- a/solution.py
+++ b/solution.py
@@ -78,7 +78,7 @@
         )
         return carry
 
-    lax.fori_loop(0, k_ref.shape[0], one_class, 0)
+    lax.fori_loop(0, k_ref.shape[0], one_class, 0, unroll=5)
 
 
 def translate(slot, buffer, kernels, chunk, tile, spread=None, devices=1):

time: 130 us -> 121 us (0.931)
  Pallas kernels: 57.7 us -> 48.5 us
    pallas_call x5, Pallas kernels: 52.5 us -> 43.3 us  [translate(): pl.pallas_call(functools.partial(translate_kernel, spread is not None, de...]
  transfers between devices with their start and end apart: 18 -> 18, of which waited for: 8 -> 8; matrix products, arithmetic and copies ran while one was open for 1% -> 1% of each run, Pallas kernels for 32% -> 29%
where the time goes in v1:
time: 121 us
  Pallas kernels  48.5 us (40%)
  starting transfers between devices  35.7 us (30%)
  local copies, waits for them, and re-layouts  17 us (14%)
  waiting for transfers between devices  13.2 us (11%)
  matrix products  3.83 us (3%)
  other arithmetic  1.88 us (2%)
    pallas_call x5, Pallas kernels, translate(): pl.pallas_call(functools.partial(translate_kernel, spread is not None, de...  43.3 us
    ppermute x12, starting transfers between devices, on_device(): total = total + lax.ppermute(sent, 'off', route)  18.7 us
    ppermute x6, starting transfers between devices, partner(): return lax.ppermute(block, axis, route)  17 us
    ppermute x6, waiting for transfers between devices, partner(): return lax.ppermute(block, axis, route)  9.37 us
    pallas_call x6, Pallas kernels, slot_table(): pl.pallas_call(invert_kernel, out_shape=jax.ShapeDtypeStruct((classes, pa...  5.2 us
    unnamed x20, local copies, waits for them, and re-layouts  4.49 us
    gather x6, local copies, waits for them, and re-layouts, on_device(): buffer[ghost_send[0, bit_index]]  4.21 us
    dot_general x1, matrix products, on_device(): jnp.dot(multipoles.reshape(-1, 8 * width), transfer.reshape(8 * width, wi...  3.83 us
  transfers between devices with their start and end apart: 18, of which 8 were waited for; matrix products, arithmetic and copies ran while one was open for 1% of the time, Pallas kernels for 29%

profile of v1, /device:TPU:16, one launch (start us, length us, event | category | flops | bytes accessed | tf_op | source)
XLA Modules:
  0.0 120.9 jit_solution(7450431207286371832)
XLA Ops:
  0.0 0.7 fusion.51
  0.7 1.5 %copy.277 = bf16[1024,488]{1,0:T(8,128)(2,1)S(1)} copy(bf16[1024,488]{0,1:T(8,128)(2,1)} %param.11) | data formatting | bytes 1998848 | tf_op args[0]
  2.2 1.8 %reshape.502 = bf16[128,3904]{1,0:T(8,128)(2,1)S(1)} reshape(bf16[1024,488]{1,0:T(8,128)(2,1)S(1)} %copy.277) | data formatting | bytes 1998848 | tf_op jit(solution)/shard_map/reshape | solution.py:141
  4.0 3.8 %convolution_convert_fusion = bf16[128,488]{0,1:T(8,128)(2,1)S(1)} fusion(bf16[128,3904]{1,0:T(8,128)(2,1)S(1)} %reshape.502, bf16[3904,488]{1,0:T(8,128)(2,1)} %bitcast.124), kind=kOutput, calls=%fused_computation.12 | convolution fusion | flops 487781376 | bytes 4934656 | tf_op jit(solution)/shard_map/dot_general | solution.py:140
  8.9 0.6 gather_fusion.1
  9.5 0.7 gather_fusion
  10.8 0.9 shard_map.109
  11.9 0.7 gather_fusion.2
  12.6 0.6 gather_fusion.3
  13.4 1.4 %collective-permute-start.1 = (bf16[80,488]{1,0:T(8,128)(2,1)S(1)}, bf16[80,488]{1,0:T(8,128)(2,1)S(1)}, u32[]{:S(2)}, u32[]{:S(2)}) collective-permute-start(bf16[80,488]{1,0:T(8,128)(2,1)S(1)} %pad_maximum_fusion.2), channel_id=1, source_target_pairs={{0,8},{8,0},{4,12},{12,4},{16,24},{24,16},{20,28},{28,20},{32,40},... | collective-permute-start | bytes 234248 | tf_op jit(solution)/shard_map/ppermute | solution.py:18
  14.8 0.9 shard_map.110
  15.7 2.6 %collective-permute-done.1 = bf16[80,488]{1,0:T(8,128)(2,1)S(1)} collective-permute-done((bf16[80,488]{1,0:T(8,128)(2,1)S(1)}, bf16[80,488]{1,0:T(8,128)(2,1)S(1)}, u32[]{:S(2)}, u32[]{:S(2)}) %collective-permute-start.1) | collective-permute-done | bytes 78112 | tf_op jit(solution)/shard_map/ppermute | solution.py:18
  18.3 0.7 gather_fusion.4
  19.0 0.6 gather_fusion.5
  19.8 2.2 %collective-permute-start.2 = (bf16[80,488]{1,0:T(8,128)(2,1)S(1)}, bf16[80,488]{1,0:T(8,128)(2,1)S(1)}, u32[]{:S(2)}, u32[]{:S(2)}) collective-permute-start(bf16[80,488]{1,0:T(8,128)(2,1)S(1)} %pad_maximum_fusion.3), channel_id=1, source_target_pairs={{0,16},{16,0},{4,20},{20,4},{8,24},{24,8},{12,28},{28,12},{32,48},... | collective-permute-start | bytes 234248 | tf_op jit(solution)/shard_map/ppermute | solution.py:18
  21.9 0.9 shard_map.111
  22.9 2.9 %collective-permute-done.2 = bf16[80,488]{1,0:T(8,128)(2,1)S(1)} collective-permute-done((bf16[80,488]{1,0:T(8,128)(2,1)S(1)}, bf16[80,488]{1,0:T(8,128)(2,1)S(1)}, u32[]{:S(2)}, u32[]{:S(2)}) %collective-permute-start.2) | collective-permute-done | bytes 78112 | tf_op jit(solution)/shard_map/ppermute | solution.py:18
  25.8 0.7 gather_fusion.6
  26.5 0.6 gather_fusion.7
  27.3 2.0 %collective-permute-start.3 = (bf16[80,488]{1,0:T(8,128)(2,1)S(1)}, bf16[80,488]{1,0:T(8,128)(2,1)S(1)}, u32[]{:S(2)}, u32[]{:S(2)}) collective-permute-start(bf16[80,488]{1,0:T(8,128)(2,1)S(1)} %pad_maximum_fusion.4), channel_id=1, source_target_pairs={{0,32},{32,0},{4,36},{36,4},{8,40},{40,8},{12,44},{44,12},{16,48},... | collective-permute-start | bytes 234248 | tf_op jit(solution)/shard_map/ppermute | solution.py:18
  29.3 0.9 shard_map.112
  30.2 1.6 %collective-permute-done.3 = bf16[80,488]{1,0:T(8,128)(2,1)S(1)} collective-permute-done((bf16[80,488]{1,0:T(8,128)(2,1)S(1)}, bf16[80,488]{1,0:T(8,128)(2,1)S(1)}, u32[]{:S(2)}, u32[]{:S(2)}) %collective-permute-start.3) | collective-permute-done | bytes 78112 | tf_op jit(solution)/shard_map/ppermute | solution.py:18
  31.8 0.7 gather_fusion.8
  32.5 0.6 gather_fusion.9
  33.3 3.5 %collective-permute-start.4 = (bf16[80,488]{1,0:T(8,128)(2,1)S(1)}, bf16[80,488]{1,0:T(8,128)(2,1)S(1)}, u32[]{:S(2)}, u32[]{:S(2)}) collective-permute-start(bf16[80,488]{1,0:T(8,128)(2,1)S(1)} %pad_maximum_fusion.5), channel_id=1, source_target_pairs={{0,64},{64,0},{4,68},{68,4},{8,72},{72,8},{12,76},{76,12},{16,80},... | collective-permute-start | bytes 234248 | tf_op jit(solution)/shard_map/ppermute | solution.py:18
  36.8 0.9 shard_map.113
  37.8 1.5 %collective-permute-done.4 = bf16[80,488]{1,0:T(8,128)(2,1)S(1)} collective-permute-done((bf16[80,488]{1,0:T(8,128)(2,1)S(1)}, bf16[80,488]{1,0:T(8,128)(2,1)S(1)}, u32[]{:S(2)}, u32[]{:S(2)}) %collective-permute-start.4) | collective-permute-done | bytes 78112 | tf_op jit(solution)/shard_map/ppermute | solution.py:18
  39.2 0.6 gather_fusion.11
  39.8 0.7 gather_fusion.10
  40.6 7.8 %collective-permute-start.5 = (bf16[80,488]{1,0:T(8,128)(2,1)S(1)}, bf16[80,488]{1,0:T(8,128)(2,1)S(1)}, u32[]{:S(2)}, u32[]{:S(2)}) collective-permute-start(bf16[80,488]{1,0:T(8,128)(2,1)S(1)} %pad_maximum_fusion.6), channel_id=1, source_target_pairs={{0,128},{128,0},{4,132},{132,4},{8,136},{136,8},{12,140},{140,12},... | collective-permute-start | bytes 234248 | tf_op jit(solution)/shard_map/ppermute | solution.py:18
  49.9 0.9 collective-permute-done.5
  50.8 2.4 %copy-done = bf16[10,488,488]{2,1,0:T(8,128)(2,1)S(1)} copy-done((bf16[10,488,488]{2,1,0:T(8,128)(2,1)S(1)}, bf16[10,488,488]{2,1,0:T(8,128)(2,1)}, u32[]{:S(2)}) %copy-start) | copy-done | bytes 4762904
  53.2 2.8 %shard_map.115 = f32[128,488]{1,0:T(8,128)S(1)} custom-call(s32[16,128]{1,0:T(8,128)S(1)} %pad.62.slot_ref, bf16[224,488]{1,0:T(8,128)(2,1)S(1)} %slice_dynamic-update-slice_fusion.6.buf_ref, bf16[10,488,488]{2,1,0:T(8,128)(2,1)S(1)} %copy-done), custom_call_target="tpu_custom_call" | custom-call | flops 889487360 | bytes 4981504 | tf_op jit(solution)/shard_map/pallas_call | solution.py:103
  56.1 10.1 %shard_map.116 = f32[256,488]{1,0:T(8,128)S(1)} custom-call(s32[16,1024]{1,0:T(8,128)S(1)} %pad.59.slot_ref, bf16[1408,488]{1,0:T(8,128)(2,1)S(1)} %slice_dynamic-update-slice_fusion.buf_ref, bf16[10,488,488]{2,1,0:T(8,128)(2,1)} %k_ref.9, bf16[128,488]{1,0:T(8,128)(2,1)S(1)} %get-tuple-element.84.rest_0_, bf16[128,488]{1,0:T(8,128)(2,1)S(1)} %get-tuple-element.83.rest_1_, ...), custom_call_target="tpu_custom_call" | custom-call | flops 4737269760 | bytes 6137088 | tf_op jit(solution)/shard_map/pallas_call | solution.py:103
  66.3 1.6 %collective-permute-start.6 = (f32[64,488]{1,0:T(8,128)S(1)}, f32[64,488]{1,0:T(8,128)S(1)}, u32[]{:S(2)}, u32[]{:S(2)}) collective-permute-start(f32[64,488]{1,0:T(8,128)S(1)} %get-tuple-element.74), channel_id=1, source_target_pairs={{0,1},{1,2},{2,3},{3,0},{4,5},{5,6},{6,7},{7,4},{8,9},{9,10},{10,1... | collective-permute-start | bytes 374792 | tf_op jit(solution)/shard_map/ppermute | solution.py:203
  67.8 2.7 %collective-permute-start.7 = (f32[64,488]{1,0:T(8,128)S(1)}, f32[64,488]{1,0:T(8,128)S(1)}, u32[]{:S(2)}, u32[]{:S(2)}) collective-permute-start(f32[64,488]{1,0:T(8,128)S(1)} %get-tuple-element.76), channel_id=1, source_target_pairs={{0,2},{1,3},{2,0},{3,1},{4,6},{5,7},{6,4},{7,5},{8,10},{9,11},{10,... | collective-permute-start | bytes 374792 | tf_op jit(solution)/shard_map/ppermute | solution.py:203
  70.6 1.4 %collective-permute-start.8 = (f32[64,488]{1,0:T(8,128)S(1)}, f32[64,488]{1,0:T(8,128)S(1)}, u32[]{:S(2)}, u32[]{:S(2)}) collective-permute-start(f32[64,488]{1,0:T(8,128)S(1)} %get-tuple-element.75), channel_id=1, source_target_pairs={{0,3},{1,0},{2,1},{3,2},{4,7},{5,4},{6,5},{7,6},{8,11},{9,8},{10,9... | collective-permute-start | bytes 374792 | tf_op jit(solution)/shard_map/ppermute | solution.py:203
  72.0 10.1 %shard_map.117 = f32[256,488]{1,0:T(8,128)S(1)} custom-call(s32[16,1024]{1,0:T(8,128)S(1)} %pad.59.slot_ref, bf16[1408,488]{1,0:T(8,128)(2,1)S(1)} %slice_dynamic-update-slice_fusion.buf_ref, bf16[10,488,488]{2,1,0:T(8,128)(2,1)} %k_ref.9, bf16[128,488]{1,0:T(8,128)(2,1)S(1)} %get-tuple-element.84.rest_0_, bf16[128,488]{1,0:T(8,128)(2,1)S(1)} %get-tuple-element.83.rest_1_, ...), custom_call_target="tpu_custom_call" | custom-call | flops 4737269760 | bytes 6137088 | tf_op jit(solution)/shard_map/pallas_call | solution.py:103
  82.2 0.6 collective-permute-start.10
  82.8 2.8 %collective-permute-start.11 = (f32[64,488]{1,0:T(8,128)S(1)}, f32[64,488]{1,0:T(8,128)S(1)}, u32[]{:S(2)}, u32[]{:S(2)}) collective-permute-start(f32[64,488]{1,0:T(8,128)S(1)} %get-tuple-element.81), channel_id=1, source_target_pairs={{0,3},{1,0},{2,1},{3,2},{4,7},{5,4},{6,5},{7,6},{8,11},{9,8},{10,9... | collective-permute-start | bytes 374792 | tf_op jit(solution)/shard_map/ppermute | solution.py:203
  85.6 10.1 %shard_map.118 = f32[256,488]{1,0:T(8,128)S(1)} custom-call(s32[16,1024]{1,0:T(8,128)S(1)} %pad.59.slot_ref, bf16[1408,488]{1,0:T(8,128)(2,1)S(1)} %slice_dynamic-update-slice_fusion.buf_ref, bf16[10,488,488]{2,1,0:T(8,128)(2,1)} %k_ref.9, bf16[128,488]{1,0:T(8,128)(2,1)S(1)} %get-tuple-element.84.rest_0_, bf16[128,488]{1,0:T(8,128)(2,1)S(1)} %get-tuple-element.83.rest_1_, ...), custom_call_target="tpu_custom_call" | custom-call | flops 4737269760 | bytes 6137088 | tf_op jit(solution)/shard_map/pallas_call | solution.py:103
  96.1 4.5 %collective-permute-start.13 = (f32[64,488]{1,0:T(8,128)S(1)}, f32[64,488]{1,0:T(8,128)S(1)}, u32[]{:S(2)}, u32[]{:S(2)}) collective-permute-start(f32[64,488]{1,0:T(8,128)S(1)} %get-tuple-element.73), channel_id=1, source_target_pairs={{0,2},{1,3},{2,0},{3,1},{4,6},{5,7},{6,4},{7,5},{8,10},{9,11},{10,... | collective-permute-start | bytes 374792 | tf_op jit(solution)/shard_map/ppermute | solution.py:203
  100.8 10.1 %shard_map.119 = f32[256,488]{1,0:T(8,128)S(1)} custom-call(s32[16,1024]{1,0:T(8,128)S(1)} %pad.59.slot_ref, bf16[1408,488]{1,0:T(8,128)(2,1)S(1)} %slice_dynamic-update-slice_fusion.buf_ref, bf16[10,488,488]{2,1,0:T(8,128)(2,1)} %k_ref.9, bf16[128,488]{1,0:T(8,128)(2,1)S(1)} %get-tuple-element.84.rest_0_, bf16[128,488]{1,0:T(8,128)(2,1)S(1)} %get-tuple-element.83.rest_1_, ...), custom_call_target="tpu_custom_call" | custom-call | flops 4737269760 | bytes 6137088 | tf_op jit(solution)/shard_map/pallas_call | solution.py:103
  111.0 1.9 %collective-permute-start.15 = (f32[64,488]{1,0:T(8,128)S(1)}, f32[64,488]{1,0:T(8,128)S(1)}, u32[]{:S(2)}, u32[]{:S(2)}) collective-permute-start(f32[64,488]{1,0:T(8,128)S(1)} %get-tuple-element.77), channel_id=1, source_target_pairs={{0,1},{1,2},{2,3},{3,0},{4,5},{5,6},{6,7},{7,4},{8,9},{9,10},{10,1... | collective-permute-start | bytes 374792 | tf_op jit(solution)/shard_map/ppermute | solution.py:203
  112.9 2.8 %collective-permute-start.17 = (f32[64,488]{1,0:T(8,128)S(1)}, f32[64,488]{1,0:T(8,128)S(1)}, u32[]{:S(2)}, u32[]{:S(2)}) collective-permute-start(f32[64,488]{1,0:T(8,128)S(1)} %get-tuple-element.78), channel_id=1, source_target_pairs={{0,3},{1,0},{2,1},{3,2},{4,7},{5,4},{6,5},{7,6},{8,11},{9,8},{10,9... | collective-permute-start | bytes 374792 | tf_op jit(solution)/shard_map/ppermute | solution.py:203
  115.7 1.5 %collective-permute-done.15 = f32[64,488]{1,0:T(8,128)S(1)} collective-permute-done((f32[64,488]{1,0:T(8,128)S(1)}, f32[64,488]{1,0:T(8,128)S(1)}, u32[]{:S(2)}, u32[]{:S(2)}) %collective-permute-start.15) | collective-permute-done | bytes 124960 | tf_op jit(solution)/shard_map/ppermute | solution.py:203
  117.2 2.1 %collective-permute-done.16 = f32[64,488]{1,0:T(8,128)S(1)} collective-permute-done((f32[64,488]{1,0:T(8,128)S(1)}, f32[64,488]{1,0:T(8,128)S(1)}, u32[]{:S(2)}, u32[]{:S(2)}) %collective-permute-start.16) | collective-permute-done | bytes 124960 | tf_op jit(solution)/shard_map/ppermute | solution.py:203
  119.9 1.0 copy.300
  (116 shorter events, 5.1 us)
Async XLA Ops:
  8.0 0.7 copy-start.6
  8.0 0.8 copy-start.1
  8.0 0.8 copy-start.2
  8.1 0.8 copy-start.3
  8.2 2.3 %copy-start.4 = (s32[1,10,128]{2,0,1:T(1,128)S(1)}, s32[1,10,128]{2,0,1:T(1,128)}, u32[]{:S(2)}) copy-start(s32[1,10,128]{2,0,1:T(1,128)} %param.18) | copy-start | bytes 15364
  8.2 2.3 %copy-start.7 = (s32[1,10]{1,0:T(1,128)S(1)}, s32[1,10]{1,0:T(1,128)}, u32[]{:S(2)}) copy-start(s32[1,10]{1,0:T(1,128)} %param.19) | copy-start | bytes 124
  8.2 2.5 %copy-start.5 = (s32[1,10,128]{2,0,1:T(1,128)S(1)}, s32[1,10,128]{2,0,1:T(1,128)}, u32[]{:S(2)}) copy-start(s32[1,10,128]{2,0,1:T(1,128)} %param.17) | copy-start | bytes 15364
  10.3 1.6 %collective-permute-start = (bf16[80,488]{1,0:T(8,128)(2,1)S(1)}, bf16[80,488]{1,0:T(8,128)(2,1)S(1)}, u32[]{:S(2)}, u32[]{:S(2)}) collective-permute-start(bf16[80,488]{1,0:T(8,128)(2,1)S(1)} %pad_maximum_fusion.1), channel_id=1, source_target_pairs={{0,4},{4,0},{8,12},{12,8},{16,20},{20,16},{24,28},{28,24},{32,36},... | collective-permute-start | bytes 234248 | tf_op jit(solution)/shard_map/ppermute | solution.py:18
  13.4 4.9 %collective-permute-start.1 = (bf16[80,488]{1,0:T(8,128)(2,1)S(1)}, bf16[80,488]{1,0:T(8,128)(2,1)S(1)}, u32[]{:S(2)}, u32[]{:S(2)}) collective-permute-start(bf16[80,488]{1,0:T(8,128)(2,1)S(1)} %pad_maximum_fusion.2), channel_id=1, source_target_pairs={{0,8},{8,0},{4,12},{12,4},{16,24},{24,16},{20,28},{28,20},{32,40},... | collective-permute-start | bytes 234248 | tf_op jit(solution)/shard_map/ppermute | solution.py:18
  19.8 6.0 %collective-permute-start.2 = (bf16[80,488]{1,0:T(8,128)(2,1)S(1)}, bf16[80,488]{1,0:T(8,128)(2,1)S(1)}, u32[]{:S(2)}, u32[]{:S(2)}) collective-permute-start(bf16[80,488]{1,0:T(8,128)(2,1)S(1)} %pad_maximum_fusion.3), channel_id=1, source_target_pairs={{0,16},{16,0},{4,20},{20,4},{8,24},{24,8},{12,28},{28,12},{32,48},... | collective-permute-start | bytes 234248 | tf_op jit(solution)/shard_map/ppermute | solution.py:18
  27.3 4.5 %collective-permute-start.3 = (bf16[80,488]{1,0:T(8,128)(2,1)S(1)}, bf16[80,488]{1,0:T(8,128)(2,1)S(1)}, u32[]{:S(2)}, u32[]{:S(2)}) collective-permute-start(bf16[80,488]{1,0:T(8,128)(2,1)S(1)} %pad_maximum_fusion.4), channel_id=1, source_target_pairs={{0,32},{32,0},{4,36},{36,4},{8,40},{40,8},{12,44},{44,12},{16,48},... | collective-permute-start | bytes 234248 | tf_op jit(solution)/shard_map/ppermute | solution.py:18
  33.3 6.0 %collective-permute-start.4 = (bf16[80,488]{1,0:T(8,128)(2,1)S(1)}, bf16[80,488]{1,0:T(8,128)(2,1)S(1)}, u32[]{:S(2)}, u32[]{:S(2)}) collective-permute-start(bf16[80,488]{1,0:T(8,128)(2,1)S(1)} %pad_maximum_fusion.5), channel_id=1, source_target_pairs={{0,64},{64,0},{4,68},{68,4},{8,72},{72,8},{12,76},{76,12},{16,80},... | collective-permute-start | bytes 234248 | tf_op jit(solution)/shard_map/ppermute | solution.py:18
  40.6 10.2 %collective-permute-start.5 = (bf16[80,488]{1,0:T(8,128)(2,1)S(1)}, bf16[80,488]{1,0:T(8,128)(2,1)S(1)}, u32[]{:S(2)}, u32[]{:S(2)}) collective-permute-start(bf16[80,488]{1,0:T(8,128)(2,1)S(1)} %pad_maximum_fusion.6), channel_id=1, source_target_pairs={{0,128},{128,0},{4,132},{132,4},{8,136},{136,8},{12,140},{140,12},... | collective-permute-start | bytes 234248 | tf_op jit(solution)/shard_map/ppermute | solution.py:18
  50.8 2.4 %copy-start = (bf16[10,488,488]{2,1,0:T(8,128)(2,1)S(1)}, bf16[10,488,488]{2,1,0:T(8,128)(2,1)}, u32[]{:S(2)}) copy-start(bf16[10,488,488]{2,1,0:T(8,128)(2,1)} %k_ref.9) | copy-start | bytes 14288644
  66.3 19.3 %collective-permute-start.6 = (f32[64,488]{1,0:T(8,128)S(1)}, f32[64,488]{1,0:T(8,128)S(1)}, u32[]{:S(2)}, u32[]{:S(2)}) collective-permute-start(f32[64,488]{1,0:T(8,128)S(1)} %get-tuple-element.74), channel_id=1, source_target_pairs={{0,1},{1,2},{2,3},{3,0},{4,5},{5,6},{6,7},{7,4},{8,9},{9,10},{10,1... | collective-permute-start | bytes 374792 | tf_op jit(solution)/shard_map/ppermute | solution.py:203
  67.8 17.7 %collective-permute-start.7 = (f32[64,488]{1,0:T(8,128)S(1)}, f32[64,488]{1,0:T(8,128)S(1)}, u32[]{:S(2)}, u32[]{:S(2)}) collective-permute-start(f32[64,488]{1,0:T(8,128)S(1)} %get-tuple-element.76), channel_id=1, source_target_pairs={{0,2},{1,3},{2,0},{3,1},{4,6},{5,7},{6,4},{7,5},{8,10},{9,11},{10,... | collective-permute-start | bytes 374792 | tf_op jit(solution)/shard_map/ppermute | solution.py:203
  70.6 15.0 %collective-permute-start.8 = (f32[64,488]{1,0:T(8,128)S(1)}, f32[64,488]{1,0:T(8,128)S(1)}, u32[]{:S(2)}, u32[]{:S(2)}) collective-permute-start(f32[64,488]{1,0:T(8,128)S(1)} %get-tuple-element.75), channel_id=1, source_target_pairs={{0,3},{1,0},{2,1},{3,2},{4,7},{5,4},{6,5},{7,6},{8,11},{9,8},{10,9... | collective-permute-start | bytes 374792 | tf_op jit(solution)/shard_map/ppermute | solution.py:203
  82.2 18.4 %collective-permute-start.10 = (f32[64,488]{1,0:T(8,128)S(1)}, f32[64,488]{1,0:T(8,128)S(1)}, u32[]{:S(2)}, u32[]{:S(2)}) collective-permute-start(f32[64,488]{1,0:T(8,128)S(1)} %get-tuple-element.82), channel_id=1, source_target_pairs={{0,2},{1,3},{2,0},{3,1},{4,6},{5,7},{6,4},{7,5},{8,10},{9,11},{10,... | collective-permute-start | bytes 374792 | tf_op jit(solution)/shard_map/ppermute | solution.py:203
  82.8 18.0 %collective-permute-start.11 = (f32[64,488]{1,0:T(8,128)S(1)}, f32[64,488]{1,0:T(8,128)S(1)}, u32[]{:S(2)}, u32[]{:S(2)}) collective-permute-start(f32[64,488]{1,0:T(8,128)S(1)} %get-tuple-element.81), channel_id=1, source_target_pairs={{0,3},{1,0},{2,1},{3,2},{4,7},{5,4},{6,5},{7,6},{8,11},{9,8},{10,9... | collective-permute-start | bytes 374792 | tf_op jit(solution)/shard_map/ppermute | solution.py:203
  85.5 15.2 %collective-permute-start.9 = (f32[64,488]{1,0:T(8,128)S(1)}, f32[64,488]{1,0:T(8,128)S(1)}, u32[]{:S(2)}, u32[]{:S(2)}) collective-permute-start(f32[64,488]{1,0:T(8,128)S(1)} %get-tuple-element.80), channel_id=1, source_target_pairs={{0,1},{1,2},{2,3},{3,0},{4,5},{5,6},{6,7},{7,4},{8,9},{9,10},{10,1... | collective-permute-start | bytes 374792 | tf_op jit(solution)/shard_map/ppermute | solution.py:203
  95.8 17.1 %collective-permute-start.12 = (f32[64,488]{1,0:T(8,128)S(1)}, f32[64,488]{1,0:T(8,128)S(1)}, u32[]{:S(2)}, u32[]{:S(2)}) collective-permute-start(f32[64,488]{1,0:T(8,128)S(1)} %get-tuple-element.71), channel_id=1, source_target_pairs={{0,1},{1,2},{2,3},{3,0},{4,5},{5,6},{6,7},{7,4},{8,9},{9,10},{10,1... | collective-permute-start | bytes 374792 | tf_op jit(solution)/shard_map/ppermute | solution.py:203
  96.1 19.6 %collective-permute-start.13 = (f32[64,488]{1,0:T(8,128)S(1)}, f32[64,488]{1,0:T(8,128)S(1)}, u32[]{:S(2)}, u32[]{:S(2)}) collective-permute-start(f32[64,488]{1,0:T(8,128)S(1)} %get-tuple-element.73), channel_id=1, source_target_pairs={{0,2},{1,3},{2,0},{3,1},{4,6},{5,7},{6,4},{7,5},{8,10},{9,11},{10,... | collective-permute-start | bytes 374792 | tf_op jit(solution)/shard_map/ppermute | solution.py:203
  100.5 15.1 %collective-permute-start.14 = (f32[64,488]{1,0:T(8,128)S(1)}, f32[64,488]{1,0:T(8,128)S(1)}, u32[]{:S(2)}, u32[]{:S(2)}) collective-permute-start(f32[64,488]{1,0:T(8,128)S(1)} %get-tuple-element.72), channel_id=1, source_target_pairs={{0,3},{1,0},{2,1},{3,2},{4,7},{5,4},{6,5},{7,6},{8,11},{9,8},{10,9... | collective-permute-start | bytes 374792 | tf_op jit(solution)/shard_map/ppermute | solution.py:203
  111.0 6.3 %collective-permute-start.15 = (f32[64,488]{1,0:T(8,128)S(1)}, f32[64,488]{1,0:T(8,128)S(1)}, u32[]{:S(2)}, u32[]{:S(2)}) collective-permute-start(f32[64,488]{1,0:T(8,128)S(1)} %get-tuple-element.77), channel_id=1, source_target_pairs={{0,1},{1,2},{2,3},{3,0},{4,5},{5,6},{6,7},{7,4},{8,9},{9,10},{10,1... | collective-permute-start | bytes 374792 | tf_op jit(solution)/shard_map/ppermute | solution.py:203
  112.9 6.5 %collective-permute-start.16 = (f32[64,488]{1,0:T(8,128)S(1)}, f32[64,488]{1,0:T(8,128)S(1)}, u32[]{:S(2)}, u32[]{:S(2)}) collective-permute-start(f32[64,488]{1,0:T(8,128)S(1)} %get-tuple-element.79), channel_id=1, source_target_pairs={{0,2},{1,3},{2,0},{3,1},{4,6},{5,7},{6,4},{7,5},{8,10},{9,11},{10,... | collective-permute-start | bytes 374792 | tf_op jit(solution)/shard_map/ppermute | solution.py:203
  112.9 6.6 %collective-permute-start.17 = (f32[64,488]{1,0:T(8,128)S(1)}, f32[64,488]{1,0:T(8,128)S(1)}, u32[]{:S(2)}, u32[]{:S(2)}) collective-permute-start(f32[64,488]{1,0:T(8,128)S(1)} %get-tuple-element.78), channel_id=1, source_target_pairs={{0,3},{1,0},{2,1},{3,2},{4,7},{5,4},{6,5},{7,6},{8,11},{9,8},{10,9... | collective-permute-start | bytes 374792 | tf_op jit(solution)/shard_map/ppermute | solution.py:203

commit v2 on v1

--- a/solution.py
+++ b/solution.py
@@ -137,11 +137,11 @@
     leaf_rows = boxes + rounds * leaf_ghost
     coarse_rows = parents + rounds * coarse_ghost
 
-    parent = jnp.dot(
-        multipoles.reshape(-1, 8 * width),
-        transfer.reshape(8 * width, width),
-        preferred_element_type=jnp.float32,
-    ).astype(jnp.bfloat16)
+    child = 8 * lax.broadcasted_iota(jnp.int32, (16, parents), 1) + lax.broadcasted_iota(
+        jnp.int32, (16, parents), 0
+    )
+    child = jnp.where(child % 8 == lax.broadcasted_iota(jnp.int32, (16, parents), 0), child, boxes)
+    parent = translate(child, multipoles, transfer, 0, parents).astype(jnp.bfloat16)
 
     coarse_slot = slot_table(coarse_target[0], coarse_source[0], coarse_count[0], coarse_rows)
     chunks = 4

time: 121 us -> 121 us (level)
  matrix products: 3.83 us -> 0 us
  Pallas kernels: 48.5 us -> 52 us
    dot_general x1 -> x0, matrix products: 3.83 us -> none  [on_device(): jnp.dot(multipoles.reshape(-1, 8 * width), transfer.reshape(8 * width, wi...]
    pallas_call x5 -> x6, Pallas kernels: 43.3 us -> 46.8 us  [translate(): pl.pallas_call(functools.partial(translate_kernel, spread is not None, de...]
    reshape x1 -> x0, local copies, waits for them, and re-layouts: 1.79 us -> none  [on_device(): multipoles.reshape(-1, 8 * width)]
    unnamed x20 -> x22, local copies, waits for them, and re-layouts: 4.49 us -> 6.07 us
  transfers between devices with their start and end apart: 18 -> 18, of which waited for: 8 -> 8; matrix products, arithmetic and copies ran while one was open for 1% -> 1% of each run, Pallas kernels for 29% -> 30%
where the time goes in v2:
time: 121 us; the launch traced here: 120 us
  Pallas kernels  52 us (43%)
  starting transfers between devices  35.8 us (30%)
  local copies, waits for them, and re-layouts  16.7 us (14%)
  waiting for transfers between devices  13.2 us (11%)
  other arithmetic  1.94 us (2%)
    pallas_call x6, Pallas kernels, translate(): pl.pallas_call(functools.partial(translate_kernel, spread is not None, de...  46.8 us
    ppermute x12, starting transfers between devices, on_device(): total = total + lax.ppermute(sent, 'off', route)  18.7 us
    ppermute x6, starting transfers between devices, partner(): return lax.ppermute(block, axis, route)  17.1 us
    ppermute x6, waiting for transfers between devices, partner(): return lax.ppermute(block, axis, route)  9.37 us
    unnamed x22, local copies, waits for them, and re-layouts  6.07 us
    pallas_call x6, Pallas kernels, slot_table(): pl.pallas_call(invert_kernel, out_shape=jax.ShapeDtypeStruct((classes, pa...  5.2 us
    gather x6, local copies, waits for them, and re-layouts, on_device(): buffer[ghost_send[0, bit_index]]  4.21 us
    ppermute x12, waiting for transfers between devices, on_device(): total = total + lax.ppermute(sent, 'off', route)  3.82 us
  transfers between devices with their start and end apart: 18, of which 8 were waited for; matrix products, arithmetic and copies ran while one was open for 1% of the time, Pallas kernels for 30%

profile of v2, /device:TPU:16, one launch (start us, length us, event | category | flops | bytes accessed | tf_op | source)
XLA Modules:
  0.0 120.4 jit_solution(492757191938472564)
XLA Ops:
  0.0 0.8 fusion.53
  0.8 1.5 %copy.242.buf_ref = bf16[1024,488]{1,0:T(8,128)(2,1)S(1)} copy(bf16[1024,488]{0,1:T(8,128)(2,1)} %param.11) | data formatting | bytes 1998848 | tf_op args[0]
  2.5 2.1 %copy-done.1 = bf16[8,488,488]{2,1,0:T(8,128)(2,1)S(1)} copy-done((bf16[8,488,488]{2,1,0:T(8,128)(2,1)S(1)}, bf16[8,488,488]{2,1,0:T(8,128)(2,1)}, u32[]{:S(2)}) %copy-start.1) | copy-done | bytes 3810328
  4.6 3.5 %shard_map.109 = f32[128,488]{1,0:T(8,128)S(1)} custom-call(s32[16,128]{1,0:T(8,128)S(1)} %fusion.18.slot_ref, bf16[1024,488]{1,0:T(8,128)(2,1)S(1)} %copy.242.buf_ref, bf16[8,488,488]{2,1,0:T(8,128)(2,1)S(1)} %copy-done.1), custom_call_target="tpu_custom_call" | custom-call | flops 1511129088 | bytes 4809728 | tf_op jit(solution)/shard_map/pallas_call | solution.py:103
  8.4 0.7 gather_fusion
  9.1 0.6 gather_fusion.1
  10.2 0.9 shard_map.110
  11.3 0.7 gather_fusion.2
  12.0 0.6 gather_fusion.3
  12.8 1.4 %collective-permute-start.1 = (bf16[80,488]{1,0:T(8,128)(2,1)S(1)}, bf16[80,488]{1,0:T(8,128)(2,1)S(1)}, u32[]{:S(2)}, u32[]{:S(2)}) collective-permute-start(bf16[80,488]{1,0:T(8,128)(2,1)S(1)} %pad_maximum_fusion.2), channel_id=1, source_target_pairs={{0,8},{8,0},{4,12},{12,4},{16,24},{24,16},{20,28},{28,20},{32,40},... | collective-permute-start | bytes 234248 | tf_op jit(solution)/shard_map/ppermute | solution.py:18
  14.2 0.9 shard_map.111
  15.1 2.6 %collective-permute-done.1 = bf16[80,488]{1,0:T(8,128)(2,1)S(1)} collective-permute-done((bf16[80,488]{1,0:T(8,128)(2,1)S(1)}, bf16[80,488]{1,0:T(8,128)(2,1)S(1)}, u32[]{:S(2)}, u32[]{:S(2)}) %collective-permute-start.1) | collective-permute-done | bytes 78112 | tf_op jit(solution)/shard_map/ppermute | solution.py:18
  17.7 0.7 gather_fusion.4
  18.4 0.6 gather_fusion.5
  19.2 2.2 %collective-permute-start.2 = (bf16[80,488]{1,0:T(8,128)(2,1)S(1)}, bf16[80,488]{1,0:T(8,128)(2,1)S(1)}, u32[]{:S(2)}, u32[]{:S(2)}) collective-permute-start(bf16[80,488]{1,0:T(8,128)(2,1)S(1)} %pad_maximum_fusion.3), channel_id=1, source_target_pairs={{0,16},{16,0},{4,20},{20,4},{8,24},{24,8},{12,28},{28,12},{32,48},... | collective-permute-start | bytes 234248 | tf_op jit(solution)/shard_map/ppermute | solution.py:18
  21.4 0.9 shard_map.112
  22.3 2.9 %collective-permute-done.2 = bf16[80,488]{1,0:T(8,128)(2,1)S(1)} collective-permute-done((bf16[80,488]{1,0:T(8,128)(2,1)S(1)}, bf16[80,488]{1,0:T(8,128)(2,1)S(1)}, u32[]{:S(2)}, u32[]{:S(2)}) %collective-permute-start.2) | collective-permute-done | bytes 78112 | tf_op jit(solution)/shard_map/ppermute | solution.py:18
  25.2 0.7 gather_fusion.6
  25.9 0.6 gather_fusion.7
  26.7 2.0 %collective-permute-start.3 = (bf16[80,488]{1,0:T(8,128)(2,1)S(1)}, bf16[80,488]{1,0:T(8,128)(2,1)S(1)}, u32[]{:S(2)}, u32[]{:S(2)}) collective-permute-start(bf16[80,488]{1,0:T(8,128)(2,1)S(1)} %pad_maximum_fusion.4), channel_id=1, source_target_pairs={{0,32},{32,0},{4,36},{36,4},{8,40},{40,8},{12,44},{44,12},{16,48},... | collective-permute-start | bytes 234248 | tf_op jit(solution)/shard_map/ppermute | solution.py:18
  28.7 0.9 shard_map.113
  29.7 1.6 %collective-permute-done.3 = bf16[80,488]{1,0:T(8,128)(2,1)S(1)} collective-permute-done((bf16[80,488]{1,0:T(8,128)(2,1)S(1)}, bf16[80,488]{1,0:T(8,128)(2,1)S(1)}, u32[]{:S(2)}, u32[]{:S(2)}) %collective-permute-start.3) | collective-permute-done | bytes 78112 | tf_op jit(solution)/shard_map/ppermute | solution.py:18
  31.2 0.7 gather_fusion.8
  31.9 0.6 gather_fusion.9
  32.7 3.4 %collective-permute-start.4 = (bf16[80,488]{1,0:T(8,128)(2,1)S(1)}, bf16[80,488]{1,0:T(8,128)(2,1)S(1)}, u32[]{:S(2)}, u32[]{:S(2)}) collective-permute-start(bf16[80,488]{1,0:T(8,128)(2,1)S(1)} %pad_maximum_fusion.5), channel_id=1, source_target_pairs={{0,64},{64,0},{4,68},{68,4},{8,72},{72,8},{12,76},{76,12},{16,80},... | collective-permute-start | bytes 234248 | tf_op jit(solution)/shard_map/ppermute | solution.py:18
  36.1 0.9 shard_map.114
  37.0 1.5 %collective-permute-done.4 = bf16[80,488]{1,0:T(8,128)(2,1)S(1)} collective-permute-done((bf16[80,488]{1,0:T(8,128)(2,1)S(1)}, bf16[80,488]{1,0:T(8,128)(2,1)S(1)}, u32[]{:S(2)}, u32[]{:S(2)}) %collective-permute-start.4) | collective-permute-done | bytes 78112 | tf_op jit(solution)/shard_map/ppermute | solution.py:18
  38.5 0.6 gather_fusion.11
  39.1 0.7 gather_fusion.10
  39.8 8.1 %collective-permute-start.5 = (bf16[80,488]{1,0:T(8,128)(2,1)S(1)}, bf16[80,488]{1,0:T(8,128)(2,1)S(1)}, u32[]{:S(2)}, u32[]{:S(2)}) collective-permute-start(bf16[80,488]{1,0:T(8,128)(2,1)S(1)} %pad_maximum_fusion.6), channel_id=1, source_target_pairs={{0,128},{128,0},{4,132},{132,4},{8,136},{136,8},{12,140},{140,12},... | collective-permute-start | bytes 234248 | tf_op jit(solution)/shard_map/ppermute | solution.py:18
  49.4 0.9 collective-permute-done.5
  50.3 2.4 %copy-done = bf16[10,488,488]{2,1,0:T(8,128)(2,1)S(1)} copy-done((bf16[10,488,488]{2,1,0:T(8,128)(2,1)S(1)}, bf16[10,488,488]{2,1,0:T(8,128)(2,1)}, u32[]{:S(2)}) %copy-start) | copy-done | bytes 4762904
  52.7 2.8 %shard_map.116 = f32[128,488]{1,0:T(8,128)S(1)} custom-call(s32[16,128]{1,0:T(8,128)S(1)} %pad.62.slot_ref, bf16[224,488]{1,0:T(8,128)(2,1)S(1)} %slice_dynamic-update-slice_fusion.6.buf_ref, bf16[10,488,488]{2,1,0:T(8,128)(2,1)S(1)} %copy-done), custom_call_target="tpu_custom_call" | custom-call | flops 889487360 | bytes 4981504 | tf_op jit(solution)/shard_map/pallas_call | solution.py:103
  55.6 10.1 %shard_map.117 = f32[256,488]{1,0:T(8,128)S(1)} custom-call(s32[16,1024]{1,0:T(8,128)S(1)} %pad.59.slot_ref, bf16[1408,488]{1,0:T(8,128)(2,1)S(1)} %slice_dynamic-update-slice_fusion.buf_ref, bf16[10,488,488]{2,1,0:T(8,128)(2,1)} %k_ref.11, bf16[128,488]{1,0:T(8,128)(2,1)S(1)} %get-tuple-element.84.rest_0_, bf16[128,488]{1,0:T(8,128)(2,1)S(1)} %get-tuple-element.83.rest_1_, ...), custom_call_target="tpu_custom_call" | custom-call | flops 4737269760 | bytes 6137088 | tf_op jit(solution)/shard_map/pallas_call | solution.py:103
  65.8 1.6 %collective-permute-start.6 = (f32[64,488]{1,0:T(8,128)S(1)}, f32[64,488]{1,0:T(8,128)S(1)}, u32[]{:S(2)}, u32[]{:S(2)}) collective-permute-start(f32[64,488]{1,0:T(8,128)S(1)} %get-tuple-element.74), channel_id=1, source_target_pairs={{0,1},{1,2},{2,3},{3,0},{4,5},{5,6},{6,7},{7,4},{8,9},{9,10},{10,1... | collective-permute-start | bytes 374792 | tf_op jit(solution)/shard_map/ppermute | solution.py:203
  67.4 2.7 %collective-permute-start.7 = (f32[64,488]{1,0:T(8,128)S(1)}, f32[64,488]{1,0:T(8,128)S(1)}, u32[]{:S(2)}, u32[]{:S(2)}) collective-permute-start(f32[64,488]{1,0:T(8,128)S(1)} %get-tuple-element.76), channel_id=1, source_target_pairs={{0,2},{1,3},{2,0},{3,1},{4,6},{5,7},{6,4},{7,5},{8,10},{9,11},{10,... | collective-permute-start | bytes 374792 | tf_op jit(solution)/shard_map/ppermute | solution.py:203
  70.1 1.4 %collective-permute-start.8 = (f32[64,488]{1,0:T(8,128)S(1)}, f32[64,488]{1,0:T(8,128)S(1)}, u32[]{:S(2)}, u32[]{:S(2)}) collective-permute-start(f32[64,488]{1,0:T(8,128)S(1)} %get-tuple-element.75), channel_id=1, source_target_pairs={{0,3},{1,0},{2,1},{3,2},{4,7},{5,4},{6,5},{7,6},{8,11},{9,8},{10,9... | collective-permute-start | bytes 374792 | tf_op jit(solution)/shard_map/ppermute | solution.py:203
  71.5 10.1 %shard_map.118 = f32[256,488]{1,0:T(8,128)S(1)} custom-call(s32[16,1024]{1,0:T(8,128)S(1)} %pad.59.slot_ref, bf16[1408,488]{1,0:T(8,128)(2,1)S(1)} %slice_dynamic-update-slice_fusion.buf_ref, bf16[10,488,488]{2,1,0:T(8,128)(2,1)} %k_ref.11, bf16[128,488]{1,0:T(8,128)(2,1)S(1)} %get-tuple-element.84.rest_0_, bf16[128,488]{1,0:T(8,128)(2,1)S(1)} %get-tuple-element.83.rest_1_, ...), custom_call_target="tpu_custom_call" | custom-call | flops 4737269760 | bytes 6137088 | tf_op jit(solution)/shard_map/pallas_call | solution.py:103
  81.7 0.6 collective-permute-start.10
  82.3 2.8 %collective-permute-start.11 = (f32[64,488]{1,0:T(8,128)S(1)}, f32[64,488]{1,0:T(8,128)S(1)}, u32[]{:S(2)}, u32[]{:S(2)}) collective-permute-start(f32[64,488]{1,0:T(8,128)S(1)} %get-tuple-element.81), channel_id=1, source_target_pairs={{0,3},{1,0},{2,1},{3,2},{4,7},{5,4},{6,5},{7,6},{8,11},{9,8},{10,9... | collective-permute-start | bytes 374792 | tf_op jit(solution)/shard_map/ppermute | solution.py:203
  85.1 10.1 %shard_map.119 = f32[256,488]{1,0:T(8,128)S(1)} custom-call(s32[16,1024]{1,0:T(8,128)S(1)} %pad.59.slot_ref, bf16[1408,488]{1,0:T(8,128)(2,1)S(1)} %slice_dynamic-update-slice_fusion.buf_ref, bf16[10,488,488]{2,1,0:T(8,128)(2,1)} %k_ref.11, bf16[128,488]{1,0:T(8,128)(2,1)S(1)} %get-tuple-element.84.rest_0_, bf16[128,488]{1,0:T(8,128)(2,1)S(1)} %get-tuple-element.83.rest_1_, ...), custom_call_target="tpu_custom_call" | custom-call | flops 4737269760 | bytes 6137088 | tf_op jit(solution)/shard_map/pallas_call | solution.py:103
  95.6 4.5 %collective-permute-start.13 = (f32[64,488]{1,0:T(8,128)S(1)}, f32[64,488]{1,0:T(8,128)S(1)}, u32[]{:S(2)}, u32[]{:S(2)}) collective-permute-start(f32[64,488]{1,0:T(8,128)S(1)} %get-tuple-element.73), channel_id=1, source_target_pairs={{0,2},{1,3},{2,0},{3,1},{4,6},{5,7},{6,4},{7,5},{8,10},{9,11},{10,... | collective-permute-start | bytes 374792 | tf_op jit(solution)/shard_map/ppermute | solution.py:203
  100.3 10.1 %shard_map.120 = f32[256,488]{1,0:T(8,128)S(1)} custom-call(s32[16,1024]{1,0:T(8,128)S(1)} %pad.59.slot_ref, bf16[1408,488]{1,0:T(8,128)(2,1)S(1)} %slice_dynamic-update-slice_fusion.buf_ref, bf16[10,488,488]{2,1,0:T(8,128)(2,1)} %k_ref.11, bf16[128,488]{1,0:T(8,128)(2,1)S(1)} %get-tuple-element.84.rest_0_, bf16[128,488]{1,0:T(8,128)(2,1)S(1)} %get-tuple-element.83.rest_1_, ...), custom_call_target="tpu_custom_call" | custom-call | flops 4737269760 | bytes 6137088 | tf_op jit(solution)/shard_map/pallas_call | solution.py:103
  110.5 1.9 %collective-permute-start.15 = (f32[64,488]{1,0:T(8,128)S(1)}, f32[64,488]{1,0:T(8,128)S(1)}, u32[]{:S(2)}, u32[]{:S(2)}) collective-permute-start(f32[64,488]{1,0:T(8,128)S(1)} %get-tuple-element.77), channel_id=1, source_target_pairs={{0,1},{1,2},{2,3},{3,0},{4,5},{5,6},{6,7},{7,4},{8,9},{9,10},{10,1... | collective-permute-start | bytes 374792 | tf_op jit(solution)/shard_map/ppermute | solution.py:203
  112.4 2.8 %collective-permute-start.17 = (f32[64,488]{1,0:T(8,128)S(1)}, f32[64,488]{1,0:T(8,128)S(1)}, u32[]{:S(2)}, u32[]{:S(2)}) collective-permute-start(f32[64,488]{1,0:T(8,128)S(1)} %get-tuple-element.78), channel_id=1, source_target_pairs={{0,3},{1,0},{2,1},{3,2},{4,7},{5,4},{6,5},{7,6},{8,11},{9,8},{10,9... | collective-permute-start | bytes 374792 | tf_op jit(solution)/shard_map/ppermute | solution.py:203
  115.2 1.5 %collective-permute-done.15 = f32[64,488]{1,0:T(8,128)S(1)} collective-permute-done((f32[64,488]{1,0:T(8,128)S(1)}, f32[64,488]{1,0:T(8,128)S(1)}, u32[]{:S(2)}, u32[]{:S(2)}) %collective-permute-start.15) | collective-permute-done | bytes 124960 | tf_op jit(solution)/shard_map/ppermute | solution.py:203
  116.8 2.1 %collective-permute-done.16 = f32[64,488]{1,0:T(8,128)S(1)} collective-permute-done((f32[64,488]{1,0:T(8,128)S(1)}, f32[64,488]{1,0:T(8,128)S(1)}, u32[]{:S(2)}, u32[]{:S(2)}) %collective-permute-start.16) | collective-permute-done | bytes 124960 | tf_op jit(solution)/shard_map/ppermute | solution.py:203
  119.4 1.0 copy.264
  (119 shorter events, 4.4 us)
Async XLA Ops:
  0.0 2.2 %copy-start.7 = (s32[1,6,16]{2,0,1:T(1,128)S(1)}, s32[1,6,16]{2,0,1:T(1,128)}, u32[]{:S(2)}) copy-start(s32[1,6,16]{2,0,1:T(1,128)} %param.21) | copy-start | bytes 1156
  2.4 2.1 %copy-start.1 = (bf16[8,488,488]{2,1,0:T(8,128)(2,1)S(1)}, bf16[8,488,488]{2,1,0:T(8,128)(2,1)}, u32[]{:S(2)}) copy-start(bf16[8,488,488]{2,1,0:T(8,128)(2,1)} %rest_2_.7) | copy-start | bytes 11430916
  4.6 3.6 %copy-start.2 = (s32[1,10,1024]{2,0,1:T(1,128)S(1)}, s32[1,10,1024]{2,0,1:T(1,128)}, u32[]{:S(2)}) copy-start(s32[1,10,1024]{2,0,1:T(1,128)} %param.15) | copy-start | bytes 122884
  4.6 3.7 %copy-start.3 = (s32[1,10,1024]{2,0,1:T(1,128)S(1)}, s32[1,10,1024]{2,0,1:T(1,128)}, u32[]{:S(2)}) copy-start(s32[1,10,1024]{2,0,1:T(1,128)} %param.14) | copy-start | bytes 122884
  4.6 3.7 %copy-start.4 = (s32[1,10]{1,0:T(1,128)S(1)}, s32[1,10]{1,0:T(1,128)}, u32[]{:S(2)}) copy-start(s32[1,10]{1,0:T(1,128)} %param.16) | copy-start | bytes 124
  8.1 1.9 %copy-start.5 = (s32[1,10,128]{2,0,1:T(1,128)S(1)}, s32[1,10,128]{2,0,1:T(1,128)}, u32[]{:S(2)}) copy-start(s32[1,10,128]{2,0,1:T(1,128)} %param.18) | copy-start | bytes 15364
  8.1 1.9 %copy-start.8 = (s32[1,10]{1,0:T(1,128)S(1)}, s32[1,10]{1,0:T(1,128)}, u32[]{:S(2)}) copy-start(s32[1,10]{1,0:T(1,128)} %param.19) | copy-start | bytes 124
  8.1 2.0 %copy-start.6 = (s32[1,10,128]{2,0,1:T(1,128)S(1)}, s32[1,10,128]{2,0,1:T(1,128)}, u32[]{:S(2)}) copy-start(s32[1,10,128]{2,0,1:T(1,128)} %param.17) | copy-start | bytes 15364
  9.7 1.6 %collective-permute-start = (bf16[80,488]{1,0:T(8,128)(2,1)S(1)}, bf16[80,488]{1,0:T(8,128)(2,1)S(1)}, u32[]{:S(2)}, u32[]{:S(2)}) collective-permute-start(bf16[80,488]{1,0:T(8,128)(2,1)S(1)} %pad_maximum_fusion.1), channel_id=1, source_target_pairs={{0,4},{4,0},{8,12},{12,8},{16,20},{20,16},{24,28},{28,24},{32,36},... | collective-permute-start | bytes 234248 | tf_op jit(solution)/shard_map/ppermute | solution.py:18
  12.8 4.9 %collective-permute-start.1 = (bf16[80,488]{1,0:T(8,128)(2,1)S(1)}, bf16[80,488]{1,0:T(8,128)(2,1)S(1)}, u32[]{:S(2)}, u32[]{:S(2)}) collective-permute-start(bf16[80,488]{1,0:T(8,128)(2,1)S(1)} %pad_maximum_fusion.2), channel_id=1, source_target_pairs={{0,8},{8,0},{4,12},{12,4},{16,24},{24,16},{20,28},{28,20},{32,40},... | collective-permute-start | bytes 234248 | tf_op jit(solution)/shard_map/ppermute | solution.py:18
  19.2 6.0 %collective-permute-start.2 = (bf16[80,488]{1,0:T(8,128)(2,1)S(1)}, bf16[80,488]{1,0:T(8,128)(2,1)S(1)}, u32[]{:S(2)}, u32[]{:S(2)}) collective-permute-start(bf16[80,488]{1,0:T(8,128)(2,1)S(1)} %pad_maximum_fusion.3), channel_id=1, source_target_pairs={{0,16},{16,0},{4,20},{20,4},{8,24},{24,8},{12,28},{28,12},{32,48},... | collective-permute-start | bytes 234248 | tf_op jit(solution)/shard_map/ppermute | solution.py:18
  26.7 4.5 %collective-permute-start.3 = (bf16[80,488]{1,0:T(8,128)(2,1)S(1)}, bf16[80,488]{1,0:T(8,128)(2,1)S(1)}, u32[]{:S(2)}, u32[]{:S(2)}) collective-permute-start(bf16[80,488]{1,0:T(8,128)(2,1)S(1)} %pad_maximum_fusion.4), channel_id=1, source_target_pairs={{0,32},{32,0},{4,36},{36,4},{8,40},{40,8},{12,44},{44,12},{16,48},... | collective-permute-start | bytes 234248 | tf_op jit(solution)/shard_map/ppermute | solution.py:18
  32.7 5.8 %collective-permute-start.4 = (bf16[80,488]{1,0:T(8,128)(2,1)S(1)}, bf16[80,488]{1,0:T(8,128)(2,1)S(1)}, u32[]{:S(2)}, u32[]{:S(2)}) collective-permute-start(bf16[80,488]{1,0:T(8,128)(2,1)S(1)} %pad_maximum_fusion.5), channel_id=1, source_target_pairs={{0,64},{64,0},{4,68},{68,4},{8,72},{72,8},{12,76},{76,12},{16,80},... | collective-permute-start | bytes 234248 | tf_op jit(solution)/shard_map/ppermute | solution.py:18
  39.8 10.5 %collective-permute-start.5 = (bf16[80,488]{1,0:T(8,128)(2,1)S(1)}, bf16[80,488]{1,0:T(8,128)(2,1)S(1)}, u32[]{:S(2)}, u32[]{:S(2)}) collective-permute-start(bf16[80,488]{1,0:T(8,128)(2,1)S(1)} %pad_maximum_fusion.6), channel_id=1, source_target_pairs={{0,128},{128,0},{4,132},{132,4},{8,136},{136,8},{12,140},{140,12},... | collective-permute-start | bytes 234248 | tf_op jit(solution)/shard_map/ppermute | solution.py:18
  50.3 2.4 %copy-start = (bf16[10,488,488]{2,1,0:T(8,128)(2,1)S(1)}, bf16[10,488,488]{2,1,0:T(8,128)(2,1)}, u32[]{:S(2)}) copy-start(bf16[10,488,488]{2,1,0:T(8,128)(2,1)} %k_ref.11) | copy-start | bytes 14288644
  65.8 19.3 %collective-permute-start.6 = (f32[64,488]{1,0:T(8,128)S(1)}, f32[64,488]{1,0:T(8,128)S(1)}, u32[]{:S(2)}, u32[]{:S(2)}) collective-permute-start(f32[64,488]{1,0:T(8,128)S(1)} %get-tuple-element.74), channel_id=1, source_target_pairs={{0,1},{1,2},{2,3},{3,0},{4,5},{5,6},{6,7},{7,4},{8,9},{9,10},{10,1... | collective-permute-start | bytes 374792 | tf_op jit(solution)/shard_map/ppermute | solution.py:203
  67.4 17.7 %collective-permute-start.7 = (f32[64,488]{1,0:T(8,128)S(1)}, f32[64,488]{1,0:T(8,128)S(1)}, u32[]{:S(2)}, u32[]{:S(2)}) collective-permute-start(f32[64,488]{1,0:T(8,128)S(1)} %get-tuple-element.76), channel_id=1, source_target_pairs={{0,2},{1,3},{2,0},{3,1},{4,6},{5,7},{6,4},{7,5},{8,10},{9,11},{10,... | collective-permute-start | bytes 374792 | tf_op jit(solution)/shard_map/ppermute | solution.py:203
  70.1 15.0 %collective-permute-start.8 = (f32[64,488]{1,0:T(8,128)S(1)}, f32[64,488]{1,0:T(8,128)S(1)}, u32[]{:S(2)}, u32[]{:S(2)}) collective-permute-start(f32[64,488]{1,0:T(8,128)S(1)} %get-tuple-element.75), channel_id=1, source_target_pairs={{0,3},{1,0},{2,1},{3,2},{4,7},{5,4},{6,5},{7,6},{8,11},{9,8},{10,9... | collective-permute-start | bytes 374792 | tf_op jit(solution)/shard_map/ppermute | solution.py:203
  81.7 18.4 %collective-permute-start.10 = (f32[64,488]{1,0:T(8,128)S(1)}, f32[64,488]{1,0:T(8,128)S(1)}, u32[]{:S(2)}, u32[]{:S(2)}) collective-permute-start(f32[64,488]{1,0:T(8,128)S(1)} %get-tuple-element.82), channel_id=1, source_target_pairs={{0,2},{1,3},{2,0},{3,1},{4,6},{5,7},{6,4},{7,5},{8,10},{9,11},{10,... | collective-permute-start | bytes 374792 | tf_op jit(solution)/shard_map/ppermute | solution.py:203
  82.3 18.0 %collective-permute-start.11 = (f32[64,488]{1,0:T(8,128)S(1)}, f32[64,488]{1,0:T(8,128)S(1)}, u32[]{:S(2)}, u32[]{:S(2)}) collective-permute-start(f32[64,488]{1,0:T(8,128)S(1)} %get-tuple-element.81), channel_id=1, source_target_pairs={{0,3},{1,0},{2,1},{3,2},{4,7},{5,4},{6,5},{7,6},{8,11},{9,8},{10,9... | collective-permute-start | bytes 374792 | tf_op jit(solution)/shard_map/ppermute | solution.py:203
  85.0 15.2 %collective-permute-start.9 = (f32[64,488]{1,0:T(8,128)S(1)}, f32[64,488]{1,0:T(8,128)S(1)}, u32[]{:S(2)}, u32[]{:S(2)}) collective-permute-start(f32[64,488]{1,0:T(8,128)S(1)} %get-tuple-element.80), channel_id=1, source_target_pairs={{0,1},{1,2},{2,3},{3,0},{4,5},{5,6},{6,7},{7,4},{8,9},{9,10},{10,1... | collective-permute-start | bytes 374792 | tf_op jit(solution)/shard_map/ppermute | solution.py:203
  95.3 17.1 %collective-permute-start.12 = (f32[64,488]{1,0:T(8,128)S(1)}, f32[64,488]{1,0:T(8,128)S(1)}, u32[]{:S(2)}, u32[]{:S(2)}) collective-permute-start(f32[64,488]{1,0:T(8,128)S(1)} %get-tuple-element.71), channel_id=1, source_target_pairs={{0,1},{1,2},{2,3},{3,0},{4,5},{5,6},{6,7},{7,4},{8,9},{9,10},{10,1... | collective-permute-start | bytes 374792 | tf_op jit(solution)/shard_map/ppermute | solution.py:203
  95.6 19.6 %collective-permute-start.13 = (f32[64,488]{1,0:T(8,128)S(1)}, f32[64,488]{1,0:T(8,128)S(1)}, u32[]{:S(2)}, u32[]{:S(2)}) collective-permute-start(f32[64,488]{1,0:T(8,128)S(1)} %get-tuple-element.73), channel_id=1, source_target_pairs={{0,2},{1,3},{2,0},{3,1},{4,6},{5,7},{6,4},{7,5},{8,10},{9,11},{10,... | collective-permute-start | bytes 374792 | tf_op jit(solution)/shard_map/ppermute | solution.py:203
  100.1 15.1 %collective-permute-start.14 = (f32[64,488]{1,0:T(8,128)S(1)}, f32[64,488]{1,0:T(8,128)S(1)}, u32[]{:S(2)}, u32[]{:S(2)}) collective-permute-start(f32[64,488]{1,0:T(8,128)S(1)} %get-tuple-element.72), channel_id=1, source_target_pairs={{0,3},{1,0},{2,1},{3,2},{4,7},{5,4},{6,5},{7,6},{8,11},{9,8},{10,9... | collective-permute-start | bytes 374792 | tf_op jit(solution)/shard_map/ppermute | solution.py:203
  110.5 6.3 %collective-permute-start.15 = (f32[64,488]{1,0:T(8,128)S(1)}, f32[64,488]{1,0:T(8,128)S(1)}, u32[]{:S(2)}, u32[]{:S(2)}) collective-permute-start(f32[64,488]{1,0:T(8,128)S(1)} %get-tuple-element.77), channel_id=1, source_target_pairs={{0,1},{1,2},{2,3},{3,0},{4,5},{5,6},{6,7},{7,4},{8,9},{9,10},{10,1... | collective-permute-start | bytes 374792 | tf_op jit(solution)/shard_map/ppermute | solution.py:203
  112.4 6.5 %collective-permute-start.16 = (f32[64,488]{1,0:T(8,128)S(1)}, f32[64,488]{1,0:T(8,128)S(1)}, u32[]{:S(2)}, u32[]{:S(2)}) collective-permute-start(f32[64,488]{1,0:T(8,128)S(1)} %get-tuple-element.79), channel_id=1, source_target_pairs={{0,2},{1,3},{2,0},{3,1},{4,6},{5,7},{6,4},{7,5},{8,10},{9,11},{10,... | collective-permute-start | bytes 374792 | tf_op jit(solution)/shard_map/ppermute | solution.py:203
  112.4 6.6 %collective-permute-start.17 = (f32[64,488]{1,0:T(8,128)S(1)}, f32[64,488]{1,0:T(8,128)S(1)}, u32[]{:S(2)}, u32[]{:S(2)}) collective-permute-start(f32[64,488]{1,0:T(8,128)S(1)} %get-tuple-element.78), channel_id=1, source_target_pairs={{0,3},{1,0},{2,1},{3,2},{4,7},{5,4},{6,5},{7,6},{8,11},{9,8},{10,9... | collective-permute-start | bytes 374792 | tf_op jit(solution)/shard_map/ppermute | solution.py:203

commit v3 on v2

--- a/solution.py
+++ b/solution.py
@@ -81,12 +81,13 @@
     lax.fori_loop(0, k_ref.shape[0], one_class, 0, unroll=5)
 
 
-def translate(slot, buffer, kernels, chunk, tile, spread=None, devices=1):
+def translate(slot, buffer, kernels, chunk, tile, spread=None, devices=1, rows=None, row_block=0):
     classes = kernels.shape[0]
-    rows, width = buffer.shape
+    width = buffer.shape[1]
+    rows = rows or buffer.shape[0]
     in_specs = [
         pl.BlockSpec((slot.shape[0], tile), lambda g: (0, chunk)),
-        pl.BlockSpec((rows, width), lambda g: (0, 0)),
+        pl.BlockSpec((rows, width), lambda g: (row_block, 0)),
         pl.BlockSpec((classes, width, width), lambda g: (0, 0, 0)),
     ]
     operands = [slot, buffer, kernels]
@@ -150,17 +151,16 @@
     per = 8 // chunks
     coarse_slot = jnp.pad(coarse_slot, ((0, 16 - classes), (0, 0)), constant_values=coarse_rows)
 
-    buffer = jnp.zeros((leaf_rows, width), multipoles.dtype)
-    buffer = lax.dynamic_update_slice(buffer, multipoles, (0, 0))
-    coarse_buffer = jnp.zeros((coarse_rows, width), parent.dtype)
-    coarse_buffer = lax.dynamic_update_slice(coarse_buffer, parent, (0, 0))
+    leaf_region = -(-leaf_rows // coarse_rows) * coarse_rows
+    rows_all = jnp.zeros((leaf_region + coarse_rows, width), multipoles.dtype)
+    rows_all = lax.dynamic_update_slice(rows_all, multipoles, (0, 0))
+    rows_all = lax.dynamic_update_slice(rows_all, parent, (leaf_region, 0))
     group = -(-classes // (rounds - 1))
     groups = [(low, min(low + group, classes)) for low in range(0, classes, group)]
     slot_parts = []
     for bit_index in range(rounds):
-        outgoing = jnp.concatenate(
-            [buffer[ghost_send[0, bit_index]], coarse_buffer[coarse_send[0, bit_index]]], axis=0
-        )
+        picks = jnp.concatenate([ghost_send[0, bit_index], coarse_send[0, bit_index] + leaf_region])
+        outgoing = rows_all[picks]
         if bit_index < len(groups):
             low, high = groups[bit_index]
             tables, outgoing = lax.optimization_barrier(
@@ -170,18 +170,20 @@
         if bit_index < len(groups):
             part, arrived = lax.optimization_barrier((slot_table(*tables, leaf_rows), arrived))
             slot_parts.append(part)
-        buffer = lax.dynamic_update_slice(
-            buffer, arrived[:leaf_ghost], (boxes + bit_index * leaf_ghost, 0)
-        )
-        coarse_buffer = lax.dynamic_update_slice(
-            coarse_buffer, arrived[leaf_ghost:], (parents + bit_index * coarse_ghost, 0)
+        rows_all = lax.dynamic_update_slice(
+            rows_all, arrived[:leaf_ghost], (boxes + bit_index * leaf_ghost, 0)
+        )
+        rows_all = lax.dynamic_update_slice(
+            rows_all, arrived[leaf_ghost:], (leaf_region + parents + bit_index * coarse_ghost, 0)
         )
 
     leaf_slot = jnp.concatenate(slot_parts, axis=0)
     leaf_slot = leaf_slot.reshape(classes, devices, span, chunks, per)
     leaf_slot = leaf_slot.transpose(0, 3, 1, 4, 2).reshape(classes, boxes)
     leaf_slot = jnp.pad(leaf_slot, ((0, 16 - classes), (0, 0)), constant_values=leaf_rows)
-    coarse_local = 0.5 * translate(coarse_slot, coarse_buffer, kernels, 0, parents)
+    coarse_local = 0.5 * translate(
+        coarse_slot, rows_all, kernels, 0, parents, rows=coarse_rows, row_block=leaf_region // coarse_rows
+    )
     coarse_high = coarse_local.astype(jnp.bfloat16)
     coarse_low = (coarse_local - coarse_high.astype(jnp.float32)).astype(jnp.bfloat16)
     tile = boxes // chunks
@@ -193,7 +195,8 @@
         if chunk >= 2:
             slot_in, _ = lax.optimization_barrier((leaf_slot, mine[chunk - 2]))
         partial_sum = translate(
-            slot_in, buffer, kernels, chunk, tile, (coarse_high, coarse_low, transfer), devices
+            slot_in, rows_all, kernels, chunk, tile, (coarse_high, coarse_low, transfer), devices,
+            rows=leaf_rows,
         )
         total = lax.dynamic_slice_in_dim(partial_sum, me * block, block, 0)
         for shift in range(1, devices):

time: 121 us -> 118 us (0.975)
  local copies, waits for them, and re-layouts: 16.7 us -> 11.7 us
  Pallas kernels: 52 us -> 54.5 us
    gather x12 -> x6, local copies, waits for them, and re-layouts: 7.75 us -> 4.43 us  [on_device(): outgoing = rows_all[picks]]
    pallas_call x6, Pallas kernels: 46.8 us -> 49.3 us  [translate(): pl.pallas_call(functools.partial(translate_kernel, spread is not None, de...]
    unnamed x22 -> x18, local copies, waits for them, and re-layouts: 6.07 us -> 3.65 us
  transfers between devices with their start and end apart: 18 -> 18, of which waited for: 8 -> 8; matrix products, arithmetic and copies ran while one was open for 1% -> 2% of each run, Pallas kernels for 30% -> 30%
where the time goes in v3:
time: 118 us
  Pallas kernels  54.5 us (46%)
  starting transfers between devices  35.8 us (30%)
  waiting for transfers between devices  13.1 us (11%)
  local copies, waits for them, and re-layouts  11.7 us (10%)
  other arithmetic  2.08 us (2%)
    pallas_call x6, Pallas kernels, translate(): pl.pallas_call(functools.partial(translate_kernel, spread is not None, de...  49.3 us
    ppermute x12, starting transfers between devices, on_device(): total = total + lax.ppermute(sent, 'off', route)  18.7 us
    ppermute x6, starting transfers between devices, partner(): return lax.ppermute(block, axis, route)  17.1 us
    ppermute x6, waiting for transfers between devices, partner(): return lax.ppermute(block, axis, route)  9.31 us
    pallas_call x6, Pallas kernels, slot_table(): pl.pallas_call(invert_kernel, out_shape=jax.ShapeDtypeStruct((classes, pa...  5.2 us
    gather x6, local copies, waits for them, and re-layouts, on_device(): outgoing = rows_all[picks]  4.43 us
    ppermute x12, waiting for transfers between devices, on_device(): total = total + lax.ppermute(sent, 'off', route)  3.82 us
    unnamed x18, local copies, waits for them, and re-layouts  3.65 us
  transfers between devices with their start and end apart: 18, of which 8 were waited for; matrix products, arithmetic and copies ran while one was open for 2% of the time, Pallas kernels for 30%

profile of v3, /device:TPU:16, one launch (start us, length us, event | category | flops | bytes accessed | tf_op | source)
XLA Modules:
  0.0 117.8 jit_solution(7256578401644548287)
XLA Ops:
  0.0 0.8 slice_bitcast_fusion
  0.8 0.7 add_bitcast_fusion.2
  1.6 1.5 %copy.242.buf_ref = bf16[1024,488]{1,0:T(8,128)(2,1)S(1)} copy(bf16[1024,488]{0,1:T(8,128)(2,1)} %param.11) | data formatting | bytes 1998848 | tf_op args[0]
  3.5 2.1 %copy-done = bf16[8,488,488]{2,1,0:T(8,128)(2,1)S(1)} copy-done((bf16[8,488,488]{2,1,0:T(8,128)(2,1)S(1)}, bf16[8,488,488]{2,1,0:T(8,128)(2,1)}, u32[]{:S(2)}) %copy-start) | copy-done | bytes 3810328
  5.6 3.5 %shard_map.109 = f32[128,488]{1,0:T(8,128)S(1)} custom-call(s32[16,128]{1,0:T(8,128)S(1)} %fusion.18.slot_ref, bf16[1024,488]{1,0:T(8,128)(2,1)S(1)} %copy.242.buf_ref, bf16[8,488,488]{2,1,0:T(8,128)(2,1)S(1)} %copy-done), custom_call_target="tpu_custom_call" | custom-call | flops 1511129088 | bytes 4809728 | tf_op jit(solution)/shard_map/pallas_call | solution.py:104
  9.2 0.7 gather_fusion
  10.6 0.9 shard_map.110
  11.7 0.7 gather_fusion.1
  12.6 1.4 %collective-permute-start.1 = (bf16[80,488]{1,0:T(8,128)(2,1)S(1)}, bf16[80,488]{1,0:T(8,128)(2,1)S(1)}, u32[]{:S(2)}, u32[]{:S(2)}) collective-permute-start(bf16[80,488]{1,0:T(8,128)(2,1)S(1)} %gather_fusion.1), channel_id=1, source_target_pairs={{0,8},{8,0},{4,12},{12,4},{16,24},{24,16},{20,28},{28,20},{32,40},... | collective-permute-start | bytes 234248 | tf_op jit(solution)/shard_map/ppermute | solution.py:18
  14.0 0.9 shard_map.111
  14.9 2.6 %collective-permute-done.1 = bf16[80,488]{1,0:T(8,128)(2,1)S(1)} collective-permute-done((bf16[80,488]{1,0:T(8,128)(2,1)S(1)}, bf16[80,488]{1,0:T(8,128)(2,1)S(1)}, u32[]{:S(2)}, u32[]{:S(2)}) %collective-permute-start.1) | collective-permute-done | bytes 78112 | tf_op jit(solution)/shard_map/ppermute | solution.py:18
  17.5 0.7 gather_fusion.2
  18.4 2.2 %collective-permute-start.2 = (bf16[80,488]{1,0:T(8,128)(2,1)S(1)}, bf16[80,488]{1,0:T(8,128)(2,1)S(1)}, u32[]{:S(2)}, u32[]{:S(2)}) collective-permute-start(bf16[80,488]{1,0:T(8,128)(2,1)S(1)} %gather_fusion.2), channel_id=1, source_target_pairs={{0,16},{16,0},{4,20},{20,4},{8,24},{24,8},{12,28},{28,12},{32,48},... | collective-permute-start | bytes 234248 | tf_op jit(solution)/shard_map/ppermute | solution.py:18
  20.6 0.9 shard_map.112
  21.5 2.9 %collective-permute-done.2 = bf16[80,488]{1,0:T(8,128)(2,1)S(1)} collective-permute-done((bf16[80,488]{1,0:T(8,128)(2,1)S(1)}, bf16[80,488]{1,0:T(8,128)(2,1)S(1)}, u32[]{:S(2)}, u32[]{:S(2)}) %collective-permute-start.2) | collective-permute-done | bytes 78112 | tf_op jit(solution)/shard_map/ppermute | solution.py:18
  24.4 0.7 gather_fusion.3
  25.3 2.0 %collective-permute-start.3 = (bf16[80,488]{1,0:T(8,128)(2,1)S(1)}, bf16[80,488]{1,0:T(8,128)(2,1)S(1)}, u32[]{:S(2)}, u32[]{:S(2)}) collective-permute-start(bf16[80,488]{1,0:T(8,128)(2,1)S(1)} %gather_fusion.3), channel_id=1, source_target_pairs={{0,32},{32,0},{4,36},{36,4},{8,40},{40,8},{12,44},{44,12},{16,48},... | collective-permute-start | bytes 234248 | tf_op jit(solution)/shard_map/ppermute | solution.py:18
  27.4 0.9 shard_map.113
  28.3 1.5 %collective-permute-done.3 = bf16[80,488]{1,0:T(8,128)(2,1)S(1)} collective-permute-done((bf16[80,488]{1,0:T(8,128)(2,1)S(1)}, bf16[80,488]{1,0:T(8,128)(2,1)S(1)}, u32[]{:S(2)}, u32[]{:S(2)}) %collective-permute-start.3) | collective-permute-done | bytes 78112 | tf_op jit(solution)/shard_map/ppermute | solution.py:18
  29.9 0.7 gather_fusion.4
  30.8 3.4 %collective-permute-start.4 = (bf16[80,488]{1,0:T(8,128)(2,1)S(1)}, bf16[80,488]{1,0:T(8,128)(2,1)S(1)}, u32[]{:S(2)}, u32[]{:S(2)}) collective-permute-start(bf16[80,488]{1,0:T(8,128)(2,1)S(1)} %gather_fusion.4), channel_id=1, source_target_pairs={{0,64},{64,0},{4,68},{68,4},{8,72},{72,8},{12,76},{76,12},{16,80},... | collective-permute-start | bytes 234248 | tf_op jit(solution)/shard_map/ppermute | solution.py:18
  34.2 0.9 shard_map.114
  35.1 1.5 %collective-permute-done.4 = bf16[80,488]{1,0:T(8,128)(2,1)S(1)} collective-permute-done((bf16[80,488]{1,0:T(8,128)(2,1)S(1)}, bf16[80,488]{1,0:T(8,128)(2,1)S(1)}, u32[]{:S(2)}, u32[]{:S(2)}) %collective-permute-start.4) | collective-permute-done | bytes 78112 | tf_op jit(solution)/shard_map/ppermute | solution.py:18
  36.6 0.7 gather_fusion.5
  37.3 8.0 %collective-permute-start.5 = (bf16[80,488]{1,0:T(8,128)(2,1)S(1)}, bf16[80,488]{1,0:T(8,128)(2,1)S(1)}, u32[]{:S(2)}, u32[]{:S(2)}) collective-permute-start(bf16[80,488]{1,0:T(8,128)(2,1)S(1)} %gather_fusion.5), channel_id=1, source_target_pairs={{0,128},{128,0},{4,132},{132,4},{8,136},{136,8},{12,140},{140,12},... | collective-permute-start | bytes 234248 | tf_op jit(solution)/shard_map/ppermute | solution.py:18
  45.3 0.5 shard_map.115
  45.9 0.2 copy.261
  46.2 0.5 copy.262
  46.9 0.9 collective-permute-done.5
  47.7 5.2 %shard_map.116 = f32[128,488]{1,0:T(8,128)S(1)} custom-call(s32[16,128]{1,0:T(8,128)S(1)} %pad.61.slot_ref, bf16[1792,488]{1,0:T(8,128)(2,1)S(1)} %slice_dynamic-update-slice_fusion.6.buf_ref, bf16[10,488,488]{2,1,0:T(8,128)(2,1)} %k_ref.11), custom_call_target="tpu_custom_call" | custom-call | flops 889487360 | bytes 6511872 | tf_op jit(solution)/shard_map/pallas_call | solution.py:104
  53.0 10.1 %shard_map.117 = f32[256,488]{1,0:T(8,128)S(1)} custom-call(s32[16,1024]{1,0:T(8,128)S(1)} %pad.58.slot_ref, bf16[1792,488]{1,0:T(8,128)(2,1)S(1)} %slice_dynamic-update-slice_fusion.6.buf_ref, bf16[10,488,488]{2,1,0:T(8,128)(2,1)} %k_ref.11, bf16[128,488]{1,0:T(8,128)(2,1)S(1)} %get-tuple-element.84.rest_0_, ...), custom_call_target="tpu_custom_call" | custom-call | flops 4737269760 | bytes 6511872 | tf_op jit(solution)/shard_map/pallas_call | solution.py:104
  63.2 1.6 %collective-permute-start.6 = (f32[64,488]{1,0:T(8,128)S(1)}, f32[64,488]{1,0:T(8,128)S(1)}, u32[]{:S(2)}, u32[]{:S(2)}) collective-permute-start(f32[64,488]{1,0:T(8,128)S(1)} %get-tuple-element.74), channel_id=1, source_target_pairs={{0,1},{1,2},{2,3},{3,0},{4,5},{5,6},{6,7},{7,4},{8,9},{9,10},{10,1... | collective-permute-start | bytes 374792 | tf_op jit(solution)/shard_map/ppermute | solution.py:206
  64.8 2.7 %collective-permute-start.7 = (f32[64,488]{1,0:T(8,128)S(1)}, f32[64,488]{1,0:T(8,128)S(1)}, u32[]{:S(2)}, u32[]{:S(2)}) collective-permute-start(f32[64,488]{1,0:T(8,128)S(1)} %get-tuple-element.76), channel_id=1, source_target_pairs={{0,2},{1,3},{2,0},{3,1},{4,6},{5,7},{6,4},{7,5},{8,10},{9,11},{10,... | collective-permute-start | bytes 374792 | tf_op jit(solution)/shard_map/ppermute | solution.py:206
  67.5 1.4 %collective-permute-start.8 = (f32[64,488]{1,0:T(8,128)S(1)}, f32[64,488]{1,0:T(8,128)S(1)}, u32[]{:S(2)}, u32[]{:S(2)}) collective-permute-start(f32[64,488]{1,0:T(8,128)S(1)} %get-tuple-element.75), channel_id=1, source_target_pairs={{0,3},{1,0},{2,1},{3,2},{4,7},{5,4},{6,5},{7,6},{8,11},{9,8},{10,9... | collective-permute-start | bytes 374792 | tf_op jit(solution)/shard_map/ppermute | solution.py:206
  68.9 10.1 %shard_map.118 = f32[256,488]{1,0:T(8,128)S(1)} custom-call(s32[16,1024]{1,0:T(8,128)S(1)} %pad.58.slot_ref, bf16[1792,488]{1,0:T(8,128)(2,1)S(1)} %slice_dynamic-update-slice_fusion.6.buf_ref, bf16[10,488,488]{2,1,0:T(8,128)(2,1)} %k_ref.11, bf16[128,488]{1,0:T(8,128)(2,1)S(1)} %get-tuple-element.84.rest_0_, ...), custom_call_target="tpu_custom_call" | custom-call | flops 4737269760 | bytes 6511872 | tf_op jit(solution)/shard_map/pallas_call | solution.py:104
  79.1 0.6 collective-permute-start.10
  79.7 2.7 %collective-permute-start.11 = (f32[64,488]{1,0:T(8,128)S(1)}, f32[64,488]{1,0:T(8,128)S(1)}, u32[]{:S(2)}, u32[]{:S(2)}) collective-permute-start(f32[64,488]{1,0:T(8,128)S(1)} %get-tuple-element.81), channel_id=1, source_target_pairs={{0,3},{1,0},{2,1},{3,2},{4,7},{5,4},{6,5},{7,6},{8,11},{9,8},{10,9... | collective-permute-start | bytes 374792 | tf_op jit(solution)/shard_map/ppermute | solution.py:206
  82.5 10.1 %shard_map.119 = f32[256,488]{1,0:T(8,128)S(1)} custom-call(s32[16,1024]{1,0:T(8,128)S(1)} %pad.58.slot_ref, bf16[1792,488]{1,0:T(8,128)(2,1)S(1)} %slice_dynamic-update-slice_fusion.6.buf_ref, bf16[10,488,488]{2,1,0:T(8,128)(2,1)} %k_ref.11, bf16[128,488]{1,0:T(8,128)(2,1)S(1)} %get-tuple-element.84.rest_0_, ...), custom_call_target="tpu_custom_call" | custom-call | flops 4737269760 | bytes 6511872 | tf_op jit(solution)/shard_map/pallas_call | solution.py:104
  92.7 0.3 collective-permute-start.12
  93.0 4.5 %collective-permute-start.13 = (f32[64,488]{1,0:T(8,128)S(1)}, f32[64,488]{1,0:T(8,128)S(1)}, u32[]{:S(2)}, u32[]{:S(2)}) collective-permute-start(f32[64,488]{1,0:T(8,128)S(1)} %get-tuple-element.73), channel_id=1, source_target_pairs={{0,2},{1,3},{2,0},{3,1},{4,6},{5,7},{6,4},{7,5},{8,10},{9,11},{10,... | collective-permute-start | bytes 374792 | tf_op jit(solution)/shard_map/ppermute | solution.py:206
  97.5 0.2 collective-permute-start.14
  97.7 10.1 %shard_map.120 = f32[256,488]{1,0:T(8,128)S(1)} custom-call(s32[16,1024]{1,0:T(8,128)S(1)} %pad.58.slot_ref, bf16[1792,488]{1,0:T(8,128)(2,1)S(1)} %slice_dynamic-update-slice_fusion.6.buf_ref, bf16[10,488,488]{2,1,0:T(8,128)(2,1)} %k_ref.11, bf16[128,488]{1,0:T(8,128)(2,1)S(1)} %get-tuple-element.84.rest_0_, ...), custom_call_target="tpu_custom_call" | custom-call | flops 4737269760 | bytes 6511872 | tf_op jit(solution)/shard_map/pallas_call | solution.py:104
  107.9 1.9 %collective-permute-start.15 = (f32[64,488]{1,0:T(8,128)S(1)}, f32[64,488]{1,0:T(8,128)S(1)}, u32[]{:S(2)}, u32[]{:S(2)}) collective-permute-start(f32[64,488]{1,0:T(8,128)S(1)} %get-tuple-element.77), channel_id=1, source_target_pairs={{0,1},{1,2},{2,3},{3,0},{4,5},{5,6},{6,7},{7,4},{8,9},{9,10},{10,1... | collective-permute-start | bytes 374792 | tf_op jit(solution)/shard_map/ppermute | solution.py:206
  109.8 2.8 %collective-permute-start.17 = (f32[64,488]{1,0:T(8,128)S(1)}, f32[64,488]{1,0:T(8,128)S(1)}, u32[]{:S(2)}, u32[]{:S(2)}) collective-permute-start(f32[64,488]{1,0:T(8,128)S(1)} %get-tuple-element.78), channel_id=1, source_target_pairs={{0,3},{1,0},{2,1},{3,2},{4,7},{5,4},{6,5},{7,6},{8,11},{9,8},{10,9... | collective-permute-start | bytes 374792 | tf_op jit(solution)/shard_map/ppermute | solution.py:206
  112.6 1.5 %collective-permute-done.15 = f32[64,488]{1,0:T(8,128)S(1)} collective-permute-done((f32[64,488]{1,0:T(8,128)S(1)}, f32[64,488]{1,0:T(8,128)S(1)}, u32[]{:S(2)}, u32[]{:S(2)}) %collective-permute-start.15) | collective-permute-done | bytes 124960 | tf_op jit(solution)/shard_map/ppermute | solution.py:206
  114.2 2.1 %collective-permute-done.16 = f32[64,488]{1,0:T(8,128)S(1)} collective-permute-done((f32[64,488]{1,0:T(8,128)S(1)}, f32[64,488]{1,0:T(8,128)S(1)}, u32[]{:S(2)}, u32[]{:S(2)}) %collective-permute-start.16) | collective-permute-done | bytes 124960 | tf_op jit(solution)/shard_map/ppermute | solution.py:206
  116.5 0.3 copy.288
  116.8 1.0 copy.264
  (105 shorter events, 2.6 us)
Async XLA Ops:
  0.0 3.1 %copy-start.1 = (s32[1,10,1024]{2,0,1:T(1,128)S(1)}, s32[1,10,1024]{2,0,1:T(1,128)}, u32[]{:S(2)}) copy-start(s32[1,10,1024]{2,0,1:T(1,128)} %param.15) | copy-start | bytes 122884
  0.0 3.2 %copy-start.2 = (s32[1,10,1024]{2,0,1:T(1,128)S(1)}, s32[1,10,1024]{2,0,1:T(1,128)}, u32[]{:S(2)}) copy-start(s32[1,10,1024]{2,0,1:T(1,128)} %param.14) | copy-start | bytes 122884
  0.0 3.2 %copy-start.3 = (s32[1,10]{1,0:T(1,128)S(1)}, s32[1,10]{1,0:T(1,128)}, u32[]{:S(2)}) copy-start(s32[1,10]{1,0:T(1,128)} %param.16) | copy-start | bytes 124
  3.5 2.1 %copy-start = (bf16[8,488,488]{2,1,0:T(8,128)(2,1)S(1)}, bf16[8,488,488]{2,1,0:T(8,128)(2,1)}, u32[]{:S(2)}) copy-start(bf16[8,488,488]{2,1,0:T(8,128)(2,1)} %rest_2_.7) | copy-start | bytes 11430916
  5.6 4.8 %copy-start.4 = (s32[1,10,128]{2,0,1:T(1,128)S(1)}, s32[1,10,128]{2,0,1:T(1,128)}, u32[]{:S(2)}) copy-start(s32[1,10,128]{2,0,1:T(1,128)} %param.18) | copy-start | bytes 15364
  5.6 4.8 %copy-start.6 = (s32[1,10]{1,0:T(1,128)S(1)}, s32[1,10]{1,0:T(1,128)}, u32[]{:S(2)}) copy-start(s32[1,10]{1,0:T(1,128)} %param.19) | copy-start | bytes 124
  5.6 4.9 %copy-start.5 = (s32[1,10,128]{2,0,1:T(1,128)S(1)}, s32[1,10,128]{2,0,1:T(1,128)}, u32[]{:S(2)}) copy-start(s32[1,10,128]{2,0,1:T(1,128)} %param.17) | copy-start | bytes 15364
  9.9 1.7 %collective-permute-start = (bf16[80,488]{1,0:T(8,128)(2,1)S(1)}, bf16[80,488]{1,0:T(8,128)(2,1)S(1)}, u32[]{:S(2)}, u32[]{:S(2)}) collective-permute-start(bf16[80,488]{1,0:T(8,128)(2,1)S(1)} %gather_fusion), channel_id=1, source_target_pairs={{0,4},{4,0},{8,12},{12,8},{16,20},{20,16},{24,28},{28,24},{32,36},... | collective-permute-start | bytes 234248 | tf_op jit(solution)/shard_map/ppermute | solution.py:18
  12.6 4.9 %collective-permute-start.1 = (bf16[80,488]{1,0:T(8,128)(2,1)S(1)}, bf16[80,488]{1,0:T(8,128)(2,1)S(1)}, u32[]{:S(2)}, u32[]{:S(2)}) collective-permute-start(bf16[80,488]{1,0:T(8,128)(2,1)S(1)} %gather_fusion.1), channel_id=1, source_target_pairs={{0,8},{8,0},{4,12},{12,4},{16,24},{24,16},{20,28},{28,20},{32,40},... | collective-permute-start | bytes 234248 | tf_op jit(solution)/shard_map/ppermute | solution.py:18
  18.4 6.0 %collective-permute-start.2 = (bf16[80,488]{1,0:T(8,128)(2,1)S(1)}, bf16[80,488]{1,0:T(8,128)(2,1)S(1)}, u32[]{:S(2)}, u32[]{:S(2)}) collective-permute-start(bf16[80,488]{1,0:T(8,128)(2,1)S(1)} %gather_fusion.2), channel_id=1, source_target_pairs={{0,16},{16,0},{4,20},{20,4},{8,24},{24,8},{12,28},{28,12},{32,48},... | collective-permute-start | bytes 234248 | tf_op jit(solution)/shard_map/ppermute | solution.py:18
  25.3 4.5 %collective-permute-start.3 = (bf16[80,488]{1,0:T(8,128)(2,1)S(1)}, bf16[80,488]{1,0:T(8,128)(2,1)S(1)}, u32[]{:S(2)}, u32[]{:S(2)}) collective-permute-start(bf16[80,488]{1,0:T(8,128)(2,1)S(1)} %gather_fusion.3), channel_id=1, source_target_pairs={{0,32},{32,0},{4,36},{36,4},{8,40},{40,8},{12,44},{44,12},{16,48},... | collective-permute-start | bytes 234248 | tf_op jit(solution)/shard_map/ppermute | solution.py:18
  30.8 5.8 %collective-permute-start.4 = (bf16[80,488]{1,0:T(8,128)(2,1)S(1)}, bf16[80,488]{1,0:T(8,128)(2,1)S(1)}, u32[]{:S(2)}, u32[]{:S(2)}) collective-permute-start(bf16[80,488]{1,0:T(8,128)(2,1)S(1)} %gather_fusion.4), channel_id=1, source_target_pairs={{0,64},{64,0},{4,68},{68,4},{8,72},{72,8},{12,76},{76,12},{16,80},... | collective-permute-start | bytes 234248 | tf_op jit(solution)/shard_map/ppermute | solution.py:18
  37.3 10.4 %collective-permute-start.5 = (bf16[80,488]{1,0:T(8,128)(2,1)S(1)}, bf16[80,488]{1,0:T(8,128)(2,1)S(1)}, u32[]{:S(2)}, u32[]{:S(2)}) collective-permute-start(bf16[80,488]{1,0:T(8,128)(2,1)S(1)} %gather_fusion.5), channel_id=1, source_target_pairs={{0,128},{128,0},{4,132},{132,4},{8,136},{136,8},{12,140},{140,12},... | collective-permute-start | bytes 234248 | tf_op jit(solution)/shard_map/ppermute | solution.py:18
  63.2 19.2 %collective-permute-start.6 = (f32[64,488]{1,0:T(8,128)S(1)}, f32[64,488]{1,0:T(8,128)S(1)}, u32[]{:S(2)}, u32[]{:S(2)}) collective-permute-start(f32[64,488]{1,0:T(8,128)S(1)} %get-tuple-element.74), channel_id=1, source_target_pairs={{0,1},{1,2},{2,3},{3,0},{4,5},{5,6},{6,7},{7,4},{8,9},{9,10},{10,1... | collective-permute-start | bytes 374792 | tf_op jit(solution)/shard_map/ppermute | solution.py:206
  64.8 17.7 %collective-permute-start.7 = (f32[64,488]{1,0:T(8,128)S(1)}, f32[64,488]{1,0:T(8,128)S(1)}, u32[]{:S(2)}, u32[]{:S(2)}) collective-permute-start(f32[64,488]{1,0:T(8,128)S(1)} %get-tuple-element.76), channel_id=1, source_target_pairs={{0,2},{1,3},{2,0},{3,1},{4,6},{5,7},{6,4},{7,5},{8,10},{9,11},{10,... | collective-permute-start | bytes 374792 | tf_op jit(solution)/shard_map/ppermute | solution.py:206
  67.5 15.0 %collective-permute-start.8 = (f32[64,488]{1,0:T(8,128)S(1)}, f32[64,488]{1,0:T(8,128)S(1)}, u32[]{:S(2)}, u32[]{:S(2)}) collective-permute-start(f32[64,488]{1,0:T(8,128)S(1)} %get-tuple-element.75), channel_id=1, source_target_pairs={{0,3},{1,0},{2,1},{3,2},{4,7},{5,4},{6,5},{7,6},{8,11},{9,8},{10,9... | collective-permute-start | bytes 374792 | tf_op jit(solution)/shard_map/ppermute | solution.py:206
  79.1 18.4 %collective-permute-start.10 = (f32[64,488]{1,0:T(8,128)S(1)}, f32[64,488]{1,0:T(8,128)S(1)}, u32[]{:S(2)}, u32[]{:S(2)}) collective-permute-start(f32[64,488]{1,0:T(8,128)S(1)} %get-tuple-element.82), channel_id=1, source_target_pairs={{0,2},{1,3},{2,0},{3,1},{4,6},{5,7},{6,4},{7,5},{8,10},{9,11},{10,... | collective-permute-start | bytes 374792 | tf_op jit(solution)/shard_map/ppermute | solution.py:206
  79.7 18.0 %collective-permute-start.11 = (f32[64,488]{1,0:T(8,128)S(1)}, f32[64,488]{1,0:T(8,128)S(1)}, u32[]{:S(2)}, u32[]{:S(2)}) collective-permute-start(f32[64,488]{1,0:T(8,128)S(1)} %get-tuple-element.81), channel_id=1, source_target_pairs={{0,3},{1,0},{2,1},{3,2},{4,7},{5,4},{6,5},{7,6},{8,11},{9,8},{10,9... | collective-permute-start | bytes 374792 | tf_op jit(solution)/shard_map/ppermute | solution.py:206
  82.4 15.2 %collective-permute-start.9 = (f32[64,488]{1,0:T(8,128)S(1)}, f32[64,488]{1,0:T(8,128)S(1)}, u32[]{:S(2)}, u32[]{:S(2)}) collective-permute-start(f32[64,488]{1,0:T(8,128)S(1)} %get-tuple-element.80), channel_id=1, source_target_pairs={{0,1},{1,2},{2,3},{3,0},{4,5},{5,6},{6,7},{7,4},{8,9},{9,10},{10,1... | collective-permute-start | bytes 374792 | tf_op jit(solution)/shard_map/ppermute | solution.py:206
  92.7 17.1 %collective-permute-start.12 = (f32[64,488]{1,0:T(8,128)S(1)}, f32[64,488]{1,0:T(8,128)S(1)}, u32[]{:S(2)}, u32[]{:S(2)}) collective-permute-start(f32[64,488]{1,0:T(8,128)S(1)} %get-tuple-element.71), channel_id=1, source_target_pairs={{0,1},{1,2},{2,3},{3,0},{4,5},{5,6},{6,7},{7,4},{8,9},{9,10},{10,1... | collective-permute-start | bytes 374792 | tf_op jit(solution)/shard_map/ppermute | solution.py:206
  93.0 19.6 %collective-permute-start.13 = (f32[64,488]{1,0:T(8,128)S(1)}, f32[64,488]{1,0:T(8,128)S(1)}, u32[]{:S(2)}, u32[]{:S(2)}) collective-permute-start(f32[64,488]{1,0:T(8,128)S(1)} %get-tuple-element.73), channel_id=1, source_target_pairs={{0,2},{1,3},{2,0},{3,1},{4,6},{5,7},{6,4},{7,5},{8,10},{9,11},{10,... | collective-permute-start | bytes 374792 | tf_op jit(solution)/shard_map/ppermute | solution.py:206
  97.5 15.1 %collective-permute-start.14 = (f32[64,488]{1,0:T(8,128)S(1)}, f32[64,488]{1,0:T(8,128)S(1)}, u32[]{:S(2)}, u32[]{:S(2)}) collective-permute-start(f32[64,488]{1,0:T(8,128)S(1)} %get-tuple-element.72), channel_id=1, source_target_pairs={{0,3},{1,0},{2,1},{3,2},{4,7},{5,4},{6,5},{7,6},{8,11},{9,8},{10,9... | collective-permute-start | bytes 374792 | tf_op jit(solution)/shard_map/ppermute | solution.py:206
  107.9 6.3 %collective-permute-start.15 = (f32[64,488]{1,0:T(8,128)S(1)}, f32[64,488]{1,0:T(8,128)S(1)}, u32[]{:S(2)}, u32[]{:S(2)}) collective-permute-start(f32[64,488]{1,0:T(8,128)S(1)} %get-tuple-element.77), channel_id=1, source_target_pairs={{0,1},{1,2},{2,3},{3,0},{4,5},{5,6},{6,7},{7,4},{8,9},{9,10},{10,1... | collective-permute-start | bytes 374792 | tf_op jit(solution)/shard_map/ppermute | solution.py:206
  109.8 6.5 %collective-permute-start.16 = (f32[64,488]{1,0:T(8,128)S(1)}, f32[64,488]{1,0:T(8,128)S(1)}, u32[]{:S(2)}, u32[]{:S(2)}) collective-permute-start(f32[64,488]{1,0:T(8,128)S(1)} %get-tuple-element.79), channel_id=1, source_target_pairs={{0,2},{1,3},{2,0},{3,1},{4,6},{5,7},{6,4},{7,5},{8,10},{9,11},{10,... | collective-permute-start | bytes 374792 | tf_op jit(solution)/shard_map/ppermute | solution.py:206
  109.8 6.6 %collective-permute-start.17 = (f32[64,488]{1,0:T(8,128)S(1)}, f32[64,488]{1,0:T(8,128)S(1)}, u32[]{:S(2)}, u32[]{:S(2)}) collective-permute-start(f32[64,488]{1,0:T(8,128)S(1)} %get-tuple-element.78), channel_id=1, source_target_pairs={{0,3},{1,0},{2,1},{3,2},{4,7},{5,4},{6,5},{7,6},{8,11},{9,8},{10,9... | collective-permute-start | bytes 374792 | tf_op jit(solution)/shard_map/ppermute | solution.py:206

commit v4 on v3

--- a/solution.py
+++ b/solution.py
@@ -181,9 +181,7 @@
     leaf_slot = leaf_slot.reshape(classes, devices, span, chunks, per)
     leaf_slot = leaf_slot.transpose(0, 3, 1, 4, 2).reshape(classes, boxes)
     leaf_slot = jnp.pad(leaf_slot, ((0, 16 - classes), (0, 0)), constant_values=leaf_rows)
-    coarse_local = 0.5 * translate(
-        coarse_slot, rows_all, kernels, 0, parents, rows=coarse_rows, row_block=leaf_region // coarse_rows
-    )
+    coarse_local = 0.5 * translate(coarse_slot, rows_all[leaf_region:], kernels, 0, parents)
     coarse_high = coarse_local.astype(jnp.bfloat16)
     coarse_low = (coarse_local - coarse_high.astype(jnp.float32)).astype(jnp.bfloat16)
     tile = boxes // chunks

time: 118 us -> 118 us (level)
  Pallas kernels: 54.5 us -> 52 us
  local copies, waits for them, and re-layouts: 11.7 us -> 14.2 us
    pallas_call x6, Pallas kernels: 49.3 us -> 46.8 us  [translate(): pl.pallas_call(functools.partial(translate_kernel, spread is not None, de...]
    unnamed x18 -> x20, local copies, waits for them, and re-layouts: 3.65 us -> 6.06 us
where the time goes in v4:
time: 118 us
  Pallas kernels  52 us (44%)
  starting transfers between devices  35.8 us (30%)
  local copies, waits for them, and re-layouts  14.2 us (12%)
  waiting for transfers between devices  13.1 us (11%)
  other arithmetic  2.08 us (2%)
    pallas_call x6, Pallas kernels, translate(): pl.pallas_call(functools.partial(translate_kernel, spread is not None, de...  46.8 us
    ppermute x12, starting transfers between devices, on_device(): total = total + lax.ppermute(sent, 'off', route)  18.7 us
    ppermute x6, starting transfers between devices, partner(): return lax.ppermute(block, axis, route)  17.1 us
    ppermute x6, waiting for transfers between devices, partner(): return lax.ppermute(block, axis, route)  9.31 us
    unnamed x20, local copies, waits for them, and re-layouts  6.06 us
    pallas_call x6, Pallas kernels, slot_table(): pl.pallas_call(invert_kernel, out_shape=jax.ShapeDtypeStruct((classes, pa...  5.2 us
    gather x6, local copies, waits for them, and re-layouts, on_device(): outgoing = rows_all[picks]  4.43 us
    ppermute x12, waiting for transfers between devices, on_device(): total = total + lax.ppermute(sent, 'off', route)  3.84 us
  transfers between devices with their start and end apart: 18, of which 8 were waited for; matrix products, arithmetic and copies ran while one was open for 2% of the time, Pallas kernels for 30%

profile of v4, /device:TPU:16, one launch (start us, length us, event | category | flops | bytes accessed | tf_op | source)
XLA Modules:
  0.0 117.8 jit_solution(16591046237772636557)
XLA Ops:
  0.0 0.8 slice_bitcast_fusion
  0.8 0.7 add_bitcast_fusion.2
  1.6 1.5 %copy.242.buf_ref = bf16[1024,488]{1,0:T(8,128)(2,1)S(1)} copy(bf16[1024,488]{0,1:T(8,128)(2,1)} %param.11) | data formatting | bytes 1998848 | tf_op args[0]
  3.5 2.1 %copy-done.1 = bf16[8,488,488]{2,1,0:T(8,128)(2,1)S(1)} copy-done((bf16[8,488,488]{2,1,0:T(8,128)(2,1)S(1)}, bf16[8,488,488]{2,1,0:T(8,128)(2,1)}, u32[]{:S(2)}) %copy-start.1) | copy-done | bytes 3810328
  5.6 3.5 %shard_map.109 = f32[128,488]{1,0:T(8,128)S(1)} custom-call(s32[16,128]{1,0:T(8,128)S(1)} %fusion.18.slot_ref, bf16[1024,488]{1,0:T(8,128)(2,1)S(1)} %copy.242.buf_ref, bf16[8,488,488]{2,1,0:T(8,128)(2,1)S(1)} %copy-done.1), custom_call_target="tpu_custom_call" | custom-call | flops 1511129088 | bytes 4809728 | tf_op jit(solution)/shard_map/pallas_call | solution.py:104
  9.2 0.7 gather_fusion
  10.6 0.9 shard_map.110
  11.7 0.7 gather_fusion.1
  12.6 1.4 %collective-permute-start.1 = (bf16[80,488]{1,0:T(8,128)(2,1)S(1)}, bf16[80,488]{1,0:T(8,128)(2,1)S(1)}, u32[]{:S(2)}, u32[]{:S(2)}) collective-permute-start(bf16[80,488]{1,0:T(8,128)(2,1)S(1)} %gather_fusion.1), channel_id=1, source_target_pairs={{0,8},{8,0},{4,12},{12,4},{16,24},{24,16},{20,28},{28,20},{32,40},... | collective-permute-start | bytes 234248 | tf_op jit(solution)/shard_map/ppermute | solution.py:18
  14.0 0.9 shard_map.111
  14.9 2.6 %collective-permute-done.1 = bf16[80,488]{1,0:T(8,128)(2,1)S(1)} collective-permute-done((bf16[80,488]{1,0:T(8,128)(2,1)S(1)}, bf16[80,488]{1,0:T(8,128)(2,1)S(1)}, u32[]{:S(2)}, u32[]{:S(2)}) %collective-permute-start.1) | collective-permute-done | bytes 78112 | tf_op jit(solution)/shard_map/ppermute | solution.py:18
  17.5 0.7 gather_fusion.2
  18.4 2.2 %collective-permute-start.2 = (bf16[80,488]{1,0:T(8,128)(2,1)S(1)}, bf16[80,488]{1,0:T(8,128)(2,1)S(1)}, u32[]{:S(2)}, u32[]{:S(2)}) collective-permute-start(bf16[80,488]{1,0:T(8,128)(2,1)S(1)} %gather_fusion.2), channel_id=1, source_target_pairs={{0,16},{16,0},{4,20},{20,4},{8,24},{24,8},{12,28},{28,12},{32,48},... | collective-permute-start | bytes 234248 | tf_op jit(solution)/shard_map/ppermute | solution.py:18
  20.6 0.9 shard_map.112
  21.5 2.9 %collective-permute-done.2 = bf16[80,488]{1,0:T(8,128)(2,1)S(1)} collective-permute-done((bf16[80,488]{1,0:T(8,128)(2,1)S(1)}, bf16[80,488]{1,0:T(8,128)(2,1)S(1)}, u32[]{:S(2)}, u32[]{:S(2)}) %collective-permute-start.2) | collective-permute-done | bytes 78112 | tf_op jit(solution)/shard_map/ppermute | solution.py:18
  24.4 0.7 gather_fusion.3
  25.3 2.0 %collective-permute-start.3 = (bf16[80,488]{1,0:T(8,128)(2,1)S(1)}, bf16[80,488]{1,0:T(8,128)(2,1)S(1)}, u32[]{:S(2)}, u32[]{:S(2)}) collective-permute-start(bf16[80,488]{1,0:T(8,128)(2,1)S(1)} %gather_fusion.3), channel_id=1, source_target_pairs={{0,32},{32,0},{4,36},{36,4},{8,40},{40,8},{12,44},{44,12},{16,48},... | collective-permute-start | bytes 234248 | tf_op jit(solution)/shard_map/ppermute | solution.py:18
  27.4 0.9 shard_map.113
  28.3 1.5 %collective-permute-done.3 = bf16[80,488]{1,0:T(8,128)(2,1)S(1)} collective-permute-done((bf16[80,488]{1,0:T(8,128)(2,1)S(1)}, bf16[80,488]{1,0:T(8,128)(2,1)S(1)}, u32[]{:S(2)}, u32[]{:S(2)}) %collective-permute-start.3) | collective-permute-done | bytes 78112 | tf_op jit(solution)/shard_map/ppermute | solution.py:18
  29.9 0.7 gather_fusion.4
  30.8 3.4 %collective-permute-start.4 = (bf16[80,488]{1,0:T(8,128)(2,1)S(1)}, bf16[80,488]{1,0:T(8,128)(2,1)S(1)}, u32[]{:S(2)}, u32[]{:S(2)}) collective-permute-start(bf16[80,488]{1,0:T(8,128)(2,1)S(1)} %gather_fusion.4), channel_id=1, source_target_pairs={{0,64},{64,0},{4,68},{68,4},{8,72},{72,8},{12,76},{76,12},{16,80},... | collective-permute-start | bytes 234248 | tf_op jit(solution)/shard_map/ppermute | solution.py:18
  34.2 0.9 shard_map.114
  35.1 1.5 %collective-permute-done.4 = bf16[80,488]{1,0:T(8,128)(2,1)S(1)} collective-permute-done((bf16[80,488]{1,0:T(8,128)(2,1)S(1)}, bf16[80,488]{1,0:T(8,128)(2,1)S(1)}, u32[]{:S(2)}, u32[]{:S(2)}) %collective-permute-start.4) | collective-permute-done | bytes 78112 | tf_op jit(solution)/shard_map/ppermute | solution.py:18
  36.6 0.7 gather_fusion.5
  37.3 8.0 %collective-permute-start.5 = (bf16[80,488]{1,0:T(8,128)(2,1)S(1)}, bf16[80,488]{1,0:T(8,128)(2,1)S(1)}, u32[]{:S(2)}, u32[]{:S(2)}) collective-permute-start(bf16[80,488]{1,0:T(8,128)(2,1)S(1)} %gather_fusion.5), channel_id=1, source_target_pairs={{0,128},{128,0},{4,132},{132,4},{8,136},{136,8},{12,140},{140,12},... | collective-permute-start | bytes 234248 | tf_op jit(solution)/shard_map/ppermute | solution.py:18
  45.3 0.5 shard_map.115
  46.2 0.5 copy.262
  46.9 0.9 collective-permute-done.5
  47.8 2.4 %copy-done = bf16[10,488,488]{2,1,0:T(8,128)(2,1)S(1)} copy-done((bf16[10,488,488]{2,1,0:T(8,128)(2,1)S(1)}, bf16[10,488,488]{2,1,0:T(8,128)(2,1)}, u32[]{:S(2)}) %copy-start) | copy-done | bytes 4762904
  50.2 2.8 %shard_map.116 = f32[128,488]{1,0:T(8,128)S(1)} custom-call(s32[16,128]{1,0:T(8,128)S(1)} %pad.61.slot_ref, bf16[224,488]{1,0:T(8,128)(2,1)S(1)} %slice.174.buf_ref, bf16[10,488,488]{2,1,0:T(8,128)(2,1)S(1)} %copy-done), custom_call_target="tpu_custom_call" | custom-call | flops 889487360 | bytes 4981504 | tf_op jit(solution)/shard_map/pallas_call | solution.py:104
  53.0 10.1 %shard_map.117 = f32[256,488]{1,0:T(8,128)S(1)} custom-call(s32[16,1024]{1,0:T(8,128)S(1)} %pad.58.slot_ref, bf16[1792,488]{1,0:T(8,128)(2,1)S(1)} %slice_dynamic-update-slice_fusion.6.buf_ref, bf16[10,488,488]{2,1,0:T(8,128)(2,1)} %k_ref.11, bf16[128,488]{1,0:T(8,128)(2,1)S(1)} %get-tuple-element.84.rest_0_, ...), custom_call_target="tpu_custom_call" | custom-call | flops 4737269760 | bytes 6511872 | tf_op jit(solution)/shard_map/pallas_call | solution.py:104
  63.2 1.6 %collective-permute-start.6 = (f32[64,488]{1,0:T(8,128)S(1)}, f32[64,488]{1,0:T(8,128)S(1)}, u32[]{:S(2)}, u32[]{:S(2)}) collective-permute-start(f32[64,488]{1,0:T(8,128)S(1)} %get-tuple-element.74), channel_id=1, source_target_pairs={{0,1},{1,2},{2,3},{3,0},{4,5},{5,6},{6,7},{7,4},{8,9},{9,10},{10,1... | collective-permute-start | bytes 374792 | tf_op jit(solution)/shard_map/ppermute | solution.py:204
  64.8 2.7 %collective-permute-start.7 = (f32[64,488]{1,0:T(8,128)S(1)}, f32[64,488]{1,0:T(8,128)S(1)}, u32[]{:S(2)}, u32[]{:S(2)}) collective-permute-start(f32[64,488]{1,0:T(8,128)S(1)} %get-tuple-element.76), channel_id=1, source_target_pairs={{0,2},{1,3},{2,0},{3,1},{4,6},{5,7},{6,4},{7,5},{8,10},{9,11},{10,... | collective-permute-start | bytes 374792 | tf_op jit(solution)/shard_map/ppermute | solution.py:204
  67.5 1.4 %collective-permute-start.8 = (f32[64,488]{1,0:T(8,128)S(1)}, f32[64,488]{1,0:T(8,128)S(1)}, u32[]{:S(2)}, u32[]{:S(2)}) collective-permute-start(f32[64,488]{1,0:T(8,128)S(1)} %get-tuple-element.75), channel_id=1, source_target_pairs={{0,3},{1,0},{2,1},{3,2},{4,7},{5,4},{6,5},{7,6},{8,11},{9,8},{10,9... | collective-permute-start | bytes 374792 | tf_op jit(solution)/shard_map/ppermute | solution.py:204
  68.9 10.1 %shard_map.118 = f32[256,488]{1,0:T(8,128)S(1)} custom-call(s32[16,1024]{1,0:T(8,128)S(1)} %pad.58.slot_ref, bf16[1792,488]{1,0:T(8,128)(2,1)S(1)} %slice_dynamic-update-slice_fusion.6.buf_ref, bf16[10,488,488]{2,1,0:T(8,128)(2,1)} %k_ref.11, bf16[128,488]{1,0:T(8,128)(2,1)S(1)} %get-tuple-element.84.rest_0_, ...), custom_call_target="tpu_custom_call" | custom-call | flops 4737269760 | bytes 6511872 | tf_op jit(solution)/shard_map/pallas_call | solution.py:104
  79.1 0.6 collective-permute-start.10
  79.7 2.7 %collective-permute-start.11 = (f32[64,488]{1,0:T(8,128)S(1)}, f32[64,488]{1,0:T(8,128)S(1)}, u32[]{:S(2)}, u32[]{:S(2)}) collective-permute-start(f32[64,488]{1,0:T(8,128)S(1)} %get-tuple-element.81), channel_id=1, source_target_pairs={{0,3},{1,0},{2,1},{3,2},{4,7},{5,4},{6,5},{7,6},{8,11},{9,8},{10,9... | collective-permute-start | bytes 374792 | tf_op jit(solution)/shard_map/ppermute | solution.py:204
  82.5 10.1 %shard_map.119 = f32[256,488]{1,0:T(8,128)S(1)} custom-call(s32[16,1024]{1,0:T(8,128)S(1)} %pad.58.slot_ref, bf16[1792,488]{1,0:T(8,128)(2,1)S(1)} %slice_dynamic-update-slice_fusion.6.buf_ref, bf16[10,488,488]{2,1,0:T(8,128)(2,1)} %k_ref.11, bf16[128,488]{1,0:T(8,128)(2,1)S(1)} %get-tuple-element.84.rest_0_, ...), custom_call_target="tpu_custom_call" | custom-call | flops 4737269760 | bytes 6511872 | tf_op jit(solution)/shard_map/pallas_call | solution.py:104
  92.7 0.3 collective-permute-start.12
  93.0 4.5 %collective-permute-start.13 = (f32[64,488]{1,0:T(8,128)S(1)}, f32[64,488]{1,0:T(8,128)S(1)}, u32[]{:S(2)}, u32[]{:S(2)}) collective-permute-start(f32[64,488]{1,0:T(8,128)S(1)} %get-tuple-element.73), channel_id=1, source_target_pairs={{0,2},{1,3},{2,0},{3,1},{4,6},{5,7},{6,4},{7,5},{8,10},{9,11},{10,... | collective-permute-start | bytes 374792 | tf_op jit(solution)/shard_map/ppermute | solution.py:204
  97.5 0.2 collective-permute-start.14
  97.7 10.1 %shard_map.120 = f32[256,488]{1,0:T(8,128)S(1)} custom-call(s32[16,1024]{1,0:T(8,128)S(1)} %pad.58.slot_ref, bf16[1792,488]{1,0:T(8,128)(2,1)S(1)} %slice_dynamic-update-slice_fusion.6.buf_ref, bf16[10,488,488]{2,1,0:T(8,128)(2,1)} %k_ref.11, bf16[128,488]{1,0:T(8,128)(2,1)S(1)} %get-tuple-element.84.rest_0_, ...), custom_call_target="tpu_custom_call" | custom-call | flops 4737269760 | bytes 6511872 | tf_op jit(solution)/shard_map/pallas_call | solution.py:104
  107.9 1.9 %collective-permute-start.15 = (f32[64,488]{1,0:T(8,128)S(1)}, f32[64,488]{1,0:T(8,128)S(1)}, u32[]{:S(2)}, u32[]{:S(2)}) collective-permute-start(f32[64,488]{1,0:T(8,128)S(1)} %get-tuple-element.77), channel_id=1, source_target_pairs={{0,1},{1,2},{2,3},{3,0},{4,5},{5,6},{6,7},{7,4},{8,9},{9,10},{10,1... | collective-permute-start | bytes 374792 | tf_op jit(solution)/shard_map/ppermute | solution.py:204
  109.8 2.8 %collective-permute-start.17 = (f32[64,488]{1,0:T(8,128)S(1)}, f32[64,488]{1,0:T(8,128)S(1)}, u32[]{:S(2)}, u32[]{:S(2)}) collective-permute-start(f32[64,488]{1,0:T(8,128)S(1)} %get-tuple-element.78), channel_id=1, source_target_pairs={{0,3},{1,0},{2,1},{3,2},{4,7},{5,4},{6,5},{7,6},{8,11},{9,8},{10,9... | collective-permute-start | bytes 374792 | tf_op jit(solution)/shard_map/ppermute | solution.py:204
  112.6 1.6 %collective-permute-done.15 = f32[64,488]{1,0:T(8,128)S(1)} collective-permute-done((f32[64,488]{1,0:T(8,128)S(1)}, f32[64,488]{1,0:T(8,128)S(1)}, u32[]{:S(2)}, u32[]{:S(2)}) %collective-permute-start.15) | collective-permute-done | bytes 124960 | tf_op jit(solution)/shard_map/ppermute | solution.py:204
  114.2 2.1 %collective-permute-done.16 = f32[64,488]{1,0:T(8,128)S(1)} collective-permute-done((f32[64,488]{1,0:T(8,128)S(1)}, f32[64,488]{1,0:T(8,128)S(1)}, u32[]{:S(2)}, u32[]{:S(2)}) %collective-permute-start.16) | collective-permute-done | bytes 124960 | tf_op jit(solution)/shard_map/ppermute | solution.py:204
  116.5 0.3 copy.288
  116.8 1.0 copy.264
  (108 shorter events, 2.8 us)
Async XLA Ops:
  0.0 3.1 %copy-start.2 = (s32[1,10,1024]{2,0,1:T(1,128)S(1)}, s32[1,10,1024]{2,0,1:T(1,128)}, u32[]{:S(2)}) copy-start(s32[1,10,1024]{2,0,1:T(1,128)} %param.15) | copy-start | bytes 122884
  0.0 3.2 %copy-start.3 = (s32[1,10,1024]{2,0,1:T(1,128)S(1)}, s32[1,10,1024]{2,0,1:T(1,128)}, u32[]{:S(2)}) copy-start(s32[1,10,1024]{2,0,1:T(1,128)} %param.14) | copy-start | bytes 122884
  0.0 3.2 %copy-start.4 = (s32[1,10]{1,0:T(1,128)S(1)}, s32[1,10]{1,0:T(1,128)}, u32[]{:S(2)}) copy-start(s32[1,10]{1,0:T(1,128)} %param.16) | copy-start | bytes 124
  3.5 2.1 %copy-start.1 = (bf16[8,488,488]{2,1,0:T(8,128)(2,1)S(1)}, bf16[8,488,488]{2,1,0:T(8,128)(2,1)}, u32[]{:S(2)}) copy-start(bf16[8,488,488]{2,1,0:T(8,128)(2,1)} %rest_2_.7) | copy-start | bytes 11430916
  5.6 4.8 %copy-start.5 = (s32[1,10,128]{2,0,1:T(1,128)S(1)}, s32[1,10,128]{2,0,1:T(1,128)}, u32[]{:S(2)}) copy-start(s32[1,10,128]{2,0,1:T(1,128)} %param.18) | copy-start | bytes 15364
  5.6 4.8 %copy-start.7 = (s32[1,10]{1,0:T(1,128)S(1)}, s32[1,10]{1,0:T(1,128)}, u32[]{:S(2)}) copy-start(s32[1,10]{1,0:T(1,128)} %param.19) | copy-start | bytes 124
  5.6 4.9 %copy-start.6 = (s32[1,10,128]{2,0,1:T(1,128)S(1)}, s32[1,10,128]{2,0,1:T(1,128)}, u32[]{:S(2)}) copy-start(s32[1,10,128]{2,0,1:T(1,128)} %param.17) | copy-start | bytes 15364
  9.9 1.7 %collective-permute-start = (bf16[80,488]{1,0:T(8,128)(2,1)S(1)}, bf16[80,488]{1,0:T(8,128)(2,1)S(1)}, u32[]{:S(2)}, u32[]{:S(2)}) collective-permute-start(bf16[80,488]{1,0:T(8,128)(2,1)S(1)} %gather_fusion), channel_id=1, source_target_pairs={{0,4},{4,0},{8,12},{12,8},{16,20},{20,16},{24,28},{28,24},{32,36},... | collective-permute-start | bytes 234248 | tf_op jit(solution)/shard_map/ppermute | solution.py:18
  12.6 4.9 %collective-permute-start.1 = (bf16[80,488]{1,0:T(8,128)(2,1)S(1)}, bf16[80,488]{1,0:T(8,128)(2,1)S(1)}, u32[]{:S(2)}, u32[]{:S(2)}) collective-permute-start(bf16[80,488]{1,0:T(8,128)(2,1)S(1)} %gather_fusion.1), channel_id=1, source_target_pairs={{0,8},{8,0},{4,12},{12,4},{16,24},{24,16},{20,28},{28,20},{32,40},... | collective-permute-start | bytes 234248 | tf_op jit(solution)/shard_map/ppermute | solution.py:18
  18.4 6.0 %collective-permute-start.2 = (bf16[80,488]{1,0:T(8,128)(2,1)S(1)}, bf16[80,488]{1,0:T(8,128)(2,1)S(1)}, u32[]{:S(2)}, u32[]{:S(2)}) collective-permute-start(bf16[80,488]{1,0:T(8,128)(2,1)S(1)} %gather_fusion.2), channel_id=1, source_target_pairs={{0,16},{16,0},{4,20},{20,4},{8,24},{24,8},{12,28},{28,12},{32,48},... | collective-permute-start | bytes 234248 | tf_op jit(solution)/shard_map/ppermute | solution.py:18
  25.3 4.5 %collective-permute-start.3 = (bf16[80,488]{1,0:T(8,128)(2,1)S(1)}, bf16[80,488]{1,0:T(8,128)(2,1)S(1)}, u32[]{:S(2)}, u32[]{:S(2)}) collective-permute-start(bf16[80,488]{1,0:T(8,128)(2,1)S(1)} %gather_fusion.3), channel_id=1, source_target_pairs={{0,32},{32,0},{4,36},{36,4},{8,40},{40,8},{12,44},{44,12},{16,48},... | collective-permute-start | bytes 234248 | tf_op jit(solution)/shard_map/ppermute | solution.py:18
  30.8 5.8 %collective-permute-start.4 = (bf16[80,488]{1,0:T(8,128)(2,1)S(1)}, bf16[80,488]{1,0:T(8,128)(2,1)S(1)}, u32[]{:S(2)}, u32[]{:S(2)}) collective-permute-start(bf16[80,488]{1,0:T(8,128)(2,1)S(1)} %gather_fusion.4), channel_id=1, source_target_pairs={{0,64},{64,0},{4,68},{68,4},{8,72},{72,8},{12,76},{76,12},{16,80},... | collective-permute-start | bytes 234248 | tf_op jit(solution)/shard_map/ppermute | solution.py:18
  37.3 10.4 %collective-permute-start.5 = (bf16[80,488]{1,0:T(8,128)(2,1)S(1)}, bf16[80,488]{1,0:T(8,128)(2,1)S(1)}, u32[]{:S(2)}, u32[]{:S(2)}) collective-permute-start(bf16[80,488]{1,0:T(8,128)(2,1)S(1)} %gather_fusion.5), channel_id=1, source_target_pairs={{0,128},{128,0},{4,132},{132,4},{8,136},{136,8},{12,140},{140,12},... | collective-permute-start | bytes 234248 | tf_op jit(solution)/shard_map/ppermute | solution.py:18
  47.8 2.4 %copy-start = (bf16[10,488,488]{2,1,0:T(8,128)(2,1)S(1)}, bf16[10,488,488]{2,1,0:T(8,128)(2,1)}, u32[]{:S(2)}) copy-start(bf16[10,488,488]{2,1,0:T(8,128)(2,1)} %k_ref.11) | copy-start | bytes 14288644
  63.2 19.2 %collective-permute-start.6 = (f32[64,488]{1,0:T(8,128)S(1)}, f32[64,488]{1,0:T(8,128)S(1)}, u32[]{:S(2)}, u32[]{:S(2)}) collective-permute-start(f32[64,488]{1,0:T(8,128)S(1)} %get-tuple-element.74), channel_id=1, source_target_pairs={{0,1},{1,2},{2,3},{3,0},{4,5},{5,6},{6,7},{7,4},{8,9},{9,10},{10,1... | collective-permute-start | bytes 374792 | tf_op jit(solution)/shard_map/ppermute | solution.py:204
  64.8 17.7 %collective-permute-start.7 = (f32[64,488]{1,0:T(8,128)S(1)}, f32[64,488]{1,0:T(8,128)S(1)}, u32[]{:S(2)}, u32[]{:S(2)}) collective-permute-start(f32[64,488]{1,0:T(8,128)S(1)} %get-tuple-element.76), channel_id=1, source_target_pairs={{0,2},{1,3},{2,0},{3,1},{4,6},{5,7},{6,4},{7,5},{8,10},{9,11},{10,... | collective-permute-start | bytes 374792 | tf_op jit(solution)/shard_map/ppermute | solution.py:204
  67.5 15.0 %collective-permute-start.8 = (f32[64,488]{1,0:T(8,128)S(1)}, f32[64,488]{1,0:T(8,128)S(1)}, u32[]{:S(2)}, u32[]{:S(2)}) collective-permute-start(f32[64,488]{1,0:T(8,128)S(1)} %get-tuple-element.75), channel_id=1, source_target_pairs={{0,3},{1,0},{2,1},{3,2},{4,7},{5,4},{6,5},{7,6},{8,11},{9,8},{10,9... | collective-permute-start | bytes 374792 | tf_op jit(solution)/shard_map/ppermute | solution.py:204
  79.1 18.4 %collective-permute-start.10 = (f32[64,488]{1,0:T(8,128)S(1)}, f32[64,488]{1,0:T(8,128)S(1)}, u32[]{:S(2)}, u32[]{:S(2)}) collective-permute-start(f32[64,488]{1,0:T(8,128)S(1)} %get-tuple-element.82), channel_id=1, source_target_pairs={{0,2},{1,3},{2,0},{3,1},{4,6},{5,7},{6,4},{7,5},{8,10},{9,11},{10,... | collective-permute-start | bytes 374792 | tf_op jit(solution)/shard_map/ppermute | solution.py:204
  79.7 18.0 %collective-permute-start.11 = (f32[64,488]{1,0:T(8,128)S(1)}, f32[64,488]{1,0:T(8,128)S(1)}, u32[]{:S(2)}, u32[]{:S(2)}) collective-permute-start(f32[64,488]{1,0:T(8,128)S(1)} %get-tuple-element.81), channel_id=1, source_target_pairs={{0,3},{1,0},{2,1},{3,2},{4,7},{5,4},{6,5},{7,6},{8,11},{9,8},{10,9... | collective-permute-start | bytes 374792 | tf_op jit(solution)/shard_map/ppermute | solution.py:204
  82.5 15.2 %collective-permute-start.9 = (f32[64,488]{1,0:T(8,128)S(1)}, f32[64,488]{1,0:T(8,128)S(1)}, u32[]{:S(2)}, u32[]{:S(2)}) collective-permute-start(f32[64,488]{1,0:T(8,128)S(1)} %get-tuple-element.80), channel_id=1, source_target_pairs={{0,1},{1,2},{2,3},{3,0},{4,5},{5,6},{6,7},{7,4},{8,9},{9,10},{10,1... | collective-permute-start | bytes 374792 | tf_op jit(solution)/shard_map/ppermute | solution.py:204
  92.7 17.1 %collective-permute-start.12 = (f32[64,488]{1,0:T(8,128)S(1)}, f32[64,488]{1,0:T(8,128)S(1)}, u32[]{:S(2)}, u32[]{:S(2)}) collective-permute-start(f32[64,488]{1,0:T(8,128)S(1)} %get-tuple-element.71), channel_id=1, source_target_pairs={{0,1},{1,2},{2,3},{3,0},{4,5},{5,6},{6,7},{7,4},{8,9},{9,10},{10,1... | collective-permute-start | bytes 374792 | tf_op jit(solution)/shard_map/ppermute | solution.py:204
  93.0 19.6 %collective-permute-start.13 = (f32[64,488]{1,0:T(8,128)S(1)}, f32[64,488]{1,0:T(8,128)S(1)}, u32[]{:S(2)}, u32[]{:S(2)}) collective-permute-start(f32[64,488]{1,0:T(8,128)S(1)} %get-tuple-element.73), channel_id=1, source_target_pairs={{0,2},{1,3},{2,0},{3,1},{4,6},{5,7},{6,4},{7,5},{8,10},{9,11},{10,... | collective-permute-start | bytes 374792 | tf_op jit(solution)/shard_map/ppermute | solution.py:204
  97.5 15.1 %collective-permute-start.14 = (f32[64,488]{1,0:T(8,128)S(1)}, f32[64,488]{1,0:T(8,128)S(1)}, u32[]{:S(2)}, u32[]{:S(2)}) collective-permute-start(f32[64,488]{1,0:T(8,128)S(1)} %get-tuple-element.72), channel_id=1, source_target_pairs={{0,3},{1,0},{2,1},{3,2},{4,7},{5,4},{6,5},{7,6},{8,11},{9,8},{10,9... | collective-permute-start | bytes 374792 | tf_op jit(solution)/shard_map/ppermute | solution.py:204
  107.9 6.3 %collective-permute-start.15 = (f32[64,488]{1,0:T(8,128)S(1)}, f32[64,488]{1,0:T(8,128)S(1)}, u32[]{:S(2)}, u32[]{:S(2)}) collective-permute-start(f32[64,488]{1,0:T(8,128)S(1)} %get-tuple-element.77), channel_id=1, source_target_pairs={{0,1},{1,2},{2,3},{3,0},{4,5},{5,6},{6,7},{7,4},{8,9},{9,10},{10,1... | collective-permute-start | bytes 374792 | tf_op jit(solution)/shard_map/ppermute | solution.py:204
  109.8 6.5 %collective-permute-start.16 = (f32[64,488]{1,0:T(8,128)S(1)}, f32[64,488]{1,0:T(8,128)S(1)}, u32[]{:S(2)}, u32[]{:S(2)}) collective-permute-start(f32[64,488]{1,0:T(8,128)S(1)} %get-tuple-element.79), channel_id=1, source_target_pairs={{0,2},{1,3},{2,0},{3,1},{4,6},{5,7},{6,4},{7,5},{8,10},{9,11},{10,... | collective-permute-start | bytes 374792 | tf_op jit(solution)/shard_map/ppermute | solution.py:204
  109.8 6.6 %collective-permute-start.17 = (f32[64,488]{1,0:T(8,128)S(1)}, f32[64,488]{1,0:T(8,128)S(1)}, u32[]{:S(2)}, u32[]{:S(2)}) collective-permute-start(f32[64,488]{1,0:T(8,128)S(1)} %get-tuple-element.78), channel_id=1, source_target_pairs={{0,3},{1,0},{2,1},{3,2},{4,7},{5,4},{6,5},{7,6},{8,11},{9,8},{10,9... | collective-permute-start | bytes 374792 | tf_op jit(solution)/shard_map/ppermute | solution.py:204

commit v5 on v3

--- a/solution.py
+++ b/solution.py
@@ -45,40 +45,49 @@
     )(target, split)
 
 
-def translate_kernel(spread, devices, slot_ref, buf_ref, k_ref, *rest):
+def translate_kernel(spread, devices, classes, slot_ref, buf_ref, k_ref, *rest):
     *rest, column_ref = rest
-    if spread:
-        high_ref, low_ref, t_ref, out_ref = rest
-        nt = (((1,), (1,)), ((), ()))
-        octants = t_ref.shape[0]
-        span = high_ref.shape[0] // devices
-        for h in range(octants):
-            term = lax.dot_general(
-                high_ref[...], t_ref[h], nt, preferred_element_type=jnp.float32
-            ) + lax.dot_general(low_ref[...], t_ref[h], nt, preferred_element_type=jnp.float32)
-            for d in range(devices):
-                at = (d * octants + h) * span
-                out_ref[at:at + span, :] = term[d * span:(d + 1) * span]
-    else:
-        (out_ref,) = rest
-        out_ref[...] = jnp.zeros(out_ref.shape, out_ref.dtype)
+    step = pl.program_id(0)
+    out_ref = rest[-1]
+
+    def init(rest):
+        if spread:
+            high_ref, low_ref, t_ref, out_ref = rest
+            nt = (((1,), (1,)), ((), ()))
+            octants = t_ref.shape[0]
+            span = high_ref.shape[0] // devices
+            for h in range(octants):
+                term = lax.dot_general(
+                    high_ref[...], t_ref[h], nt, preferred_element_type=jnp.float32
+                ) + lax.dot_general(low_ref[...], t_ref[h], nt, preferred_element_type=jnp.float32)
+                for d in range(devices):
+                    at = (d * octants + h) * span
+                    out_ref[at:at + span, :] = term[d * span:(d + 1) * span]
+        else:
+            (out_ref,) = rest
+            out_ref[...] = jnp.zeros(out_ref.shape, out_ref.dtype)
+
+    @pl.when(step == 0)
+    def _():
+        init(rest)
+        columns = jnp.transpose(slot_ref[...])
+        for c in range(classes):
+            column_ref[c] = columns[:, c:c + 1]
+
     rows = buf_ref.shape[0]
     tile = out_ref.shape[0]
-    columns = jnp.transpose(slot_ref[...])
-    for c in range(k_ref.shape[0]):
-        column_ref[c] = columns[:, c:c + 1]
+    per_step = k_ref.shape[0]
 
     def one_class(c, carry):
-        hot = (column_ref[c] == lax.broadcasted_iota(jnp.int32, (tile, rows), 1)).astype(
-            buf_ref.dtype
-        )
+        spots = lax.broadcasted_iota(jnp.int32, (tile, rows), 1)
+        hot = (column_ref[step * per_step + c] == spots).astype(buf_ref.dtype)
         picked = jnp.dot(hot, buf_ref[...], preferred_element_type=jnp.float32)
         out_ref[...] += jnp.dot(
             picked.astype(k_ref.dtype), k_ref[c], preferred_element_type=jnp.float32
         )
         return carry
 
-    lax.fori_loop(0, k_ref.shape[0], one_class, 0, unroll=5)
+    lax.fori_loop(0, per_step, one_class, 0, unroll=True)
 
 
 def translate(slot, buffer, kernels, chunk, tile, spread=None, devices=1, rows=None, row_block=0):
@@ -88,7 +97,7 @@
     in_specs = [
         pl.BlockSpec((slot.shape[0], tile), lambda g: (0, chunk)),
         pl.BlockSpec((rows, width), lambda g: (row_block, 0)),
-        pl.BlockSpec((classes, width, width), lambda g: (0, 0, 0)),
+        pl.BlockSpec((classes // 2, width, width), lambda g: (g, 0, 0)),
     ]
     operands = [slot, buffer, kernels]
     if spread is not None:
@@ -102,8 +111,8 @@
         operands += [high, low, transfer]
     flops = 2 * classes * tile * width * (rows + width)
     return pl.pallas_call(
-        functools.partial(translate_kernel, spread is not None, devices),
-        grid=(1,),
+        functools.partial(translate_kernel, spread is not None, devices, classes),
+        grid=(2,),
         in_specs=in_specs,
         out_specs=pl.BlockSpec((tile, width), lambda g: (0, 0)),
         out_shape=jax.ShapeDtypeStruct((tile, width), jnp.float32),

time: 118 us -> 114 us (0.966)
  Pallas kernels: 54.5 us -> 50.7 us
    pallas_call x6, Pallas kernels: 49.3 us -> 45.5 us  [translate(): pl.pallas_call(functools.partial(translate_kernel, spread is not None, de...]
  transfers between devices with their start and end apart: 18 -> 18, of which waited for: 8 -> 8; matrix products, arithmetic and copies ran while one was open for 2% -> 2% of each run, Pallas kernels for 30% -> 29%
where the time goes in v5:
time: 114 us
  Pallas kernels  50.7 us (44%)
  starting transfers between devices  35.7 us (31%)
  waiting for transfers between devices  13.2 us (12%)
  local copies, waits for them, and re-layouts  11.7 us (10%)
  other arithmetic  2.08 us (2%)
    pallas_call x6, Pallas kernels, translate(): pl.pallas_call(functools.partial(translate_kernel, spread is not None, de...  45.5 us
    ppermute x12, starting transfers between devices, on_device(): total = total + lax.ppermute(sent, 'off', route)  18.7 us
    ppermute x6, starting transfers between devices, partner(): return lax.ppermute(block, axis, route)  17 us
    ppermute x6, waiting for transfers between devices, partner(): return lax.ppermute(block, axis, route)  9.37 us
    pallas_call x6, Pallas kernels, slot_table(): pl.pallas_call(invert_kernel, out_shape=jax.ShapeDtypeStruct((classes, pa...  5.2 us
    gather x6, local copies, waits for them, and re-layouts, on_device(): outgoing = rows_all[picks]  4.43 us
    ppermute x12, waiting for transfers between devices, on_device(): total = total + lax.ppermute(sent, 'off', route)  3.82 us
    unnamed x18, local copies, waits for them, and re-layouts  3.65 us
  transfers between devices with their start and end apart: 18, of which 8 were waited for; matrix products, arithmetic and copies ran while one was open for 2% of the time, Pallas kernels for 29%

profile of v5, /device:TPU:16, one launch (start us, length us, event | category | flops | bytes accessed | tf_op | source)
XLA Modules:
  0.0 114.0 jit_solution(10670300055073752358)
XLA Ops:
  0.0 0.8 slice_bitcast_fusion
  0.8 0.7 add_bitcast_fusion.2
  1.6 1.5 %copy.242.buf_ref = bf16[1024,488]{1,0:T(8,128)(2,1)S(1)} copy(bf16[1024,488]{0,1:T(8,128)(2,1)} %param.11) | data formatting | bytes 1998848 | tf_op args[0]
  3.5 2.1 %copy-done = bf16[8,488,488]{2,1,0:T(8,128)(2,1)S(1)} copy-done((bf16[8,488,488]{2,1,0:T(8,128)(2,1)S(1)}, bf16[8,488,488]{2,1,0:T(8,128)(2,1)}, u32[]{:S(2)}) %copy-start) | copy-done | bytes 3810328
  5.6 3.2 %shard_map.109 = f32[128,488]{1,0:T(8,128)S(1)} custom-call(s32[16,128]{1,0:T(8,128)S(1)} %fusion.18.slot_ref, bf16[1024,488]{1,0:T(8,128)(2,1)S(1)} %copy.242.buf_ref, bf16[8,488,488]{2,1,0:T(8,128)(2,1)S(1)} %copy-done), custom_call_target="tpu_custom_call" | custom-call | flops 1511129088 | bytes 4809728 | tf_op jit(solution)/shard_map/pallas_call | solution.py:113
  8.9 0.7 gather_fusion
  10.3 0.9 shard_map.110
  11.4 0.7 gather_fusion.1
  12.3 1.4 %collective-permute-start.1 = (bf16[80,488]{1,0:T(8,128)(2,1)S(1)}, bf16[80,488]{1,0:T(8,128)(2,1)S(1)}, u32[]{:S(2)}, u32[]{:S(2)}) collective-permute-start(bf16[80,488]{1,0:T(8,128)(2,1)S(1)} %gather_fusion.1), channel_id=1, source_target_pairs={{0,8},{8,0},{4,12},{12,4},{16,24},{24,16},{20,28},{28,20},{32,40},... | collective-permute-start | bytes 234248 | tf_op jit(solution)/shard_map/ppermute | solution.py:18
  13.7 0.9 shard_map.111
  14.6 2.6 %collective-permute-done.1 = bf16[80,488]{1,0:T(8,128)(2,1)S(1)} collective-permute-done((bf16[80,488]{1,0:T(8,128)(2,1)S(1)}, bf16[80,488]{1,0:T(8,128)(2,1)S(1)}, u32[]{:S(2)}, u32[]{:S(2)}) %collective-permute-start.1) | collective-permute-done | bytes 78112 | tf_op jit(solution)/shard_map/ppermute | solution.py:18
  17.2 0.7 gather_fusion.2
  18.1 2.2 %collective-permute-start.2 = (bf16[80,488]{1,0:T(8,128)(2,1)S(1)}, bf16[80,488]{1,0:T(8,128)(2,1)S(1)}, u32[]{:S(2)}, u32[]{:S(2)}) collective-permute-start(bf16[80,488]{1,0:T(8,128)(2,1)S(1)} %gather_fusion.2), channel_id=1, source_target_pairs={{0,16},{16,0},{4,20},{20,4},{8,24},{24,8},{12,28},{28,12},{32,48},... | collective-permute-start | bytes 234248 | tf_op jit(solution)/shard_map/ppermute | solution.py:18
  20.3 0.9 shard_map.112
  21.2 2.9 %collective-permute-done.2 = bf16[80,488]{1,0:T(8,128)(2,1)S(1)} collective-permute-done((bf16[80,488]{1,0:T(8,128)(2,1)S(1)}, bf16[80,488]{1,0:T(8,128)(2,1)S(1)}, u32[]{:S(2)}, u32[]{:S(2)}) %collective-permute-start.2) | collective-permute-done | bytes 78112 | tf_op jit(solution)/shard_map/ppermute | solution.py:18
  24.1 0.7 gather_fusion.3
  25.0 2.0 %collective-permute-start.3 = (bf16[80,488]{1,0:T(8,128)(2,1)S(1)}, bf16[80,488]{1,0:T(8,128)(2,1)S(1)}, u32[]{:S(2)}, u32[]{:S(2)}) collective-permute-start(bf16[80,488]{1,0:T(8,128)(2,1)S(1)} %gather_fusion.3), channel_id=1, source_target_pairs={{0,32},{32,0},{4,36},{36,4},{8,40},{40,8},{12,44},{44,12},{16,48},... | collective-permute-start | bytes 234248 | tf_op jit(solution)/shard_map/ppermute | solution.py:18
  27.1 0.9 shard_map.113
  28.0 1.6 %collective-permute-done.3 = bf16[80,488]{1,0:T(8,128)(2,1)S(1)} collective-permute-done((bf16[80,488]{1,0:T(8,128)(2,1)S(1)}, bf16[80,488]{1,0:T(8,128)(2,1)S(1)}, u32[]{:S(2)}, u32[]{:S(2)}) %collective-permute-start.3) | collective-permute-done | bytes 78112 | tf_op jit(solution)/shard_map/ppermute | solution.py:18
  29.6 0.7 gather_fusion.4
  30.5 3.4 %collective-permute-start.4 = (bf16[80,488]{1,0:T(8,128)(2,1)S(1)}, bf16[80,488]{1,0:T(8,128)(2,1)S(1)}, u32[]{:S(2)}, u32[]{:S(2)}) collective-permute-start(bf16[80,488]{1,0:T(8,128)(2,1)S(1)} %gather_fusion.4), channel_id=1, source_target_pairs={{0,64},{64,0},{4,68},{68,4},{8,72},{72,8},{12,76},{76,12},{16,80},... | collective-permute-start | bytes 234248 | tf_op jit(solution)/shard_map/ppermute | solution.py:18
  33.9 0.9 shard_map.114
  34.8 1.5 %collective-permute-done.4 = bf16[80,488]{1,0:T(8,128)(2,1)S(1)} collective-permute-done((bf16[80,488]{1,0:T(8,128)(2,1)S(1)}, bf16[80,488]{1,0:T(8,128)(2,1)S(1)}, u32[]{:S(2)}, u32[]{:S(2)}) %collective-permute-start.4) | collective-permute-done | bytes 78112 | tf_op jit(solution)/shard_map/ppermute | solution.py:18
  36.3 0.7 gather_fusion.5
  37.0 8.0 %collective-permute-start.5 = (bf16[80,488]{1,0:T(8,128)(2,1)S(1)}, bf16[80,488]{1,0:T(8,128)(2,1)S(1)}, u32[]{:S(2)}, u32[]{:S(2)}) collective-permute-start(bf16[80,488]{1,0:T(8,128)(2,1)S(1)} %gather_fusion.5), channel_id=1, source_target_pairs={{0,128},{128,0},{4,132},{132,4},{8,136},{136,8},{12,140},{140,12},... | collective-permute-start | bytes 234248 | tf_op jit(solution)/shard_map/ppermute | solution.py:18
  45.0 0.5 shard_map.115
  45.6 0.2 copy.261
  45.8 0.5 copy.262
  46.5 0.9 collective-permute-done.5
  47.4 4.5 %shard_map.116 = f32[128,488]{1,0:T(8,128)S(1)} custom-call(s32[16,128]{1,0:T(8,128)S(1)} %pad.61.slot_ref, bf16[1792,488]{1,0:T(8,128)(2,1)S(1)} %slice_dynamic-update-slice_fusion.6.buf_ref, bf16[10,488,488]{2,1,0:T(8,128)(2,1)} %k_ref.11), custom_call_target="tpu_custom_call" | custom-call | flops 889487360 | bytes 6511872 | tf_op jit(solution)/shard_map/pallas_call | solution.py:113
  52.0 9.4 %shard_map.117 = f32[256,488]{1,0:T(8,128)S(1)} custom-call(s32[16,1024]{1,0:T(8,128)S(1)} %pad.58.slot_ref, bf16[1792,488]{1,0:T(8,128)(2,1)S(1)} %slice_dynamic-update-slice_fusion.6.buf_ref, bf16[10,488,488]{2,1,0:T(8,128)(2,1)} %k_ref.11, bf16[128,488]{1,0:T(8,128)(2,1)S(1)} %get-tuple-element.84.rest_0_, ...), custom_call_target="tpu_custom_call" | custom-call | flops 4737269760 | bytes 6511872 | tf_op jit(solution)/shard_map/pallas_call | solution.py:113
  61.5 1.6 %collective-permute-start.6 = (f32[64,488]{1,0:T(8,128)S(1)}, f32[64,488]{1,0:T(8,128)S(1)}, u32[]{:S(2)}, u32[]{:S(2)}) collective-permute-start(f32[64,488]{1,0:T(8,128)S(1)} %get-tuple-element.74), channel_id=1, source_target_pairs={{0,1},{1,2},{2,3},{3,0},{4,5},{5,6},{6,7},{7,4},{8,9},{9,10},{10,1... | collective-permute-start | bytes 374792 | tf_op jit(solution)/shard_map/ppermute | solution.py:215
  63.1 2.7 %collective-permute-start.7 = (f32[64,488]{1,0:T(8,128)S(1)}, f32[64,488]{1,0:T(8,128)S(1)}, u32[]{:S(2)}, u32[]{:S(2)}) collective-permute-start(f32[64,488]{1,0:T(8,128)S(1)} %get-tuple-element.76), channel_id=1, source_target_pairs={{0,2},{1,3},{2,0},{3,1},{4,6},{5,7},{6,4},{7,5},{8,10},{9,11},{10,... | collective-permute-start | bytes 374792 | tf_op jit(solution)/shard_map/ppermute | solution.py:215
  65.8 1.4 %collective-permute-start.8 = (f32[64,488]{1,0:T(8,128)S(1)}, f32[64,488]{1,0:T(8,128)S(1)}, u32[]{:S(2)}, u32[]{:S(2)}) collective-permute-start(f32[64,488]{1,0:T(8,128)S(1)} %get-tuple-element.75), channel_id=1, source_target_pairs={{0,3},{1,0},{2,1},{3,2},{4,7},{5,4},{6,5},{7,6},{8,11},{9,8},{10,9... | collective-permute-start | bytes 374792 | tf_op jit(solution)/shard_map/ppermute | solution.py:215
  67.2 9.4 %shard_map.118 = f32[256,488]{1,0:T(8,128)S(1)} custom-call(s32[16,1024]{1,0:T(8,128)S(1)} %pad.58.slot_ref, bf16[1792,488]{1,0:T(8,128)(2,1)S(1)} %slice_dynamic-update-slice_fusion.6.buf_ref, bf16[10,488,488]{2,1,0:T(8,128)(2,1)} %k_ref.11, bf16[128,488]{1,0:T(8,128)(2,1)S(1)} %get-tuple-element.84.rest_0_, ...), custom_call_target="tpu_custom_call" | custom-call | flops 4737269760 | bytes 6511872 | tf_op jit(solution)/shard_map/pallas_call | solution.py:113
  76.7 0.6 collective-permute-start.10
  77.3 2.8 %collective-permute-start.11 = (f32[64,488]{1,0:T(8,128)S(1)}, f32[64,488]{1,0:T(8,128)S(1)}, u32[]{:S(2)}, u32[]{:S(2)}) collective-permute-start(f32[64,488]{1,0:T(8,128)S(1)} %get-tuple-element.81), channel_id=1, source_target_pairs={{0,3},{1,0},{2,1},{3,2},{4,7},{5,4},{6,5},{7,6},{8,11},{9,8},{10,9... | collective-permute-start | bytes 374792 | tf_op jit(solution)/shard_map/ppermute | solution.py:215
  80.1 9.4 %shard_map.119 = f32[256,488]{1,0:T(8,128)S(1)} custom-call(s32[16,1024]{1,0:T(8,128)S(1)} %pad.58.slot_ref, bf16[1792,488]{1,0:T(8,128)(2,1)S(1)} %slice_dynamic-update-slice_fusion.6.buf_ref, bf16[10,488,488]{2,1,0:T(8,128)(2,1)} %k_ref.11, bf16[128,488]{1,0:T(8,128)(2,1)S(1)} %get-tuple-element.84.rest_0_, ...), custom_call_target="tpu_custom_call" | custom-call | flops 4737269760 | bytes 6511872 | tf_op jit(solution)/shard_map/pallas_call | solution.py:113
  89.6 0.3 collective-permute-start.12
  89.9 4.5 %collective-permute-start.13 = (f32[64,488]{1,0:T(8,128)S(1)}, f32[64,488]{1,0:T(8,128)S(1)}, u32[]{:S(2)}, u32[]{:S(2)}) collective-permute-start(f32[64,488]{1,0:T(8,128)S(1)} %get-tuple-element.73), channel_id=1, source_target_pairs={{0,2},{1,3},{2,0},{3,1},{4,6},{5,7},{6,4},{7,5},{8,10},{9,11},{10,... | collective-permute-start | bytes 374792 | tf_op jit(solution)/shard_map/ppermute | solution.py:215
  94.4 0.2 collective-permute-start.14
  94.7 9.4 %shard_map.120 = f32[256,488]{1,0:T(8,128)S(1)} custom-call(s32[16,1024]{1,0:T(8,128)S(1)} %pad.58.slot_ref, bf16[1792,488]{1,0:T(8,128)(2,1)S(1)} %slice_dynamic-update-slice_fusion.6.buf_ref, bf16[10,488,488]{2,1,0:T(8,128)(2,1)} %k_ref.11, bf16[128,488]{1,0:T(8,128)(2,1)S(1)} %get-tuple-element.84.rest_0_, ...), custom_call_target="tpu_custom_call" | custom-call | flops 4737269760 | bytes 6511872 | tf_op jit(solution)/shard_map/pallas_call | solution.py:113
  104.1 1.9 %collective-permute-start.15 = (f32[64,488]{1,0:T(8,128)S(1)}, f32[64,488]{1,0:T(8,128)S(1)}, u32[]{:S(2)}, u32[]{:S(2)}) collective-permute-start(f32[64,488]{1,0:T(8,128)S(1)} %get-tuple-element.77), channel_id=1, source_target_pairs={{0,1},{1,2},{2,3},{3,0},{4,5},{5,6},{6,7},{7,4},{8,9},{9,10},{10,1... | collective-permute-start | bytes 374792 | tf_op jit(solution)/shard_map/ppermute | solution.py:215
  106.0 2.8 %collective-permute-start.17 = (f32[64,488]{1,0:T(8,128)S(1)}, f32[64,488]{1,0:T(8,128)S(1)}, u32[]{:S(2)}, u32[]{:S(2)}) collective-permute-start(f32[64,488]{1,0:T(8,128)S(1)} %get-tuple-element.78), channel_id=1, source_target_pairs={{0,3},{1,0},{2,1},{3,2},{4,7},{5,4},{6,5},{7,6},{8,11},{9,8},{10,9... | collective-permute-start | bytes 374792 | tf_op jit(solution)/shard_map/ppermute | solution.py:215
  108.9 1.5 %collective-permute-done.15 = f32[64,488]{1,0:T(8,128)S(1)} collective-permute-done((f32[64,488]{1,0:T(8,128)S(1)}, f32[64,488]{1,0:T(8,128)S(1)}, u32[]{:S(2)}, u32[]{:S(2)}) %collective-permute-start.15) | collective-permute-done | bytes 124960 | tf_op jit(solution)/shard_map/ppermute | solution.py:215
  110.4 2.1 %collective-permute-done.16 = f32[64,488]{1,0:T(8,128)S(1)} collective-permute-done((f32[64,488]{1,0:T(8,128)S(1)}, f32[64,488]{1,0:T(8,128)S(1)}, u32[]{:S(2)}, u32[]{:S(2)}) %collective-permute-start.16) | collective-permute-done | bytes 124960 | tf_op jit(solution)/shard_map/ppermute | solution.py:215
  112.8 0.3 copy.288
  113.1 1.0 copy.264
  (105 shorter events, 2.5 us)
Async XLA Ops:
  0.0 3.1 %copy-start.1 = (s32[1,10,1024]{2,0,1:T(1,128)S(1)}, s32[1,10,1024]{2,0,1:T(1,128)}, u32[]{:S(2)}) copy-start(s32[1,10,1024]{2,0,1:T(1,128)} %param.15) | copy-start | bytes 122884
  0.0 3.2 %copy-start.2 = (s32[1,10,1024]{2,0,1:T(1,128)S(1)}, s32[1,10,1024]{2,0,1:T(1,128)}, u32[]{:S(2)}) copy-start(s32[1,10,1024]{2,0,1:T(1,128)} %param.14) | copy-start | bytes 122884
  0.0 3.2 %copy-start.3 = (s32[1,10]{1,0:T(1,128)S(1)}, s32[1,10]{1,0:T(1,128)}, u32[]{:S(2)}) copy-start(s32[1,10]{1,0:T(1,128)} %param.16) | copy-start | bytes 124
  3.5 2.1 %copy-start = (bf16[8,488,488]{2,1,0:T(8,128)(2,1)S(1)}, bf16[8,488,488]{2,1,0:T(8,128)(2,1)}, u32[]{:S(2)}) copy-start(bf16[8,488,488]{2,1,0:T(8,128)(2,1)} %rest_2_.7) | copy-start | bytes 11430916
  5.6 4.5 %copy-start.4 = (s32[1,10,128]{2,0,1:T(1,128)S(1)}, s32[1,10,128]{2,0,1:T(1,128)}, u32[]{:S(2)}) copy-start(s32[1,10,128]{2,0,1:T(1,128)} %param.18) | copy-start | bytes 15364
  5.6 4.5 %copy-start.6 = (s32[1,10]{1,0:T(1,128)S(1)}, s32[1,10]{1,0:T(1,128)}, u32[]{:S(2)}) copy-start(s32[1,10]{1,0:T(1,128)} %param.19) | copy-start | bytes 124
  5.6 4.6 %copy-start.5 = (s32[1,10,128]{2,0,1:T(1,128)S(1)}, s32[1,10,128]{2,0,1:T(1,128)}, u32[]{:S(2)}) copy-start(s32[1,10,128]{2,0,1:T(1,128)} %param.17) | copy-start | bytes 15364
  9.6 1.7 %collective-permute-start = (bf16[80,488]{1,0:T(8,128)(2,1)S(1)}, bf16[80,488]{1,0:T(8,128)(2,1)S(1)}, u32[]{:S(2)}, u32[]{:S(2)}) collective-permute-start(bf16[80,488]{1,0:T(8,128)(2,1)S(1)} %gather_fusion), channel_id=1, source_target_pairs={{0,4},{4,0},{8,12},{12,8},{16,20},{20,16},{24,28},{28,24},{32,36},... | collective-permute-start | bytes 234248 | tf_op jit(solution)/shard_map/ppermute | solution.py:18
  12.3 4.9 %collective-permute-start.1 = (bf16[80,488]{1,0:T(8,128)(2,1)S(1)}, bf16[80,488]{1,0:T(8,128)(2,1)S(1)}, u32[]{:S(2)}, u32[]{:S(2)}) collective-permute-start(bf16[80,488]{1,0:T(8,128)(2,1)S(1)} %gather_fusion.1), channel_id=1, source_target_pairs={{0,8},{8,0},{4,12},{12,4},{16,24},{24,16},{20,28},{28,20},{32,40},... | collective-permute-start | bytes 234248 | tf_op jit(solution)/shard_map/ppermute | solution.py:18
  18.1 6.0 %collective-permute-start.2 = (bf16[80,488]{1,0:T(8,128)(2,1)S(1)}, bf16[80,488]{1,0:T(8,128)(2,1)S(1)}, u32[]{:S(2)}, u32[]{:S(2)}) collective-permute-start(bf16[80,488]{1,0:T(8,128)(2,1)S(1)} %gather_fusion.2), channel_id=1, source_target_pairs={{0,16},{16,0},{4,20},{20,4},{8,24},{24,8},{12,28},{28,12},{32,48},... | collective-permute-start | bytes 234248 | tf_op jit(solution)/shard_map/ppermute | solution.py:18
  25.0 4.5 %collective-permute-start.3 = (bf16[80,488]{1,0:T(8,128)(2,1)S(1)}, bf16[80,488]{1,0:T(8,128)(2,1)S(1)}, u32[]{:S(2)}, u32[]{:S(2)}) collective-permute-start(bf16[80,488]{1,0:T(8,128)(2,1)S(1)} %gather_fusion.3), channel_id=1, source_target_pairs={{0,32},{32,0},{4,36},{36,4},{8,40},{40,8},{12,44},{44,12},{16,48},... | collective-permute-start | bytes 234248 | tf_op jit(solution)/shard_map/ppermute | solution.py:18
  30.5 5.8 %collective-permute-start.4 = (bf16[80,488]{1,0:T(8,128)(2,1)S(1)}, bf16[80,488]{1,0:T(8,128)(2,1)S(1)}, u32[]{:S(2)}, u32[]{:S(2)}) collective-permute-start(bf16[80,488]{1,0:T(8,128)(2,1)S(1)} %gather_fusion.4), channel_id=1, source_target_pairs={{0,64},{64,0},{4,68},{68,4},{8,72},{72,8},{12,76},{76,12},{16,80},... | collective-permute-start | bytes 234248 | tf_op jit(solution)/shard_map/ppermute | solution.py:18
  37.0 10.4 %collective-permute-start.5 = (bf16[80,488]{1,0:T(8,128)(2,1)S(1)}, bf16[80,488]{1,0:T(8,128)(2,1)S(1)}, u32[]{:S(2)}, u32[]{:S(2)}) collective-permute-start(bf16[80,488]{1,0:T(8,128)(2,1)S(1)} %gather_fusion.5), channel_id=1, source_target_pairs={{0,128},{128,0},{4,132},{132,4},{8,136},{136,8},{12,140},{140,12},... | collective-permute-start | bytes 234248 | tf_op jit(solution)/shard_map/ppermute | solution.py:18
  61.5 18.6 %collective-permute-start.6 = (f32[64,488]{1,0:T(8,128)S(1)}, f32[64,488]{1,0:T(8,128)S(1)}, u32[]{:S(2)}, u32[]{:S(2)}) collective-permute-start(f32[64,488]{1,0:T(8,128)S(1)} %get-tuple-element.74), channel_id=1, source_target_pairs={{0,1},{1,2},{2,3},{3,0},{4,5},{5,6},{6,7},{7,4},{8,9},{9,10},{10,1... | collective-permute-start | bytes 374792 | tf_op jit(solution)/shard_map/ppermute | solution.py:215
  63.1 17.0 %collective-permute-start.7 = (f32[64,488]{1,0:T(8,128)S(1)}, f32[64,488]{1,0:T(8,128)S(1)}, u32[]{:S(2)}, u32[]{:S(2)}) collective-permute-start(f32[64,488]{1,0:T(8,128)S(1)} %get-tuple-element.76), channel_id=1, source_target_pairs={{0,2},{1,3},{2,0},{3,1},{4,6},{5,7},{6,4},{7,5},{8,10},{9,11},{10,... | collective-permute-start | bytes 374792 | tf_op jit(solution)/shard_map/ppermute | solution.py:215
  65.8 14.3 %collective-permute-start.8 = (f32[64,488]{1,0:T(8,128)S(1)}, f32[64,488]{1,0:T(8,128)S(1)}, u32[]{:S(2)}, u32[]{:S(2)}) collective-permute-start(f32[64,488]{1,0:T(8,128)S(1)} %get-tuple-element.75), channel_id=1, source_target_pairs={{0,3},{1,0},{2,1},{3,2},{4,7},{5,4},{6,5},{7,6},{8,11},{9,8},{10,9... | collective-permute-start | bytes 374792 | tf_op jit(solution)/shard_map/ppermute | solution.py:215
  76.7 17.7 %collective-permute-start.10 = (f32[64,488]{1,0:T(8,128)S(1)}, f32[64,488]{1,0:T(8,128)S(1)}, u32[]{:S(2)}, u32[]{:S(2)}) collective-permute-start(f32[64,488]{1,0:T(8,128)S(1)} %get-tuple-element.82), channel_id=1, source_target_pairs={{0,2},{1,3},{2,0},{3,1},{4,6},{5,7},{6,4},{7,5},{8,10},{9,11},{10,... | collective-permute-start | bytes 374792 | tf_op jit(solution)/shard_map/ppermute | solution.py:215
  77.3 17.3 %collective-permute-start.11 = (f32[64,488]{1,0:T(8,128)S(1)}, f32[64,488]{1,0:T(8,128)S(1)}, u32[]{:S(2)}, u32[]{:S(2)}) collective-permute-start(f32[64,488]{1,0:T(8,128)S(1)} %get-tuple-element.81), channel_id=1, source_target_pairs={{0,3},{1,0},{2,1},{3,2},{4,7},{5,4},{6,5},{7,6},{8,11},{9,8},{10,9... | collective-permute-start | bytes 374792 | tf_op jit(solution)/shard_map/ppermute | solution.py:215
  80.1 14.5 %collective-permute-start.9 = (f32[64,488]{1,0:T(8,128)S(1)}, f32[64,488]{1,0:T(8,128)S(1)}, u32[]{:S(2)}, u32[]{:S(2)}) collective-permute-start(f32[64,488]{1,0:T(8,128)S(1)} %get-tuple-element.80), channel_id=1, source_target_pairs={{0,1},{1,2},{2,3},{3,0},{4,5},{5,6},{6,7},{7,4},{8,9},{9,10},{10,1... | collective-permute-start | bytes 374792 | tf_op jit(solution)/shard_map/ppermute | solution.py:215
  89.6 16.4 %collective-permute-start.12 = (f32[64,488]{1,0:T(8,128)S(1)}, f32[64,488]{1,0:T(8,128)S(1)}, u32[]{:S(2)}, u32[]{:S(2)}) collective-permute-start(f32[64,488]{1,0:T(8,128)S(1)} %get-tuple-element.71), channel_id=1, source_target_pairs={{0,1},{1,2},{2,3},{3,0},{4,5},{5,6},{6,7},{7,4},{8,9},{9,10},{10,1... | collective-permute-start | bytes 374792 | tf_op jit(solution)/shard_map/ppermute | solution.py:215
  89.9 18.9 %collective-permute-start.13 = (f32[64,488]{1,0:T(8,128)S(1)}, f32[64,488]{1,0:T(8,128)S(1)}, u32[]{:S(2)}, u32[]{:S(2)}) collective-permute-start(f32[64,488]{1,0:T(8,128)S(1)} %get-tuple-element.73), channel_id=1, source_target_pairs={{0,2},{1,3},{2,0},{3,1},{4,6},{5,7},{6,4},{7,5},{8,10},{9,11},{10,... | collective-permute-start | bytes 374792 | tf_op jit(solution)/shard_map/ppermute | solution.py:215
  94.4 14.4 %collective-permute-start.14 = (f32[64,488]{1,0:T(8,128)S(1)}, f32[64,488]{1,0:T(8,128)S(1)}, u32[]{:S(2)}, u32[]{:S(2)}) collective-permute-start(f32[64,488]{1,0:T(8,128)S(1)} %get-tuple-element.72), channel_id=1, source_target_pairs={{0,3},{1,0},{2,1},{3,2},{4,7},{5,4},{6,5},{7,6},{8,11},{9,8},{10,9... | collective-permute-start | bytes 374792 | tf_op jit(solution)/shard_map/ppermute | solution.py:215
  104.1 6.3 %collective-permute-start.15 = (f32[64,488]{1,0:T(8,128)S(1)}, f32[64,488]{1,0:T(8,128)S(1)}, u32[]{:S(2)}, u32[]{:S(2)}) collective-permute-start(f32[64,488]{1,0:T(8,128)S(1)} %get-tuple-element.77), channel_id=1, source_target_pairs={{0,1},{1,2},{2,3},{3,0},{4,5},{5,6},{6,7},{7,4},{8,9},{9,10},{10,1... | collective-permute-start | bytes 374792 | tf_op jit(solution)/shard_map/ppermute | solution.py:215
  106.0 6.5 %collective-permute-start.16 = (f32[64,488]{1,0:T(8,128)S(1)}, f32[64,488]{1,0:T(8,128)S(1)}, u32[]{:S(2)}, u32[]{:S(2)}) collective-permute-start(f32[64,488]{1,0:T(8,128)S(1)} %get-tuple-element.79), channel_id=1, source_target_pairs={{0,2},{1,3},{2,0},{3,1},{4,6},{5,7},{6,4},{7,5},{8,10},{9,11},{10,... | collective-permute-start | bytes 374792 | tf_op jit(solution)/shard_map/ppermute | solution.py:215
  106.0 6.6 %collective-permute-start.17 = (f32[64,488]{1,0:T(8,128)S(1)}, f32[64,488]{1,0:T(8,128)S(1)}, u32[]{:S(2)}, u32[]{:S(2)}) collective-permute-start(f32[64,488]{1,0:T(8,128)S(1)} %get-tuple-element.78), channel_id=1, source_target_pairs={{0,3},{1,0},{2,1},{3,2},{4,7},{5,4},{6,5},{7,6},{8,11},{9,8},{10,9... | collective-permute-start | bytes 374792 | tf_op jit(solution)/shard_map/ppermute | solution.py:215

commit v6 on v5

--- a/solution.py
+++ b/solution.py
@@ -97,7 +97,7 @@
     in_specs = [
         pl.BlockSpec((slot.shape[0], tile), lambda g: (0, chunk)),
         pl.BlockSpec((rows, width), lambda g: (row_block, 0)),
-        pl.BlockSpec((classes // 2, width, width), lambda g: (g, 0, 0)),
+        pl.BlockSpec((2, width, width), lambda g: (g, 0, 0)),
     ]
     operands = [slot, buffer, kernels]
     if spread is not None:
@@ -112,7 +112,7 @@
     flops = 2 * classes * tile * width * (rows + width)
     return pl.pallas_call(
         functools.partial(translate_kernel, spread is not None, devices, classes),
-        grid=(2,),
+        grid=(classes // 2,),
         in_specs=in_specs,
         out_specs=pl.BlockSpec((tile, width), lambda g: (0, 0)),
         out_shape=jax.ShapeDtypeStruct((tile, width), jnp.float32),

time: 114 us -> 117 us (1.026)
  Pallas kernels: 50.7 us -> 53.7 us
    pallas_call x6, Pallas kernels: 45.5 us -> 48.5 us  [translate(): pl.pallas_call(functools.partial(translate_kernel, spread is not None, de...]
where the time goes in v6:
time: 117 us
  Pallas kernels  53.7 us (46%)
  starting transfers between devices  35.7 us (31%)
  waiting for transfers between devices  13.2 us (11%)
  local copies, waits for them, and re-layouts  11.7 us (10%)
  other arithmetic  2.08 us (2%)
    pallas_call x6, Pallas kernels, translate(): pl.pallas_call(functools.partial(translate_kernel, spread is not None, de...  48.5 us
    ppermute x12, starting transfers between devices, on_device(): total = total + lax.ppermute(sent, 'off', route)  18.7 us
    ppermute x6, starting transfers between devices, partner(): return lax.ppermute(block, axis, route)  17 us
    ppermute x6, waiting for transfers between devices, partner(): return lax.ppermute(block, axis, route)  9.34 us
    pallas_call x6, Pallas kernels, slot_table(): pl.pallas_call(invert_kernel, out_shape=jax.ShapeDtypeStruct((classes, pa...  5.2 us
    gather x6, local copies, waits for them, and re-layouts, on_device(): outgoing = rows_all[picks]  4.43 us
    ppermute x12, waiting for transfers between devices, on_device(): total = total + lax.ppermute(sent, 'off', route)  3.85 us
    unnamed x18, local copies, waits for them, and re-layouts  3.65 us
  transfers between devices with their start and end apart: 18, of which 8 were waited for; matrix products, arithmetic and copies ran while one was open for 2% of the time, Pallas kernels for 29%

profile of v6, /device:TPU:16, one launch (start us, length us, event | category | flops | bytes accessed | tf_op | source)
XLA Modules:
  0.0 117.1 jit_solution(9137811472565071571)
XLA Ops:
  0.0 0.8 slice_bitcast_fusion
  0.8 0.7 add_bitcast_fusion.2
  1.6 1.5 %copy.242.buf_ref = bf16[1024,488]{1,0:T(8,128)(2,1)S(1)} copy(bf16[1024,488]{0,1:T(8,128)(2,1)} %param.11) | data formatting | bytes 1998848 | tf_op args[0]
  3.5 2.1 %copy-done = bf16[8,488,488]{2,1,0:T(8,128)(2,1)S(1)} copy-done((bf16[8,488,488]{2,1,0:T(8,128)(2,1)S(1)}, bf16[8,488,488]{2,1,0:T(8,128)(2,1)}, u32[]{:S(2)}) %copy-start) | copy-done | bytes 3810328
  5.6 3.7 %shard_map.109 = f32[128,488]{1,0:T(8,128)S(1)} custom-call(s32[16,128]{1,0:T(8,128)S(1)} %fusion.18.slot_ref, bf16[1024,488]{1,0:T(8,128)(2,1)S(1)} %copy.242.buf_ref, bf16[8,488,488]{2,1,0:T(8,128)(2,1)S(1)} %copy-done), custom_call_target="tpu_custom_call" | custom-call | flops 1511129088 | bytes 4809728 | tf_op jit(solution)/shard_map/pallas_call | solution.py:113
  9.3 0.7 gather_fusion
  10.8 0.9 shard_map.110
  11.8 0.7 gather_fusion.1
  12.7 1.4 %collective-permute-start.1 = (bf16[80,488]{1,0:T(8,128)(2,1)S(1)}, bf16[80,488]{1,0:T(8,128)(2,1)S(1)}, u32[]{:S(2)}, u32[]{:S(2)}) collective-permute-start(bf16[80,488]{1,0:T(8,128)(2,1)S(1)} %gather_fusion.1), channel_id=1, source_target_pairs={{0,8},{8,0},{4,12},{12,4},{16,24},{24,16},{20,28},{28,20},{32,40},... | collective-permute-start | bytes 234248 | tf_op jit(solution)/shard_map/ppermute | solution.py:18
  14.1 0.9 shard_map.111
  15.1 2.6 %collective-permute-done.1 = bf16[80,488]{1,0:T(8,128)(2,1)S(1)} collective-permute-done((bf16[80,488]{1,0:T(8,128)(2,1)S(1)}, bf16[80,488]{1,0:T(8,128)(2,1)S(1)}, u32[]{:S(2)}, u32[]{:S(2)}) %collective-permute-start.1) | collective-permute-done | bytes 78112 | tf_op jit(solution)/shard_map/ppermute | solution.py:18
  17.7 0.7 gather_fusion.2
  18.6 2.2 %collective-permute-start.2 = (bf16[80,488]{1,0:T(8,128)(2,1)S(1)}, bf16[80,488]{1,0:T(8,128)(2,1)S(1)}, u32[]{:S(2)}, u32[]{:S(2)}) collective-permute-start(bf16[80,488]{1,0:T(8,128)(2,1)S(1)} %gather_fusion.2), channel_id=1, source_target_pairs={{0,16},{16,0},{4,20},{20,4},{8,24},{24,8},{12,28},{28,12},{32,48},... | collective-permute-start | bytes 234248 | tf_op jit(solution)/shard_map/ppermute | solution.py:18
  20.8 0.9 shard_map.112
  21.7 2.9 %collective-permute-done.2 = bf16[80,488]{1,0:T(8,128)(2,1)S(1)} collective-permute-done((bf16[80,488]{1,0:T(8,128)(2,1)S(1)}, bf16[80,488]{1,0:T(8,128)(2,1)S(1)}, u32[]{:S(2)}, u32[]{:S(2)}) %collective-permute-start.2) | collective-permute-done | bytes 78112 | tf_op jit(solution)/shard_map/ppermute | solution.py:18
  24.6 0.7 gather_fusion.3
  25.5 2.0 %collective-permute-start.3 = (bf16[80,488]{1,0:T(8,128)(2,1)S(1)}, bf16[80,488]{1,0:T(8,128)(2,1)S(1)}, u32[]{:S(2)}, u32[]{:S(2)}) collective-permute-start(bf16[80,488]{1,0:T(8,128)(2,1)S(1)} %gather_fusion.3), channel_id=1, source_target_pairs={{0,32},{32,0},{4,36},{36,4},{8,40},{40,8},{12,44},{44,12},{16,48},... | collective-permute-start | bytes 234248 | tf_op jit(solution)/shard_map/ppermute | solution.py:18
  27.5 0.9 shard_map.113
  28.5 1.5 %collective-permute-done.3 = bf16[80,488]{1,0:T(8,128)(2,1)S(1)} collective-permute-done((bf16[80,488]{1,0:T(8,128)(2,1)S(1)}, bf16[80,488]{1,0:T(8,128)(2,1)S(1)}, u32[]{:S(2)}, u32[]{:S(2)}) %collective-permute-start.3) | collective-permute-done | bytes 78112 | tf_op jit(solution)/shard_map/ppermute | solution.py:18
  30.0 0.7 gather_fusion.4
  30.9 3.4 %collective-permute-start.4 = (bf16[80,488]{1,0:T(8,128)(2,1)S(1)}, bf16[80,488]{1,0:T(8,128)(2,1)S(1)}, u32[]{:S(2)}, u32[]{:S(2)}) collective-permute-start(bf16[80,488]{1,0:T(8,128)(2,1)S(1)} %gather_fusion.4), channel_id=1, source_target_pairs={{0,64},{64,0},{4,68},{68,4},{8,72},{72,8},{12,76},{76,12},{16,80},... | collective-permute-start | bytes 234248 | tf_op jit(solution)/shard_map/ppermute | solution.py:18
  34.3 0.9 shard_map.114
  35.3 1.5 %collective-permute-done.4 = bf16[80,488]{1,0:T(8,128)(2,1)S(1)} collective-permute-done((bf16[80,488]{1,0:T(8,128)(2,1)S(1)}, bf16[80,488]{1,0:T(8,128)(2,1)S(1)}, u32[]{:S(2)}, u32[]{:S(2)}) %collective-permute-start.4) | collective-permute-done | bytes 78112 | tf_op jit(solution)/shard_map/ppermute | solution.py:18
  36.7 0.7 gather_fusion.5
  37.5 8.0 %collective-permute-start.5 = (bf16[80,488]{1,0:T(8,128)(2,1)S(1)}, bf16[80,488]{1,0:T(8,128)(2,1)S(1)}, u32[]{:S(2)}, u32[]{:S(2)}) collective-permute-start(bf16[80,488]{1,0:T(8,128)(2,1)S(1)} %gather_fusion.5), channel_id=1, source_target_pairs={{0,128},{128,0},{4,132},{132,4},{8,136},{136,8},{12,140},{140,12},... | collective-permute-start | bytes 234248 | tf_op jit(solution)/shard_map/ppermute | solution.py:18
  45.5 0.5 shard_map.115
  46.1 0.2 copy.261
  46.3 0.5 copy.262
  47.0 0.9 collective-permute-done.5
  47.9 5.8 %shard_map.116 = f32[128,488]{1,0:T(8,128)S(1)} custom-call(s32[16,128]{1,0:T(8,128)S(1)} %pad.61.slot_ref, bf16[1792,488]{1,0:T(8,128)(2,1)S(1)} %slice_dynamic-update-slice_fusion.6.buf_ref, bf16[10,488,488]{2,1,0:T(8,128)(2,1)} %k_ref.11), custom_call_target="tpu_custom_call" | custom-call | flops 889487360 | bytes 6511872 | tf_op jit(solution)/shard_map/pallas_call | solution.py:113
  53.8 9.7 %shard_map.117 = f32[256,488]{1,0:T(8,128)S(1)} custom-call(s32[16,1024]{1,0:T(8,128)S(1)} %pad.58.slot_ref, bf16[1792,488]{1,0:T(8,128)(2,1)S(1)} %slice_dynamic-update-slice_fusion.6.buf_ref, bf16[10,488,488]{2,1,0:T(8,128)(2,1)} %k_ref.11, bf16[128,488]{1,0:T(8,128)(2,1)S(1)} %get-tuple-element.84.rest_0_, ...), custom_call_target="tpu_custom_call" | custom-call | flops 4737269760 | bytes 6511872 | tf_op jit(solution)/shard_map/pallas_call | solution.py:113
  63.6 1.6 %collective-permute-start.6 = (f32[64,488]{1,0:T(8,128)S(1)}, f32[64,488]{1,0:T(8,128)S(1)}, u32[]{:S(2)}, u32[]{:S(2)}) collective-permute-start(f32[64,488]{1,0:T(8,128)S(1)} %get-tuple-element.74), channel_id=1, source_target_pairs={{0,1},{1,2},{2,3},{3,0},{4,5},{5,6},{6,7},{7,4},{8,9},{9,10},{10,1... | collective-permute-start | bytes 374792 | tf_op jit(solution)/shard_map/ppermute | solution.py:215
  65.1 2.7 %collective-permute-start.7 = (f32[64,488]{1,0:T(8,128)S(1)}, f32[64,488]{1,0:T(8,128)S(1)}, u32[]{:S(2)}, u32[]{:S(2)}) collective-permute-start(f32[64,488]{1,0:T(8,128)S(1)} %get-tuple-element.76), channel_id=1, source_target_pairs={{0,2},{1,3},{2,0},{3,1},{4,6},{5,7},{6,4},{7,5},{8,10},{9,11},{10,... | collective-permute-start | bytes 374792 | tf_op jit(solution)/shard_map/ppermute | solution.py:215
  67.9 1.4 %collective-permute-start.8 = (f32[64,488]{1,0:T(8,128)S(1)}, f32[64,488]{1,0:T(8,128)S(1)}, u32[]{:S(2)}, u32[]{:S(2)}) collective-permute-start(f32[64,488]{1,0:T(8,128)S(1)} %get-tuple-element.75), channel_id=1, source_target_pairs={{0,3},{1,0},{2,1},{3,2},{4,7},{5,4},{6,5},{7,6},{8,11},{9,8},{10,9... | collective-permute-start | bytes 374792 | tf_op jit(solution)/shard_map/ppermute | solution.py:215
  69.3 9.7 %shard_map.118 = f32[256,488]{1,0:T(8,128)S(1)} custom-call(s32[16,1024]{1,0:T(8,128)S(1)} %pad.58.slot_ref, bf16[1792,488]{1,0:T(8,128)(2,1)S(1)} %slice_dynamic-update-slice_fusion.6.buf_ref, bf16[10,488,488]{2,1,0:T(8,128)(2,1)} %k_ref.11, bf16[128,488]{1,0:T(8,128)(2,1)S(1)} %get-tuple-element.84.rest_0_, ...), custom_call_target="tpu_custom_call" | custom-call | flops 4737269760 | bytes 6511872 | tf_op jit(solution)/shard_map/pallas_call | solution.py:113
  79.1 0.6 collective-permute-start.10
  79.7 2.8 %collective-permute-start.11 = (f32[64,488]{1,0:T(8,128)S(1)}, f32[64,488]{1,0:T(8,128)S(1)}, u32[]{:S(2)}, u32[]{:S(2)}) collective-permute-start(f32[64,488]{1,0:T(8,128)S(1)} %get-tuple-element.81), channel_id=1, source_target_pairs={{0,3},{1,0},{2,1},{3,2},{4,7},{5,4},{6,5},{7,6},{8,11},{9,8},{10,9... | collective-permute-start | bytes 374792 | tf_op jit(solution)/shard_map/ppermute | solution.py:215
  82.5 9.7 %shard_map.119 = f32[256,488]{1,0:T(8,128)S(1)} custom-call(s32[16,1024]{1,0:T(8,128)S(1)} %pad.58.slot_ref, bf16[1792,488]{1,0:T(8,128)(2,1)S(1)} %slice_dynamic-update-slice_fusion.6.buf_ref, bf16[10,488,488]{2,1,0:T(8,128)(2,1)} %k_ref.11, bf16[128,488]{1,0:T(8,128)(2,1)S(1)} %get-tuple-element.84.rest_0_, ...), custom_call_target="tpu_custom_call" | custom-call | flops 4737269760 | bytes 6511872 | tf_op jit(solution)/shard_map/pallas_call | solution.py:113
  92.3 0.3 collective-permute-start.12
  92.6 4.5 %collective-permute-start.13 = (f32[64,488]{1,0:T(8,128)S(1)}, f32[64,488]{1,0:T(8,128)S(1)}, u32[]{:S(2)}, u32[]{:S(2)}) collective-permute-start(f32[64,488]{1,0:T(8,128)S(1)} %get-tuple-element.73), channel_id=1, source_target_pairs={{0,2},{1,3},{2,0},{3,1},{4,6},{5,7},{6,4},{7,5},{8,10},{9,11},{10,... | collective-permute-start | bytes 374792 | tf_op jit(solution)/shard_map/ppermute | solution.py:215
  97.1 0.2 collective-permute-start.14
  97.4 9.8 %shard_map.120 = f32[256,488]{1,0:T(8,128)S(1)} custom-call(s32[16,1024]{1,0:T(8,128)S(1)} %pad.58.slot_ref, bf16[1792,488]{1,0:T(8,128)(2,1)S(1)} %slice_dynamic-update-slice_fusion.6.buf_ref, bf16[10,488,488]{2,1,0:T(8,128)(2,1)} %k_ref.11, bf16[128,488]{1,0:T(8,128)(2,1)S(1)} %get-tuple-element.84.rest_0_, ...), custom_call_target="tpu_custom_call" | custom-call | flops 4737269760 | bytes 6511872 | tf_op jit(solution)/shard_map/pallas_call | solution.py:113
  107.2 1.9 %collective-permute-start.15 = (f32[64,488]{1,0:T(8,128)S(1)}, f32[64,488]{1,0:T(8,128)S(1)}, u32[]{:S(2)}, u32[]{:S(2)}) collective-permute-start(f32[64,488]{1,0:T(8,128)S(1)} %get-tuple-element.77), channel_id=1, source_target_pairs={{0,1},{1,2},{2,3},{3,0},{4,5},{5,6},{6,7},{7,4},{8,9},{9,10},{10,1... | collective-permute-start | bytes 374792 | tf_op jit(solution)/shard_map/ppermute | solution.py:215
  109.0 2.8 %collective-permute-start.17 = (f32[64,488]{1,0:T(8,128)S(1)}, f32[64,488]{1,0:T(8,128)S(1)}, u32[]{:S(2)}, u32[]{:S(2)}) collective-permute-start(f32[64,488]{1,0:T(8,128)S(1)} %get-tuple-element.78), channel_id=1, source_target_pairs={{0,3},{1,0},{2,1},{3,2},{4,7},{5,4},{6,5},{7,6},{8,11},{9,8},{10,9... | collective-permute-start | bytes 374792 | tf_op jit(solution)/shard_map/ppermute | solution.py:215
  111.9 1.6 %collective-permute-done.15 = f32[64,488]{1,0:T(8,128)S(1)} collective-permute-done((f32[64,488]{1,0:T(8,128)S(1)}, f32[64,488]{1,0:T(8,128)S(1)}, u32[]{:S(2)}, u32[]{:S(2)}) %collective-permute-start.15) | collective-permute-done | bytes 124960 | tf_op jit(solution)/shard_map/ppermute | solution.py:215
  113.4 2.1 %collective-permute-done.16 = f32[64,488]{1,0:T(8,128)S(1)} collective-permute-done((f32[64,488]{1,0:T(8,128)S(1)}, f32[64,488]{1,0:T(8,128)S(1)}, u32[]{:S(2)}, u32[]{:S(2)}) %collective-permute-start.16) | collective-permute-done | bytes 124960 | tf_op jit(solution)/shard_map/ppermute | solution.py:215
  115.8 0.3 copy.288
  116.1 1.0 copy.264
  (105 shorter events, 2.6 us)
Async XLA Ops:
  0.0 3.1 %copy-start.1 = (s32[1,10,1024]{2,0,1:T(1,128)S(1)}, s32[1,10,1024]{2,0,1:T(1,128)}, u32[]{:S(2)}) copy-start(s32[1,10,1024]{2,0,1:T(1,128)} %param.15) | copy-start | bytes 122884
  0.0 3.2 %copy-start.2 = (s32[1,10,1024]{2,0,1:T(1,128)S(1)}, s32[1,10,1024]{2,0,1:T(1,128)}, u32[]{:S(2)}) copy-start(s32[1,10,1024]{2,0,1:T(1,128)} %param.14) | copy-start | bytes 122884
  0.0 3.2 %copy-start.3 = (s32[1,10]{1,0:T(1,128)S(1)}, s32[1,10]{1,0:T(1,128)}, u32[]{:S(2)}) copy-start(s32[1,10]{1,0:T(1,128)} %param.16) | copy-start | bytes 124
  3.5 2.1 %copy-start = (bf16[8,488,488]{2,1,0:T(8,128)(2,1)S(1)}, bf16[8,488,488]{2,1,0:T(8,128)(2,1)}, u32[]{:S(2)}) copy-start(bf16[8,488,488]{2,1,0:T(8,128)(2,1)} %rest_2_.7) | copy-start | bytes 11430916
  5.6 5.0 %copy-start.4 = (s32[1,10,128]{2,0,1:T(1,128)S(1)}, s32[1,10,128]{2,0,1:T(1,128)}, u32[]{:S(2)}) copy-start(s32[1,10,128]{2,0,1:T(1,128)} %param.18) | copy-start | bytes 15364
  5.6 5.0 %copy-start.6 = (s32[1,10]{1,0:T(1,128)S(1)}, s32[1,10]{1,0:T(1,128)}, u32[]{:S(2)}) copy-start(s32[1,10]{1,0:T(1,128)} %param.19) | copy-start | bytes 124
  5.6 5.1 %copy-start.5 = (s32[1,10,128]{2,0,1:T(1,128)S(1)}, s32[1,10,128]{2,0,1:T(1,128)}, u32[]{:S(2)}) copy-start(s32[1,10,128]{2,0,1:T(1,128)} %param.17) | copy-start | bytes 15364
  10.1 1.7 %collective-permute-start = (bf16[80,488]{1,0:T(8,128)(2,1)S(1)}, bf16[80,488]{1,0:T(8,128)(2,1)S(1)}, u32[]{:S(2)}, u32[]{:S(2)}) collective-permute-start(bf16[80,488]{1,0:T(8,128)(2,1)S(1)} %gather_fusion), channel_id=1, source_target_pairs={{0,4},{4,0},{8,12},{12,8},{16,20},{20,16},{24,28},{28,24},{32,36},... | collective-permute-start | bytes 234248 | tf_op jit(solution)/shard_map/ppermute | solution.py:18
  12.7 4.9 %collective-permute-start.1 = (bf16[80,488]{1,0:T(8,128)(2,1)S(1)}, bf16[80,488]{1,0:T(8,128)(2,1)S(1)}, u32[]{:S(2)}, u32[]{:S(2)}) collective-permute-start(bf16[80,488]{1,0:T(8,128)(2,1)S(1)} %gather_fusion.1), channel_id=1, source_target_pairs={{0,8},{8,0},{4,12},{12,4},{16,24},{24,16},{20,28},{28,20},{32,40},... | collective-permute-start | bytes 234248 | tf_op jit(solution)/shard_map/ppermute | solution.py:18
  18.6 6.0 %collective-permute-start.2 = (bf16[80,488]{1,0:T(8,128)(2,1)S(1)}, bf16[80,488]{1,0:T(8,128)(2,1)S(1)}, u32[]{:S(2)}, u32[]{:S(2)}) collective-permute-start(bf16[80,488]{1,0:T(8,128)(2,1)S(1)} %gather_fusion.2), channel_id=1, source_target_pairs={{0,16},{16,0},{4,20},{20,4},{8,24},{24,8},{12,28},{28,12},{32,48},... | collective-permute-start | bytes 234248 | tf_op jit(solution)/shard_map/ppermute | solution.py:18
  25.5 4.5 %collective-permute-start.3 = (bf16[80,488]{1,0:T(8,128)(2,1)S(1)}, bf16[80,488]{1,0:T(8,128)(2,1)S(1)}, u32[]{:S(2)}, u32[]{:S(2)}) collective-permute-start(bf16[80,488]{1,0:T(8,128)(2,1)S(1)} %gather_fusion.3), channel_id=1, source_target_pairs={{0,32},{32,0},{4,36},{36,4},{8,40},{40,8},{12,44},{44,12},{16,48},... | collective-permute-start | bytes 234248 | tf_op jit(solution)/shard_map/ppermute | solution.py:18
  30.9 5.8 %collective-permute-start.4 = (bf16[80,488]{1,0:T(8,128)(2,1)S(1)}, bf16[80,488]{1,0:T(8,128)(2,1)S(1)}, u32[]{:S(2)}, u32[]{:S(2)}) collective-permute-start(bf16[80,488]{1,0:T(8,128)(2,1)S(1)} %gather_fusion.4), channel_id=1, source_target_pairs={{0,64},{64,0},{4,68},{68,4},{8,72},{72,8},{12,76},{76,12},{16,80},... | collective-permute-start | bytes 234248 | tf_op jit(solution)/shard_map/ppermute | solution.py:18
  37.5 10.4 %collective-permute-start.5 = (bf16[80,488]{1,0:T(8,128)(2,1)S(1)}, bf16[80,488]{1,0:T(8,128)(2,1)S(1)}, u32[]{:S(2)}, u32[]{:S(2)}) collective-permute-start(bf16[80,488]{1,0:T(8,128)(2,1)S(1)} %gather_fusion.5), channel_id=1, source_target_pairs={{0,128},{128,0},{4,132},{132,4},{8,136},{136,8},{12,140},{140,12},... | collective-permute-start | bytes 234248 | tf_op jit(solution)/shard_map/ppermute | solution.py:18
  63.6 18.9 %collective-permute-start.6 = (f32[64,488]{1,0:T(8,128)S(1)}, f32[64,488]{1,0:T(8,128)S(1)}, u32[]{:S(2)}, u32[]{:S(2)}) collective-permute-start(f32[64,488]{1,0:T(8,128)S(1)} %get-tuple-element.74), channel_id=1, source_target_pairs={{0,1},{1,2},{2,3},{3,0},{4,5},{5,6},{6,7},{7,4},{8,9},{9,10},{10,1... | collective-permute-start | bytes 374792 | tf_op jit(solution)/shard_map/ppermute | solution.py:215
  65.1 17.3 %collective-permute-start.7 = (f32[64,488]{1,0:T(8,128)S(1)}, f32[64,488]{1,0:T(8,128)S(1)}, u32[]{:S(2)}, u32[]{:S(2)}) collective-permute-start(f32[64,488]{1,0:T(8,128)S(1)} %get-tuple-element.76), channel_id=1, source_target_pairs={{0,2},{1,3},{2,0},{3,1},{4,6},{5,7},{6,4},{7,5},{8,10},{9,11},{10,... | collective-permute-start | bytes 374792 | tf_op jit(solution)/shard_map/ppermute | solution.py:215
  67.9 14.6 %collective-permute-start.8 = (f32[64,488]{1,0:T(8,128)S(1)}, f32[64,488]{1,0:T(8,128)S(1)}, u32[]{:S(2)}, u32[]{:S(2)}) collective-permute-start(f32[64,488]{1,0:T(8,128)S(1)} %get-tuple-element.75), channel_id=1, source_target_pairs={{0,3},{1,0},{2,1},{3,2},{4,7},{5,4},{6,5},{7,6},{8,11},{9,8},{10,9... | collective-permute-start | bytes 374792 | tf_op jit(solution)/shard_map/ppermute | solution.py:215
  79.1 18.0 %collective-permute-start.10 = (f32[64,488]{1,0:T(8,128)S(1)}, f32[64,488]{1,0:T(8,128)S(1)}, u32[]{:S(2)}, u32[]{:S(2)}) collective-permute-start(f32[64,488]{1,0:T(8,128)S(1)} %get-tuple-element.82), channel_id=1, source_target_pairs={{0,2},{1,3},{2,0},{3,1},{4,6},{5,7},{6,4},{7,5},{8,10},{9,11},{10,... | collective-permute-start | bytes 374792 | tf_op jit(solution)/shard_map/ppermute | solution.py:215
  79.7 17.6 %collective-permute-start.11 = (f32[64,488]{1,0:T(8,128)S(1)}, f32[64,488]{1,0:T(8,128)S(1)}, u32[]{:S(2)}, u32[]{:S(2)}) collective-permute-start(f32[64,488]{1,0:T(8,128)S(1)} %get-tuple-element.81), channel_id=1, source_target_pairs={{0,3},{1,0},{2,1},{3,2},{4,7},{5,4},{6,5},{7,6},{8,11},{9,8},{10,9... | collective-permute-start | bytes 374792 | tf_op jit(solution)/shard_map/ppermute | solution.py:215
  82.4 14.9 %collective-permute-start.9 = (f32[64,488]{1,0:T(8,128)S(1)}, f32[64,488]{1,0:T(8,128)S(1)}, u32[]{:S(2)}, u32[]{:S(2)}) collective-permute-start(f32[64,488]{1,0:T(8,128)S(1)} %get-tuple-element.80), channel_id=1, source_target_pairs={{0,1},{1,2},{2,3},{3,0},{4,5},{5,6},{6,7},{7,4},{8,9},{9,10},{10,1... | collective-permute-start | bytes 374792 | tf_op jit(solution)/shard_map/ppermute | solution.py:215
  92.3 16.7 %collective-permute-start.12 = (f32[64,488]{1,0:T(8,128)S(1)}, f32[64,488]{1,0:T(8,128)S(1)}, u32[]{:S(2)}, u32[]{:S(2)}) collective-permute-start(f32[64,488]{1,0:T(8,128)S(1)} %get-tuple-element.71), channel_id=1, source_target_pairs={{0,1},{1,2},{2,3},{3,0},{4,5},{5,6},{6,7},{7,4},{8,9},{9,10},{10,1... | collective-permute-start | bytes 374792 | tf_op jit(solution)/shard_map/ppermute | solution.py:215
  92.6 19.2 %collective-permute-start.13 = (f32[64,488]{1,0:T(8,128)S(1)}, f32[64,488]{1,0:T(8,128)S(1)}, u32[]{:S(2)}, u32[]{:S(2)}) collective-permute-start(f32[64,488]{1,0:T(8,128)S(1)} %get-tuple-element.73), channel_id=1, source_target_pairs={{0,2},{1,3},{2,0},{3,1},{4,6},{5,7},{6,4},{7,5},{8,10},{9,11},{10,... | collective-permute-start | bytes 374792 | tf_op jit(solution)/shard_map/ppermute | solution.py:215
  97.1 14.7 %collective-permute-start.14 = (f32[64,488]{1,0:T(8,128)S(1)}, f32[64,488]{1,0:T(8,128)S(1)}, u32[]{:S(2)}, u32[]{:S(2)}) collective-permute-start(f32[64,488]{1,0:T(8,128)S(1)} %get-tuple-element.72), channel_id=1, source_target_pairs={{0,3},{1,0},{2,1},{3,2},{4,7},{5,4},{6,5},{7,6},{8,11},{9,8},{10,9... | collective-permute-start | bytes 374792 | tf_op jit(solution)/shard_map/ppermute | solution.py:215
  107.2 6.3 %collective-permute-start.15 = (f32[64,488]{1,0:T(8,128)S(1)}, f32[64,488]{1,0:T(8,128)S(1)}, u32[]{:S(2)}, u32[]{:S(2)}) collective-permute-start(f32[64,488]{1,0:T(8,128)S(1)} %get-tuple-element.77), channel_id=1, source_target_pairs={{0,1},{1,2},{2,3},{3,0},{4,5},{5,6},{6,7},{7,4},{8,9},{9,10},{10,1... | collective-permute-start | bytes 374792 | tf_op jit(solution)/shard_map/ppermute | solution.py:215
  109.0 6.5 %collective-permute-start.16 = (f32[64,488]{1,0:T(8,128)S(1)}, f32[64,488]{1,0:T(8,128)S(1)}, u32[]{:S(2)}, u32[]{:S(2)}) collective-permute-start(f32[64,488]{1,0:T(8,128)S(1)} %get-tuple-element.79), channel_id=1, source_target_pairs={{0,2},{1,3},{2,0},{3,1},{4,6},{5,7},{6,4},{7,5},{8,10},{9,11},{10,... | collective-permute-start | bytes 374792 | tf_op jit(solution)/shard_map/ppermute | solution.py:215
  109.0 6.6 %collective-permute-start.17 = (f32[64,488]{1,0:T(8,128)S(1)}, f32[64,488]{1,0:T(8,128)S(1)}, u32[]{:S(2)}, u32[]{:S(2)}) collective-permute-start(f32[64,488]{1,0:T(8,128)S(1)} %get-tuple-element.78), channel_id=1, source_target_pairs={{0,3},{1,0},{2,1},{3,2},{4,7},{5,4},{6,5},{7,6},{8,11},{9,8},{10,9... | collective-permute-start | bytes 374792 | tf_op jit(solution)/shard_map/ppermute | solution.py:215

commit v7 on v5

--- a/solution.py
+++ b/solution.py
@@ -124,6 +124,93 @@
     )(*operands)
 
 
+def first_kernel(devices, classes, slot_ref, buf_ref, k_ref, cslot_ref, cbuf_ref, t_ref,
+                 out_ref, high_ref, low_ref, column_ref, ccolumn_ref, cacc_ref):
+    step = pl.program_id(0)
+    per_step = k_ref.shape[0]
+
+    @pl.when(step == 0)
+    def _():
+        out_ref[...] = jnp.zeros(out_ref.shape, out_ref.dtype)
+        cacc_ref[...] = jnp.zeros(cacc_ref.shape, cacc_ref.dtype)
+        columns = jnp.transpose(slot_ref[...])
+        ccolumns = jnp.transpose(cslot_ref[...])
+        for c in range(classes):
+            column_ref[c] = columns[:, c:c + 1]
+            ccolumn_ref[c] = ccolumns[:, c:c + 1]
+
+    def one_class(c, carry):
+        k = k_ref[c]
+        spots = lax.broadcasted_iota(jnp.int32, (out_ref.shape[0], buf_ref.shape[0]), 1)
+        hot = (column_ref[step * per_step + c] == spots).astype(buf_ref.dtype)
+        picked = jnp.dot(hot, buf_ref[...], preferred_element_type=jnp.float32)
+        out_ref[...] += jnp.dot(picked.astype(k.dtype), k, preferred_element_type=jnp.float32)
+        cspots = lax.broadcasted_iota(jnp.int32, (cacc_ref.shape[0], cbuf_ref.shape[0]), 1)
+        chot = (ccolumn_ref[step * per_step + c] == cspots).astype(cbuf_ref.dtype)
+        cpicked = jnp.dot(chot, cbuf_ref[...], preferred_element_type=jnp.float32)
+        cacc_ref[...] += jnp.dot(cpicked.astype(k.dtype), k, preferred_element_type=jnp.float32)
+        return carry
+
+    lax.fori_loop(0, per_step, one_class, 0, unroll=True)
+
+    @pl.when(step == pl.num_programs(0) - 1)
+    def _():
+        local = 0.5 * cacc_ref[...]
+        high = local.astype(high_ref.dtype)
+        low = (local - high.astype(jnp.float32)).astype(low_ref.dtype)
+        high_ref[...] = high
+        low_ref[...] = low
+        nt = (((1,), (1,)), ((), ()))
+        octants = t_ref.shape[0]
+        span = high.shape[0] // devices
+        for h in range(octants):
+            term = lax.dot_general(
+                high, t_ref[h], nt, preferred_element_type=jnp.float32
+            ) + lax.dot_general(low, t_ref[h], nt, preferred_element_type=jnp.float32)
+            for d in range(devices):
+                at = (d * octants + h) * span
+                out_ref[at:at + span, :] += term[d * span:(d + 1) * span]
+
+
+def first_chunk(slot, rows_all, leaf_rows, kernels, coarse_slot, coarse_rows, transfer, tile, devices):
+    classes = kernels.shape[0]
+    width = rows_all.shape[1]
+    parents = coarse_slot.shape[1]
+    octants = tile // parents
+    return pl.pallas_call(
+        functools.partial(first_kernel, devices, classes),
+        grid=(2,),
+        in_specs=[
+            pl.BlockSpec((slot.shape[0], tile), lambda g: (0, 0)),
+            pl.BlockSpec((leaf_rows, width), lambda g: (0, 0)),
+            pl.BlockSpec((classes // 2, width, width), lambda g: (g, 0, 0)),
+            pl.BlockSpec(coarse_slot.shape, lambda g: (0, 0)),
+            pl.BlockSpec(coarse_rows.shape, lambda g: (0, 0)),
+            pl.BlockSpec((octants, width, width), lambda g: (0, 0, 0)),
+        ],
+        out_specs=[
+            pl.BlockSpec((tile, width), lambda g: (0, 0)),
+            pl.BlockSpec((parents, width), lambda g: (0, 0)),
+            pl.BlockSpec((parents, width), lambda g: (0, 0)),
+        ],
+        out_shape=[
+            jax.ShapeDtypeStruct((tile, width), jnp.float32),
+            jax.ShapeDtypeStruct((parents, width), jnp.bfloat16),
+            jax.ShapeDtypeStruct((parents, width), jnp.bfloat16),
+        ],
+        scratch_shapes=[
+            pltpu.VMEM((slot.shape[0], tile, 1), jnp.int32),
+            pltpu.VMEM((coarse_slot.shape[0], parents, 1), jnp.int32),
+            pltpu.VMEM((parents, width), jnp.float32),
+        ],
+        compiler_params=pltpu.CompilerParams(vmem_limit_bytes=48 * 1024 * 1024),
+        cost_estimate=pl.CostEstimate(
+            flops=2 * classes * tile * width * (leaf_rows + width), bytes_accessed=2 * kernels.size,
+            transcendentals=0,
+        ),
+    )(slot, rows_all, kernels, coarse_slot, coarse_rows, transfer)
+
+
 def on_device(
     multipoles,
     kernels,
@@ -190,11 +277,6 @@
     leaf_slot = leaf_slot.reshape(classes, devices, span, chunks, per)
     leaf_slot = leaf_slot.transpose(0, 3, 1, 4, 2).reshape(classes, boxes)
     leaf_slot = jnp.pad(leaf_slot, ((0, 16 - classes), (0, 0)), constant_values=leaf_rows)
-    coarse_local = 0.5 * translate(
-        coarse_slot, rows_all, kernels, 0, parents, rows=coarse_rows, row_block=leaf_region // coarse_rows
-    )
-    coarse_high = coarse_local.astype(jnp.bfloat16)
-    coarse_low = (coarse_local - coarse_high.astype(jnp.float32)).astype(jnp.bfloat16)
     tile = boxes // chunks
     block = tile // devices
     me = lax.axis_index("off")
@@ -203,10 +285,16 @@
         slot_in = leaf_slot
         if chunk >= 2:
             slot_in, _ = lax.optimization_barrier((leaf_slot, mine[chunk - 2]))
-        partial_sum = translate(
-            slot_in, rows_all, kernels, chunk, tile, (coarse_high, coarse_low, transfer), devices,
-            rows=leaf_rows,
-        )
+        if chunk == 0:
+            partial_sum, coarse_high, coarse_low = first_chunk(
+                slot_in, rows_all, leaf_rows, kernels, coarse_slot, rows_all[leaf_region:],
+                transfer, tile, devices,
+            )
+        else:
+            partial_sum = translate(
+                slot_in, rows_all, kernels, chunk, tile, (coarse_high, coarse_low, transfer),
+                devices, rows=leaf_rows,
+            )
         total = lax.dynamic_slice_in_dim(partial_sum, me * block, block, 0)
         for shift in range(1, devices):
             theirs = lax.rem(me + shift, devices)

time: 114 us -> 112 us (0.982)
  Pallas kernels: 50.7 us -> 48.9 us
    pallas_call x6 -> x4, Pallas kernels: 45.5 us -> 31.5 us  [translate(): pl.pallas_call(functools.partial(translate_kernel, spread is not None, de...]
    pallas_call x0 -> x1, Pallas kernels: none -> 12.2 us  [first_chunk(): pl.pallas_call(functools.partial(first_kernel, devices, classes), grid=(2...]
  transfers between devices with their start and end apart: 18 -> 18, of which waited for: 8 -> 8; matrix products, arithmetic and copies ran while one was open for 2% -> 2% of each run, Pallas kernels for 29% -> 30%
where the time goes in v7:
time: 112 us
  Pallas kernels  48.9 us (44%)
  starting transfers between devices  35.7 us (32%)
  waiting for transfers between devices  13.2 us (12%)
  local copies, waits for them, and re-layouts  11.7 us (10%)
  other arithmetic  2.05 us (2%)
    pallas_call x4, Pallas kernels, translate(): pl.pallas_call(functools.partial(translate_kernel, spread is not None, de...  31.5 us
    ppermute x12, starting transfers between devices, on_device(): total = total + lax.ppermute(sent, 'off', route)  18.7 us
    ppermute x6, starting transfers between devices, partner(): return lax.ppermute(block, axis, route)  17 us
    pallas_call x1, Pallas kernels, first_chunk(): pl.pallas_call(functools.partial(first_kernel, devices, classes), grid=(2...  12.2 us
    ppermute x6, waiting for transfers between devices, partner(): return lax.ppermute(block, axis, route)  9.37 us
    pallas_call x6, Pallas kernels, slot_table(): pl.pallas_call(invert_kernel, out_shape=jax.ShapeDtypeStruct((classes, pa...  5.2 us
    gather x6, local copies, waits for them, and re-layouts, on_device(): outgoing = rows_all[picks]  4.43 us
    ppermute x12, waiting for transfers between devices, on_device(): total = total + lax.ppermute(sent, 'off', route)  3.83 us
  transfers between devices with their start and end apart: 18, of which 8 were waited for; matrix products, arithmetic and copies ran while one was open for 2% of the time, Pallas kernels for 30%

profile of v7, /device:TPU:16, one launch (start us, length us, event | category | flops | bytes accessed | tf_op | source)
XLA Modules:
  0.0 112.2 jit_solution(14577852681318692033)
XLA Ops:
  0.0 0.8 slice_bitcast_fusion
  0.8 0.7 add_bitcast_fusion.2
  1.6 1.5 %copy.242.buf_ref = bf16[1024,488]{1,0:T(8,128)(2,1)S(1)} copy(bf16[1024,488]{0,1:T(8,128)(2,1)} %param.11) | data formatting | bytes 1998848 | tf_op args[0]
  3.5 2.1 %copy-done = bf16[8,488,488]{2,1,0:T(8,128)(2,1)S(1)} copy-done((bf16[8,488,488]{2,1,0:T(8,128)(2,1)S(1)}, bf16[8,488,488]{2,1,0:T(8,128)(2,1)}, u32[]{:S(2)}) %copy-start) | copy-done | bytes 3810328
  5.6 3.2 %shard_map.109 = f32[128,488]{1,0:T(8,128)S(1)} custom-call(s32[16,128]{1,0:T(8,128)S(1)} %fusion.18.slot_ref, bf16[1024,488]{1,0:T(8,128)(2,1)S(1)} %copy.242.buf_ref, bf16[8,488,488]{2,1,0:T(8,128)(2,1)S(1)} %copy-done), custom_call_target="tpu_custom_call" | custom-call | flops 1511129088 | bytes 4809728 | tf_op jit(solution)/shard_map/pallas_call | solution.py:113
  8.9 0.7 gather_fusion
  10.3 0.9 shard_map.110
  11.4 0.7 gather_fusion.1
  12.3 1.4 %collective-permute-start.1 = (bf16[80,488]{1,0:T(8,128)(2,1)S(1)}, bf16[80,488]{1,0:T(8,128)(2,1)S(1)}, u32[]{:S(2)}, u32[]{:S(2)}) collective-permute-start(bf16[80,488]{1,0:T(8,128)(2,1)S(1)} %gather_fusion.1), channel_id=1, source_target_pairs={{0,8},{8,0},{4,12},{12,4},{16,24},{24,16},{20,28},{28,20},{32,40},... | collective-permute-start | bytes 234248 | tf_op jit(solution)/shard_map/ppermute | solution.py:18
  13.7 0.9 shard_map.111
  14.6 2.6 %collective-permute-done.1 = bf16[80,488]{1,0:T(8,128)(2,1)S(1)} collective-permute-done((bf16[80,488]{1,0:T(8,128)(2,1)S(1)}, bf16[80,488]{1,0:T(8,128)(2,1)S(1)}, u32[]{:S(2)}, u32[]{:S(2)}) %collective-permute-start.1) | collective-permute-done | bytes 78112 | tf_op jit(solution)/shard_map/ppermute | solution.py:18
  17.2 0.7 gather_fusion.2
  18.1 2.2 %collective-permute-start.2 = (bf16[80,488]{1,0:T(8,128)(2,1)S(1)}, bf16[80,488]{1,0:T(8,128)(2,1)S(1)}, u32[]{:S(2)}, u32[]{:S(2)}) collective-permute-start(bf16[80,488]{1,0:T(8,128)(2,1)S(1)} %gather_fusion.2), channel_id=1, source_target_pairs={{0,16},{16,0},{4,20},{20,4},{8,24},{24,8},{12,28},{28,12},{32,48},... | collective-permute-start | bytes 234248 | tf_op jit(solution)/shard_map/ppermute | solution.py:18
  20.3 0.9 shard_map.112
  21.2 2.9 %collective-permute-done.2 = bf16[80,488]{1,0:T(8,128)(2,1)S(1)} collective-permute-done((bf16[80,488]{1,0:T(8,128)(2,1)S(1)}, bf16[80,488]{1,0:T(8,128)(2,1)S(1)}, u32[]{:S(2)}, u32[]{:S(2)}) %collective-permute-start.2) | collective-permute-done | bytes 78112 | tf_op jit(solution)/shard_map/ppermute | solution.py:18
  24.1 0.7 gather_fusion.3
  25.0 2.0 %collective-permute-start.3 = (bf16[80,488]{1,0:T(8,128)(2,1)S(1)}, bf16[80,488]{1,0:T(8,128)(2,1)S(1)}, u32[]{:S(2)}, u32[]{:S(2)}) collective-permute-start(bf16[80,488]{1,0:T(8,128)(2,1)S(1)} %gather_fusion.3), channel_id=1, source_target_pairs={{0,32},{32,0},{4,36},{36,4},{8,40},{40,8},{12,44},{44,12},{16,48},... | collective-permute-start | bytes 234248 | tf_op jit(solution)/shard_map/ppermute | solution.py:18
  27.1 0.9 shard_map.113
  28.0 1.6 %collective-permute-done.3 = bf16[80,488]{1,0:T(8,128)(2,1)S(1)} collective-permute-done((bf16[80,488]{1,0:T(8,128)(2,1)S(1)}, bf16[80,488]{1,0:T(8,128)(2,1)S(1)}, u32[]{:S(2)}, u32[]{:S(2)}) %collective-permute-start.3) | collective-permute-done | bytes 78112 | tf_op jit(solution)/shard_map/ppermute | solution.py:18
  29.6 0.7 gather_fusion.4
  30.5 3.4 %collective-permute-start.4 = (bf16[80,488]{1,0:T(8,128)(2,1)S(1)}, bf16[80,488]{1,0:T(8,128)(2,1)S(1)}, u32[]{:S(2)}, u32[]{:S(2)}) collective-permute-start(bf16[80,488]{1,0:T(8,128)(2,1)S(1)} %gather_fusion.4), channel_id=1, source_target_pairs={{0,64},{64,0},{4,68},{68,4},{8,72},{72,8},{12,76},{76,12},{16,80},... | collective-permute-start | bytes 234248 | tf_op jit(solution)/shard_map/ppermute | solution.py:18
  33.9 0.9 shard_map.114
  34.8 1.5 %collective-permute-done.4 = bf16[80,488]{1,0:T(8,128)(2,1)S(1)} collective-permute-done((bf16[80,488]{1,0:T(8,128)(2,1)S(1)}, bf16[80,488]{1,0:T(8,128)(2,1)S(1)}, u32[]{:S(2)}, u32[]{:S(2)}) %collective-permute-start.4) | collective-permute-done | bytes 78112 | tf_op jit(solution)/shard_map/ppermute | solution.py:18
  36.3 0.7 gather_fusion.5
  37.0 8.0 %collective-permute-start.5 = (bf16[80,488]{1,0:T(8,128)(2,1)S(1)}, bf16[80,488]{1,0:T(8,128)(2,1)S(1)}, u32[]{:S(2)}, u32[]{:S(2)}) collective-permute-start(bf16[80,488]{1,0:T(8,128)(2,1)S(1)} %gather_fusion.5), channel_id=1, source_target_pairs={{0,128},{128,0},{4,132},{132,4},{8,136},{136,8},{12,140},{140,12},... | collective-permute-start | bytes 234248 | tf_op jit(solution)/shard_map/ppermute | solution.py:18
  45.0 0.5 shard_map.115
  45.6 0.2 copy.261
  45.8 0.5 copy.262
  46.3 0.2 reshape.647
  46.5 0.9 collective-permute-done.5
  47.4 12.2 %shard_map.116 = (f32[256,488]{1,0:T(8,128)S(1)}, bf16[128,488]{1,0:T(8,128)(2,1)S(1)}, bf16[128,488]{1,0:T(8,128)(2,1)S(1)}) custom-call(s32[16,1024]{1,0:T(8,128)S(1)} %pad.58.slot_ref, bf16[1792,488]{1,0:T(8,128)(2,1)S(1)} %slice_dynamic-update-slice_fusion.6.buf_ref, bf16[10,488,488]{2,1,0:T(8,128)(2,1)} %k_ref.9, s32[16,128]{1,0:T(8,128)S(1)} %pad.61.cslot_ref, ...), custom_call_target="tpu_custom_call" | custom-call | flops 4737269760 | bytes 4762880 | tf_op jit(solution)/shard_map/pallas_call | solution.py:180
  59.7 1.6 %collective-permute-start.6 = (f32[64,488]{1,0:T(8,128)S(1)}, f32[64,488]{1,0:T(8,128)S(1)}, u32[]{:S(2)}, u32[]{:S(2)}) collective-permute-start(f32[64,488]{1,0:T(8,128)S(1)} %get-tuple-element.80), channel_id=1, source_target_pairs={{0,1},{1,2},{2,3},{3,0},{4,5},{5,6},{6,7},{7,4},{8,9},{9,10},{10,1... | collective-permute-start | bytes 374792 | tf_op jit(solution)/shard_map/ppermute | solution.py:303
  61.2 2.7 %collective-permute-start.7 = (f32[64,488]{1,0:T(8,128)S(1)}, f32[64,488]{1,0:T(8,128)S(1)}, u32[]{:S(2)}, u32[]{:S(2)}) collective-permute-start(f32[64,488]{1,0:T(8,128)S(1)} %get-tuple-element.82), channel_id=1, source_target_pairs={{0,2},{1,3},{2,0},{3,1},{4,6},{5,7},{6,4},{7,5},{8,10},{9,11},{10,... | collective-permute-start | bytes 374792 | tf_op jit(solution)/shard_map/ppermute | solution.py:303
  64.0 1.4 %collective-permute-start.8 = (f32[64,488]{1,0:T(8,128)S(1)}, f32[64,488]{1,0:T(8,128)S(1)}, u32[]{:S(2)}, u32[]{:S(2)}) collective-permute-start(f32[64,488]{1,0:T(8,128)S(1)} %get-tuple-element.81), channel_id=1, source_target_pairs={{0,3},{1,0},{2,1},{3,2},{4,7},{5,4},{6,5},{7,6},{8,11},{9,8},{10,9... | collective-permute-start | bytes 374792 | tf_op jit(solution)/shard_map/ppermute | solution.py:303
  65.4 9.4 %shard_map.117 = f32[256,488]{1,0:T(8,128)S(1)} custom-call(s32[16,1024]{1,0:T(8,128)S(1)} %pad.58.slot_ref, bf16[1792,488]{1,0:T(8,128)(2,1)S(1)} %slice_dynamic-update-slice_fusion.6.buf_ref, bf16[10,488,488]{2,1,0:T(8,128)(2,1)} %k_ref.9, bf16[128,488]{1,0:T(8,128)(2,1)S(1)} %get-tuple-element.71.rest_0_, bf16[128,488]{1,0:T(8,128)(2,1)S(1)} %get-tuple-element.72.rest_1_, ...), custom_call_target="tpu_custom_call" | custom-call | flops 4737269760 | bytes 6511872 | tf_op jit(solution)/shard_map/pallas_call | solution.py:113
  74.9 0.6 collective-permute-start.10
  75.5 2.8 %collective-permute-start.11 = (f32[64,488]{1,0:T(8,128)S(1)}, f32[64,488]{1,0:T(8,128)S(1)}, u32[]{:S(2)}, u32[]{:S(2)}) collective-permute-start(f32[64,488]{1,0:T(8,128)S(1)} %get-tuple-element.87), channel_id=1, source_target_pairs={{0,3},{1,0},{2,1},{3,2},{4,7},{5,4},{6,5},{7,6},{8,11},{9,8},{10,9... | collective-permute-start | bytes 374792 | tf_op jit(solution)/shard_map/ppermute | solution.py:303
  78.3 9.4 %shard_map.118 = f32[256,488]{1,0:T(8,128)S(1)} custom-call(s32[16,1024]{1,0:T(8,128)S(1)} %pad.58.slot_ref, bf16[1792,488]{1,0:T(8,128)(2,1)S(1)} %slice_dynamic-update-slice_fusion.6.buf_ref, bf16[10,488,488]{2,1,0:T(8,128)(2,1)} %k_ref.9, bf16[128,488]{1,0:T(8,128)(2,1)S(1)} %get-tuple-element.71.rest_0_, bf16[128,488]{1,0:T(8,128)(2,1)S(1)} %get-tuple-element.72.rest_1_, ...), custom_call_target="tpu_custom_call" | custom-call | flops 4737269760 | bytes 6511872 | tf_op jit(solution)/shard_map/pallas_call | solution.py:113
  87.8 0.3 collective-permute-start.12
  88.1 4.5 %collective-permute-start.13 = (f32[64,488]{1,0:T(8,128)S(1)}, f32[64,488]{1,0:T(8,128)S(1)}, u32[]{:S(2)}, u32[]{:S(2)}) collective-permute-start(f32[64,488]{1,0:T(8,128)S(1)} %get-tuple-element.79), channel_id=1, source_target_pairs={{0,2},{1,3},{2,0},{3,1},{4,6},{5,7},{6,4},{7,5},{8,10},{9,11},{10,... | collective-permute-start | bytes 374792 | tf_op jit(solution)/shard_map/ppermute | solution.py:303
  92.6 0.2 collective-permute-start.14
  92.8 9.4 %shard_map.119 = f32[256,488]{1,0:T(8,128)S(1)} custom-call(s32[16,1024]{1,0:T(8,128)S(1)} %pad.58.slot_ref, bf16[1792,488]{1,0:T(8,128)(2,1)S(1)} %slice_dynamic-update-slice_fusion.6.buf_ref, bf16[10,488,488]{2,1,0:T(8,128)(2,1)} %k_ref.9, bf16[128,488]{1,0:T(8,128)(2,1)S(1)} %get-tuple-element.71.rest_0_, bf16[128,488]{1,0:T(8,128)(2,1)S(1)} %get-tuple-element.72.rest_1_, ...), custom_call_target="tpu_custom_call" | custom-call | flops 4737269760 | bytes 6511872 | tf_op jit(solution)/shard_map/pallas_call | solution.py:113
  102.3 1.9 %collective-permute-start.15 = (f32[64,488]{1,0:T(8,128)S(1)}, f32[64,488]{1,0:T(8,128)S(1)}, u32[]{:S(2)}, u32[]{:S(2)}) collective-permute-start(f32[64,488]{1,0:T(8,128)S(1)} %get-tuple-element.83), channel_id=1, source_target_pairs={{0,1},{1,2},{2,3},{3,0},{4,5},{5,6},{6,7},{7,4},{8,9},{9,10},{10,1... | collective-permute-start | bytes 374792 | tf_op jit(solution)/shard_map/ppermute | solution.py:303
  104.2 2.8 %collective-permute-start.17 = (f32[64,488]{1,0:T(8,128)S(1)}, f32[64,488]{1,0:T(8,128)S(1)}, u32[]{:S(2)}, u32[]{:S(2)}) collective-permute-start(f32[64,488]{1,0:T(8,128)S(1)} %get-tuple-element.84), channel_id=1, source_target_pairs={{0,3},{1,0},{2,1},{3,2},{4,7},{5,4},{6,5},{7,6},{8,11},{9,8},{10,9... | collective-permute-start | bytes 374792 | tf_op jit(solution)/shard_map/ppermute | solution.py:303
  107.0 1.5 %collective-permute-done.15 = f32[64,488]{1,0:T(8,128)S(1)} collective-permute-done((f32[64,488]{1,0:T(8,128)S(1)}, f32[64,488]{1,0:T(8,128)S(1)}, u32[]{:S(2)}, u32[]{:S(2)}) %collective-permute-start.15) | collective-permute-done | bytes 124960 | tf_op jit(solution)/shard_map/ppermute | solution.py:303
  108.6 2.1 %collective-permute-done.16 = f32[64,488]{1,0:T(8,128)S(1)} collective-permute-done((f32[64,488]{1,0:T(8,128)S(1)}, f32[64,488]{1,0:T(8,128)S(1)}, u32[]{:S(2)}, u32[]{:S(2)}) %collective-permute-start.16) | collective-permute-done | bytes 124960 | tf_op jit(solution)/shard_map/ppermute | solution.py:303
  110.9 0.3 copy.288
  111.3 1.0 copy.264
  (104 shorter events, 2.3 us)
Async XLA Ops:
  0.0 3.1 %copy-start.1 = (s32[1,10,1024]{2,0,1:T(1,128)S(1)}, s32[1,10,1024]{2,0,1:T(1,128)}, u32[]{:S(2)}) copy-start(s32[1,10,1024]{2,0,1:T(1,128)} %param.15) | copy-start | bytes 122884
  0.0 3.2 %copy-start.2 = (s32[1,10,1024]{2,0,1:T(1,128)S(1)}, s32[1,10,1024]{2,0,1:T(1,128)}, u32[]{:S(2)}) copy-start(s32[1,10,1024]{2,0,1:T(1,128)} %param.14) | copy-start | bytes 122884
  0.0 3.2 %copy-start.3 = (s32[1,10]{1,0:T(1,128)S(1)}, s32[1,10]{1,0:T(1,128)}, u32[]{:S(2)}) copy-start(s32[1,10]{1,0:T(1,128)} %param.16) | copy-start | bytes 124
  3.5 2.1 %copy-start = (bf16[8,488,488]{2,1,0:T(8,128)(2,1)S(1)}, bf16[8,488,488]{2,1,0:T(8,128)(2,1)}, u32[]{:S(2)}) copy-start(bf16[8,488,488]{2,1,0:T(8,128)(2,1)} %rest_2_.5) | copy-start | bytes 11430916
  5.6 4.5 %copy-start.4 = (s32[1,10,128]{2,0,1:T(1,128)S(1)}, s32[1,10,128]{2,0,1:T(1,128)}, u32[]{:S(2)}) copy-start(s32[1,10,128]{2,0,1:T(1,128)} %param.18) | copy-start | bytes 15364
  5.6 4.5 %copy-start.6 = (s32[1,10]{1,0:T(1,128)S(1)}, s32[1,10]{1,0:T(1,128)}, u32[]{:S(2)}) copy-start(s32[1,10]{1,0:T(1,128)} %param.19) | copy-start | bytes 124
  5.6 4.6 %copy-start.5 = (s32[1,10,128]{2,0,1:T(1,128)S(1)}, s32[1,10,128]{2,0,1:T(1,128)}, u32[]{:S(2)}) copy-start(s32[1,10,128]{2,0,1:T(1,128)} %param.17) | copy-start | bytes 15364
  9.6 1.7 %collective-permute-start = (bf16[80,488]{1,0:T(8,128)(2,1)S(1)}, bf16[80,488]{1,0:T(8,128)(2,1)S(1)}, u32[]{:S(2)}, u32[]{:S(2)}) collective-permute-start(bf16[80,488]{1,0:T(8,128)(2,1)S(1)} %gather_fusion), channel_id=1, source_target_pairs={{0,4},{4,0},{8,12},{12,8},{16,20},{20,16},{24,28},{28,24},{32,36},... | collective-permute-start | bytes 234248 | tf_op jit(solution)/shard_map/ppermute | solution.py:18
  12.3 4.9 %collective-permute-start.1 = (bf16[80,488]{1,0:T(8,128)(2,1)S(1)}, bf16[80,488]{1,0:T(8,128)(2,1)S(1)}, u32[]{:S(2)}, u32[]{:S(2)}) collective-permute-start(bf16[80,488]{1,0:T(8,128)(2,1)S(1)} %gather_fusion.1), channel_id=1, source_target_pairs={{0,8},{8,0},{4,12},{12,4},{16,24},{24,16},{20,28},{28,20},{32,40},... | collective-permute-start | bytes 234248 | tf_op jit(solution)/shard_map/ppermute | solution.py:18
  18.1 6.0 %collective-permute-start.2 = (bf16[80,488]{1,0:T(8,128)(2,1)S(1)}, bf16[80,488]{1,0:T(8,128)(2,1)S(1)}, u32[]{:S(2)}, u32[]{:S(2)}) collective-permute-start(bf16[80,488]{1,0:T(8,128)(2,1)S(1)} %gather_fusion.2), channel_id=1, source_target_pairs={{0,16},{16,0},{4,20},{20,4},{8,24},{24,8},{12,28},{28,12},{32,48},... | collective-permute-start | bytes 234248 | tf_op jit(solution)/shard_map/ppermute | solution.py:18
  25.0 4.5 %collective-permute-start.3 = (bf16[80,488]{1,0:T(8,128)(2,1)S(1)}, bf16[80,488]{1,0:T(8,128)(2,1)S(1)}, u32[]{:S(2)}, u32[]{:S(2)}) collective-permute-start(bf16[80,488]{1,0:T(8,128)(2,1)S(1)} %gather_fusion.3), channel_id=1, source_target_pairs={{0,32},{32,0},{4,36},{36,4},{8,40},{40,8},{12,44},{44,12},{16,48},... | collective-permute-start | bytes 234248 | tf_op jit(solution)/shard_map/ppermute | solution.py:18
  30.5 5.8 %collective-permute-start.4 = (bf16[80,488]{1,0:T(8,128)(2,1)S(1)}, bf16[80,488]{1,0:T(8,128)(2,1)S(1)}, u32[]{:S(2)}, u32[]{:S(2)}) collective-permute-start(bf16[80,488]{1,0:T(8,128)(2,1)S(1)} %gather_fusion.4), channel_id=1, source_target_pairs={{0,64},{64,0},{4,68},{68,4},{8,72},{72,8},{12,76},{76,12},{16,80},... | collective-permute-start | bytes 234248 | tf_op jit(solution)/shard_map/ppermute | solution.py:18
  37.0 10.4 %collective-permute-start.5 = (bf16[80,488]{1,0:T(8,128)(2,1)S(1)}, bf16[80,488]{1,0:T(8,128)(2,1)S(1)}, u32[]{:S(2)}, u32[]{:S(2)}) collective-permute-start(bf16[80,488]{1,0:T(8,128)(2,1)S(1)} %gather_fusion.5), channel_id=1, source_target_pairs={{0,128},{128,0},{4,132},{132,4},{8,136},{136,8},{12,140},{140,12},... | collective-permute-start | bytes 234248 | tf_op jit(solution)/shard_map/ppermute | solution.py:18
  59.7 18.6 %collective-permute-start.6 = (f32[64,488]{1,0:T(8,128)S(1)}, f32[64,488]{1,0:T(8,128)S(1)}, u32[]{:S(2)}, u32[]{:S(2)}) collective-permute-start(f32[64,488]{1,0:T(8,128)S(1)} %get-tuple-element.80), channel_id=1, source_target_pairs={{0,1},{1,2},{2,3},{3,0},{4,5},{5,6},{6,7},{7,4},{8,9},{9,10},{10,1... | collective-permute-start | bytes 374792 | tf_op jit(solution)/shard_map/ppermute | solution.py:303
  61.2 17.0 %collective-permute-start.7 = (f32[64,488]{1,0:T(8,128)S(1)}, f32[64,488]{1,0:T(8,128)S(1)}, u32[]{:S(2)}, u32[]{:S(2)}) collective-permute-start(f32[64,488]{1,0:T(8,128)S(1)} %get-tuple-element.82), channel_id=1, source_target_pairs={{0,2},{1,3},{2,0},{3,1},{4,6},{5,7},{6,4},{7,5},{8,10},{9,11},{10,... | collective-permute-start | bytes 374792 | tf_op jit(solution)/shard_map/ppermute | solution.py:303
  64.0 14.3 %collective-permute-start.8 = (f32[64,488]{1,0:T(8,128)S(1)}, f32[64,488]{1,0:T(8,128)S(1)}, u32[]{:S(2)}, u32[]{:S(2)}) collective-permute-start(f32[64,488]{1,0:T(8,128)S(1)} %get-tuple-element.81), channel_id=1, source_target_pairs={{0,3},{1,0},{2,1},{3,2},{4,7},{5,4},{6,5},{7,6},{8,11},{9,8},{10,9... | collective-permute-start | bytes 374792 | tf_op jit(solution)/shard_map/ppermute | solution.py:303
  74.9 17.7 %collective-permute-start.10 = (f32[64,488]{1,0:T(8,128)S(1)}, f32[64,488]{1,0:T(8,128)S(1)}, u32[]{:S(2)}, u32[]{:S(2)}) collective-permute-start(f32[64,488]{1,0:T(8,128)S(1)} %get-tuple-element.88), channel_id=1, source_target_pairs={{0,2},{1,3},{2,0},{3,1},{4,6},{5,7},{6,4},{7,5},{8,10},{9,11},{10,... | collective-permute-start | bytes 374792 | tf_op jit(solution)/shard_map/ppermute | solution.py:303
  75.5 17.3 %collective-permute-start.11 = (f32[64,488]{1,0:T(8,128)S(1)}, f32[64,488]{1,0:T(8,128)S(1)}, u32[]{:S(2)}, u32[]{:S(2)}) collective-permute-start(f32[64,488]{1,0:T(8,128)S(1)} %get-tuple-element.87), channel_id=1, source_target_pairs={{0,3},{1,0},{2,1},{3,2},{4,7},{5,4},{6,5},{7,6},{8,11},{9,8},{10,9... | collective-permute-start | bytes 374792 | tf_op jit(solution)/shard_map/ppermute | solution.py:303
  78.2 14.5 %collective-permute-start.9 = (f32[64,488]{1,0:T(8,128)S(1)}, f32[64,488]{1,0:T(8,128)S(1)}, u32[]{:S(2)}, u32[]{:S(2)}) collective-permute-start(f32[64,488]{1,0:T(8,128)S(1)} %get-tuple-element.86), channel_id=1, source_target_pairs={{0,1},{1,2},{2,3},{3,0},{4,5},{5,6},{6,7},{7,4},{8,9},{9,10},{10,1... | collective-permute-start | bytes 374792 | tf_op jit(solution)/shard_map/ppermute | solution.py:303
  87.8 16.4 %collective-permute-start.12 = (f32[64,488]{1,0:T(8,128)S(1)}, f32[64,488]{1,0:T(8,128)S(1)}, u32[]{:S(2)}, u32[]{:S(2)}) collective-permute-start(f32[64,488]{1,0:T(8,128)S(1)} %get-tuple-element.77), channel_id=1, source_target_pairs={{0,1},{1,2},{2,3},{3,0},{4,5},{5,6},{6,7},{7,4},{8,9},{9,10},{10,1... | collective-permute-start | bytes 374792 | tf_op jit(solution)/shard_map/ppermute | solution.py:303
  88.1 18.9 %collective-permute-start.13 = (f32[64,488]{1,0:T(8,128)S(1)}, f32[64,488]{1,0:T(8,128)S(1)}, u32[]{:S(2)}, u32[]{:S(2)}) collective-permute-start(f32[64,488]{1,0:T(8,128)S(1)} %get-tuple-element.79), channel_id=1, source_target_pairs={{0,2},{1,3},{2,0},{3,1},{4,6},{5,7},{6,4},{7,5},{8,10},{9,11},{10,... | collective-permute-start | bytes 374792 | tf_op jit(solution)/shard_map/ppermute | solution.py:303
  92.6 14.4 %collective-permute-start.14 = (f32[64,488]{1,0:T(8,128)S(1)}, f32[64,488]{1,0:T(8,128)S(1)}, u32[]{:S(2)}, u32[]{:S(2)}) collective-permute-start(f32[64,488]{1,0:T(8,128)S(1)} %get-tuple-element.78), channel_id=1, source_target_pairs={{0,3},{1,0},{2,1},{3,2},{4,7},{5,4},{6,5},{7,6},{8,11},{9,8},{10,9... | collective-permute-start | bytes 374792 | tf_op jit(solution)/shard_map/ppermute | solution.py:303
  102.3 6.3 %collective-permute-start.15 = (f32[64,488]{1,0:T(8,128)S(1)}, f32[64,488]{1,0:T(8,128)S(1)}, u32[]{:S(2)}, u32[]{:S(2)}) collective-permute-start(f32[64,488]{1,0:T(8,128)S(1)} %get-tuple-element.83), channel_id=1, source_target_pairs={{0,1},{1,2},{2,3},{3,0},{4,5},{5,6},{6,7},{7,4},{8,9},{9,10},{10,1... | collective-permute-start | bytes 374792 | tf_op jit(solution)/shard_map/ppermute | solution.py:303
  104.2 6.5 %collective-permute-start.16 = (f32[64,488]{1,0:T(8,128)S(1)}, f32[64,488]{1,0:T(8,128)S(1)}, u32[]{:S(2)}, u32[]{:S(2)}) collective-permute-start(f32[64,488]{1,0:T(8,128)S(1)} %get-tuple-element.85), channel_id=1, source_target_pairs={{0,2},{1,3},{2,0},{3,1},{4,6},{5,7},{6,4},{7,5},{8,10},{9,11},{10,... | collective-permute-start | bytes 374792 | tf_op jit(solution)/shard_map/ppermute | solution.py:303
  104.2 6.6 %collective-permute-start.17 = (f32[64,488]{1,0:T(8,128)S(1)}, f32[64,488]{1,0:T(8,128)S(1)}, u32[]{:S(2)}, u32[]{:S(2)}) collective-permute-start(f32[64,488]{1,0:T(8,128)S(1)} %get-tuple-element.84), channel_id=1, source_target_pairs={{0,3},{1,0},{2,1},{3,2},{4,7},{5,4},{6,5},{7,6},{8,11},{9,8},{10,9... | collective-permute-start | bytes 374792 | tf_op jit(solution)/shard_map/ppermute | solution.py:303

commit v8 on v7

--- a/solution.py
+++ b/solution.py
@@ -238,7 +238,6 @@
         jnp.int32, (16, parents), 0
     )
     child = jnp.where(child % 8 == lax.broadcasted_iota(jnp.int32, (16, parents), 0), child, boxes)
-    parent = translate(child, multipoles, transfer, 0, parents).astype(jnp.bfloat16)
 
     coarse_slot = slot_table(coarse_target[0], coarse_source[0], coarse_count[0], coarse_rows)
     chunks = 4
@@ -250,6 +249,7 @@
     leaf_region = -(-leaf_rows // coarse_rows) * coarse_rows
     rows_all = jnp.zeros((leaf_region + coarse_rows, width), multipoles.dtype)
     rows_all = lax.dynamic_update_slice(rows_all, multipoles, (0, 0))
+    parent = translate(child, rows_all, transfer, 0, parents, rows=boxes).astype(jnp.bfloat16)
     rows_all = lax.dynamic_update_slice(rows_all, parent, (leaf_region, 0))
     group = -(-classes // (rounds - 1))
     groups = [(low, min(low + group, classes)) for low in range(0, classes, group)]

time: 112 us -> 112 us (level)
  no operation moved by 1% of the time
where the time goes in v8:
time: 112 us
  Pallas kernels  48.9 us (44%)
  starting transfers between devices  35.7 us (32%)
  waiting for transfers between devices  13.2 us (12%)
  local copies, waits for them, and re-layouts  11.7 us (10%)
  other arithmetic  2.05 us (2%)
    pallas_call x4, Pallas kernels, translate(): pl.pallas_call(functools.partial(translate_kernel, spread is not None, de...  31.5 us
    ppermute x12, starting transfers between devices, on_device(): total = total + lax.ppermute(sent, 'off', route)  18.8 us
    ppermute x6, starting transfers between devices, partner(): return lax.ppermute(block, axis, route)  17 us
    pallas_call x1, Pallas kernels, first_chunk(): pl.pallas_call(functools.partial(first_kernel, devices, classes), grid=(2...  12.2 us
    ppermute x6, waiting for transfers between devices, partner(): return lax.ppermute(block, axis, route)  9.37 us
    pallas_call x6, Pallas kernels, slot_table(): pl.pallas_call(invert_kernel, out_shape=jax.ShapeDtypeStruct((classes, pa...  5.2 us
    gather x6, local copies, waits for them, and re-layouts, on_device(): outgoing = rows_all[picks]  4.43 us
    ppermute x12, waiting for transfers between devices, on_device(): total = total + lax.ppermute(sent, 'off', route)  3.79 us
  transfers between devices with their start and end apart: 18, of which 8 were waited for; matrix products, arithmetic and copies ran while one was open for 2% of the time, Pallas kernels for 30%

profile of v8, /device:TPU:16, one launch (start us, length us, event | category | flops | bytes accessed | tf_op | source)
XLA Modules:
  0.0 112.2 jit_solution(17083949611983047800)
XLA Ops:
  0.0 0.7 slice_bitcast_fusion
  0.7 0.7 add_bitcast_fusion.2
  1.6 1.5 %copy.232 = bf16[1024,488]{1,0:T(8,128)(2,1)S(1)} copy(bf16[1024,488]{0,1:T(8,128)(2,1)} %param.11) | data formatting | bytes 1998848 | tf_op args[0]
  3.3 2.1 %copy-done = bf16[8,488,488]{2,1,0:T(8,128)(2,1)S(1)} copy-done((bf16[8,488,488]{2,1,0:T(8,128)(2,1)S(1)}, bf16[8,488,488]{2,1,0:T(8,128)(2,1)}, u32[]{:S(2)}) %copy-start) | copy-done | bytes 3810328
  5.4 3.2 %shard_map.109 = f32[128,488]{1,0:T(8,128)S(1)} custom-call(s32[16,128]{1,0:T(8,128)S(1)} %fusion.18.slot_ref, bf16[1792,488]{1,0:T(8,128)(2,1)S(1)} %dynamic_update_slice.42.buf_ref, bf16[8,488,488]{2,1,0:T(8,128)(2,1)S(1)} %copy-done), custom_call_target="tpu_custom_call" | custom-call | flops 1511129088 | bytes 5559296 | tf_op jit(solution)/shard_map/pallas_call | solution.py:113
  8.9 0.7 gather_fusion
  10.3 0.9 shard_map.110
  11.4 0.7 gather_fusion.1
  12.3 1.4 %collective-permute-start.1 = (bf16[80,488]{1,0:T(8,128)(2,1)S(1)}, bf16[80,488]{1,0:T(8,128)(2,1)S(1)}, u32[]{:S(2)}, u32[]{:S(2)}) collective-permute-start(bf16[80,488]{1,0:T(8,128)(2,1)S(1)} %gather_fusion.1), channel_id=1, source_target_pairs={{0,8},{8,0},{4,12},{12,4},{16,24},{24,16},{20,28},{28,20},{32,40},... | collective-permute-start | bytes 234248 | tf_op jit(solution)/shard_map/ppermute | solution.py:18
  13.7 0.9 shard_map.111
  14.6 2.6 %collective-permute-done.1 = bf16[80,488]{1,0:T(8,128)(2,1)S(1)} collective-permute-done((bf16[80,488]{1,0:T(8,128)(2,1)S(1)}, bf16[80,488]{1,0:T(8,128)(2,1)S(1)}, u32[]{:S(2)}, u32[]{:S(2)}) %collective-permute-start.1) | collective-permute-done | bytes 78112 | tf_op jit(solution)/shard_map/ppermute | solution.py:18
  17.2 0.7 gather_fusion.2
  18.1 2.2 %collective-permute-start.2 = (bf16[80,488]{1,0:T(8,128)(2,1)S(1)}, bf16[80,488]{1,0:T(8,128)(2,1)S(1)}, u32[]{:S(2)}, u32[]{:S(2)}) collective-permute-start(bf16[80,488]{1,0:T(8,128)(2,1)S(1)} %gather_fusion.2), channel_id=1, source_target_pairs={{0,16},{16,0},{4,20},{20,4},{8,24},{24,8},{12,28},{28,12},{32,48},... | collective-permute-start | bytes 234248 | tf_op jit(solution)/shard_map/ppermute | solution.py:18
  20.3 0.9 shard_map.112
  21.2 2.9 %collective-permute-done.2 = bf16[80,488]{1,0:T(8,128)(2,1)S(1)} collective-permute-done((bf16[80,488]{1,0:T(8,128)(2,1)S(1)}, bf16[80,488]{1,0:T(8,128)(2,1)S(1)}, u32[]{:S(2)}, u32[]{:S(2)}) %collective-permute-start.2) | collective-permute-done | bytes 78112 | tf_op jit(solution)/shard_map/ppermute | solution.py:18
  24.1 0.7 gather_fusion.3
  25.0 2.0 %collective-permute-start.3 = (bf16[80,488]{1,0:T(8,128)(2,1)S(1)}, bf16[80,488]{1,0:T(8,128)(2,1)S(1)}, u32[]{:S(2)}, u32[]{:S(2)}) collective-permute-start(bf16[80,488]{1,0:T(8,128)(2,1)S(1)} %gather_fusion.3), channel_id=1, source_target_pairs={{0,32},{32,0},{4,36},{36,4},{8,40},{40,8},{12,44},{44,12},{16,48},... | collective-permute-start | bytes 234248 | tf_op jit(solution)/shard_map/ppermute | solution.py:18
  27.1 0.9 shard_map.113
  28.0 1.6 %collective-permute-done.3 = bf16[80,488]{1,0:T(8,128)(2,1)S(1)} collective-permute-done((bf16[80,488]{1,0:T(8,128)(2,1)S(1)}, bf16[80,488]{1,0:T(8,128)(2,1)S(1)}, u32[]{:S(2)}, u32[]{:S(2)}) %collective-permute-start.3) | collective-permute-done | bytes 78112 | tf_op jit(solution)/shard_map/ppermute | solution.py:18
  29.6 0.7 gather_fusion.4
  30.5 3.4 %collective-permute-start.4 = (bf16[80,488]{1,0:T(8,128)(2,1)S(1)}, bf16[80,488]{1,0:T(8,128)(2,1)S(1)}, u32[]{:S(2)}, u32[]{:S(2)}) collective-permute-start(bf16[80,488]{1,0:T(8,128)(2,1)S(1)} %gather_fusion.4), channel_id=1, source_target_pairs={{0,64},{64,0},{4,68},{68,4},{8,72},{72,8},{12,76},{76,12},{16,80},... | collective-permute-start | bytes 234248 | tf_op jit(solution)/shard_map/ppermute | solution.py:18
  33.9 0.9 shard_map.114
  34.8 1.5 %collective-permute-done.4 = bf16[80,488]{1,0:T(8,128)(2,1)S(1)} collective-permute-done((bf16[80,488]{1,0:T(8,128)(2,1)S(1)}, bf16[80,488]{1,0:T(8,128)(2,1)S(1)}, u32[]{:S(2)}, u32[]{:S(2)}) %collective-permute-start.4) | collective-permute-done | bytes 78112 | tf_op jit(solution)/shard_map/ppermute | solution.py:18
  36.3 0.7 gather_fusion.5
  37.0 8.0 %collective-permute-start.5 = (bf16[80,488]{1,0:T(8,128)(2,1)S(1)}, bf16[80,488]{1,0:T(8,128)(2,1)S(1)}, u32[]{:S(2)}, u32[]{:S(2)}) collective-permute-start(bf16[80,488]{1,0:T(8,128)(2,1)S(1)} %gather_fusion.5), channel_id=1, source_target_pairs={{0,128},{128,0},{4,132},{132,4},{8,136},{136,8},{12,140},{140,12},... | collective-permute-start | bytes 234248 | tf_op jit(solution)/shard_map/ppermute | solution.py:18
  45.0 0.5 shard_map.115
  45.6 0.2 copy.250
  45.8 0.5 copy.251
  46.3 0.2 reshape.647
  46.5 0.9 collective-permute-done.5
  47.4 12.2 %shard_map.116 = (f32[256,488]{1,0:T(8,128)S(1)}, bf16[128,488]{1,0:T(8,128)(2,1)S(1)}, bf16[128,488]{1,0:T(8,128)(2,1)S(1)}) custom-call(s32[16,1024]{1,0:T(8,128)S(1)} %pad.58.slot_ref, bf16[1792,488]{1,0:T(8,128)(2,1)S(1)} %slice_dynamic-update-slice_fusion.6.buf_ref, bf16[10,488,488]{2,1,0:T(8,128)(2,1)} %k_ref.9, s32[16,128]{1,0:T(8,128)S(1)} %pad.61.cslot_ref, ...), custom_call_target="tpu_custom_call" | custom-call | flops 4737269760 | bytes 4762880 | tf_op jit(solution)/shard_map/pallas_call | solution.py:180
  59.7 1.6 %collective-permute-start.6 = (f32[64,488]{1,0:T(8,128)S(1)}, f32[64,488]{1,0:T(8,128)S(1)}, u32[]{:S(2)}, u32[]{:S(2)}) collective-permute-start(f32[64,488]{1,0:T(8,128)S(1)} %get-tuple-element.80), channel_id=1, source_target_pairs={{0,1},{1,2},{2,3},{3,0},{4,5},{5,6},{6,7},{7,4},{8,9},{9,10},{10,1... | collective-permute-start | bytes 374792 | tf_op jit(solution)/shard_map/ppermute | solution.py:303
  61.2 2.8 %collective-permute-start.7 = (f32[64,488]{1,0:T(8,128)S(1)}, f32[64,488]{1,0:T(8,128)S(1)}, u32[]{:S(2)}, u32[]{:S(2)}) collective-permute-start(f32[64,488]{1,0:T(8,128)S(1)} %get-tuple-element.82), channel_id=1, source_target_pairs={{0,2},{1,3},{2,0},{3,1},{4,6},{5,7},{6,4},{7,5},{8,10},{9,11},{10,... | collective-permute-start | bytes 374792 | tf_op jit(solution)/shard_map/ppermute | solution.py:303
  64.0 1.4 %collective-permute-start.8 = (f32[64,488]{1,0:T(8,128)S(1)}, f32[64,488]{1,0:T(8,128)S(1)}, u32[]{:S(2)}, u32[]{:S(2)}) collective-permute-start(f32[64,488]{1,0:T(8,128)S(1)} %get-tuple-element.81), channel_id=1, source_target_pairs={{0,3},{1,0},{2,1},{3,2},{4,7},{5,4},{6,5},{7,6},{8,11},{9,8},{10,9... | collective-permute-start | bytes 374792 | tf_op jit(solution)/shard_map/ppermute | solution.py:303
  65.4 9.4 %shard_map.117 = f32[256,488]{1,0:T(8,128)S(1)} custom-call(s32[16,1024]{1,0:T(8,128)S(1)} %pad.58.slot_ref, bf16[1792,488]{1,0:T(8,128)(2,1)S(1)} %slice_dynamic-update-slice_fusion.6.buf_ref, bf16[10,488,488]{2,1,0:T(8,128)(2,1)} %k_ref.9, bf16[128,488]{1,0:T(8,128)(2,1)S(1)} %get-tuple-element.71.rest_0_, bf16[128,488]{1,0:T(8,128)(2,1)S(1)} %get-tuple-element.72.rest_1_, ...), custom_call_target="tpu_custom_call" | custom-call | flops 4737269760 | bytes 6511872 | tf_op jit(solution)/shard_map/pallas_call | solution.py:113
  74.9 0.6 collective-permute-start.10
  75.5 2.8 %collective-permute-start.11 = (f32[64,488]{1,0:T(8,128)S(1)}, f32[64,488]{1,0:T(8,128)S(1)}, u32[]{:S(2)}, u32[]{:S(2)}) collective-permute-start(f32[64,488]{1,0:T(8,128)S(1)} %get-tuple-element.87), channel_id=1, source_target_pairs={{0,3},{1,0},{2,1},{3,2},{4,7},{5,4},{6,5},{7,6},{8,11},{9,8},{10,9... | collective-permute-start | bytes 374792 | tf_op jit(solution)/shard_map/ppermute | solution.py:303
  78.3 9.4 %shard_map.118 = f32[256,488]{1,0:T(8,128)S(1)} custom-call(s32[16,1024]{1,0:T(8,128)S(1)} %pad.58.slot_ref, bf16[1792,488]{1,0:T(8,128)(2,1)S(1)} %slice_dynamic-update-slice_fusion.6.buf_ref, bf16[10,488,488]{2,1,0:T(8,128)(2,1)} %k_ref.9, bf16[128,488]{1,0:T(8,128)(2,1)S(1)} %get-tuple-element.71.rest_0_, bf16[128,488]{1,0:T(8,128)(2,1)S(1)} %get-tuple-element.72.rest_1_, ...), custom_call_target="tpu_custom_call" | custom-call | flops 4737269760 | bytes 6511872 | tf_op jit(solution)/shard_map/pallas_call | solution.py:113
  87.8 0.2 collective-permute-start.12
  88.1 4.5 %collective-permute-start.13 = (f32[64,488]{1,0:T(8,128)S(1)}, f32[64,488]{1,0:T(8,128)S(1)}, u32[]{:S(2)}, u32[]{:S(2)}) collective-permute-start(f32[64,488]{1,0:T(8,128)S(1)} %get-tuple-element.79), channel_id=1, source_target_pairs={{0,2},{1,3},{2,0},{3,1},{4,6},{5,7},{6,4},{7,5},{8,10},{9,11},{10,... | collective-permute-start | bytes 374792 | tf_op jit(solution)/shard_map/ppermute | solution.py:303
  92.6 0.2 collective-permute-start.14
  92.8 9.4 %shard_map.119 = f32[256,488]{1,0:T(8,128)S(1)} custom-call(s32[16,1024]{1,0:T(8,128)S(1)} %pad.58.slot_ref, bf16[1792,488]{1,0:T(8,128)(2,1)S(1)} %slice_dynamic-update-slice_fusion.6.buf_ref, bf16[10,488,488]{2,1,0:T(8,128)(2,1)} %k_ref.9, bf16[128,488]{1,0:T(8,128)(2,1)S(1)} %get-tuple-element.71.rest_0_, bf16[128,488]{1,0:T(8,128)(2,1)S(1)} %get-tuple-element.72.rest_1_, ...), custom_call_target="tpu_custom_call" | custom-call | flops 4737269760 | bytes 6511872 | tf_op jit(solution)/shard_map/pallas_call | solution.py:113
  102.3 1.9 %collective-permute-start.15 = (f32[64,488]{1,0:T(8,128)S(1)}, f32[64,488]{1,0:T(8,128)S(1)}, u32[]{:S(2)}, u32[]{:S(2)}) collective-permute-start(f32[64,488]{1,0:T(8,128)S(1)} %get-tuple-element.83), channel_id=1, source_target_pairs={{0,1},{1,2},{2,3},{3,0},{4,5},{5,6},{6,7},{7,4},{8,9},{9,10},{10,1... | collective-permute-start | bytes 374792 | tf_op jit(solution)/shard_map/ppermute | solution.py:303
  104.2 2.8 %collective-permute-start.17 = (f32[64,488]{1,0:T(8,128)S(1)}, f32[64,488]{1,0:T(8,128)S(1)}, u32[]{:S(2)}, u32[]{:S(2)}) collective-permute-start(f32[64,488]{1,0:T(8,128)S(1)} %get-tuple-element.84), channel_id=1, source_target_pairs={{0,3},{1,0},{2,1},{3,2},{4,7},{5,4},{6,5},{7,6},{8,11},{9,8},{10,9... | collective-permute-start | bytes 374792 | tf_op jit(solution)/shard_map/ppermute | solution.py:303
  107.1 1.5 %collective-permute-done.15 = f32[64,488]{1,0:T(8,128)S(1)} collective-permute-done((f32[64,488]{1,0:T(8,128)S(1)}, f32[64,488]{1,0:T(8,128)S(1)}, u32[]{:S(2)}, u32[]{:S(2)}) %collective-permute-start.15) | collective-permute-done | bytes 124960 | tf_op jit(solution)/shard_map/ppermute | solution.py:303
  108.6 2.1 %collective-permute-done.16 = f32[64,488]{1,0:T(8,128)S(1)} collective-permute-done((f32[64,488]{1,0:T(8,128)S(1)}, f32[64,488]{1,0:T(8,128)S(1)}, u32[]{:S(2)}, u32[]{:S(2)}) %collective-permute-start.16) | collective-permute-done | bytes 124960 | tf_op jit(solution)/shard_map/ppermute | solution.py:303
  110.9 0.3 copy.277
  111.2 1.0 copy.253
  (104 shorter events, 2.3 us)
Async XLA Ops:
  3.3 2.1 %copy-start = (bf16[8,488,488]{2,1,0:T(8,128)(2,1)S(1)}, bf16[8,488,488]{2,1,0:T(8,128)(2,1)}, u32[]{:S(2)}) copy-start(bf16[8,488,488]{2,1,0:T(8,128)(2,1)} %rest_2_.5) | copy-start | bytes 11430916
  5.4 3.3 %copy-start.1 = (s32[1,10,1024]{2,0,1:T(1,128)S(1)}, s32[1,10,1024]{2,0,1:T(1,128)}, u32[]{:S(2)}) copy-start(s32[1,10,1024]{2,0,1:T(1,128)} %param.15) | copy-start | bytes 122884
  5.4 3.3 %copy-start.2 = (s32[1,10,1024]{2,0,1:T(1,128)S(1)}, s32[1,10,1024]{2,0,1:T(1,128)}, u32[]{:S(2)}) copy-start(s32[1,10,1024]{2,0,1:T(1,128)} %param.14) | copy-start | bytes 122884
  5.4 3.4 %copy-start.3 = (s32[1,10]{1,0:T(1,128)S(1)}, s32[1,10]{1,0:T(1,128)}, u32[]{:S(2)}) copy-start(s32[1,10]{1,0:T(1,128)} %param.16) | copy-start | bytes 124
  5.4 4.7 %copy-start.4 = (s32[1,10,128]{2,0,1:T(1,128)S(1)}, s32[1,10,128]{2,0,1:T(1,128)}, u32[]{:S(2)}) copy-start(s32[1,10,128]{2,0,1:T(1,128)} %param.18) | copy-start | bytes 15364
  5.4 4.7 %copy-start.6 = (s32[1,10]{1,0:T(1,128)S(1)}, s32[1,10]{1,0:T(1,128)}, u32[]{:S(2)}) copy-start(s32[1,10]{1,0:T(1,128)} %param.19) | copy-start | bytes 124
  5.4 4.8 %copy-start.5 = (s32[1,10,128]{2,0,1:T(1,128)S(1)}, s32[1,10,128]{2,0,1:T(1,128)}, u32[]{:S(2)}) copy-start(s32[1,10,128]{2,0,1:T(1,128)} %param.17) | copy-start | bytes 15364
  9.6 1.7 %collective-permute-start = (bf16[80,488]{1,0:T(8,128)(2,1)S(1)}, bf16[80,488]{1,0:T(8,128)(2,1)S(1)}, u32[]{:S(2)}, u32[]{:S(2)}) collective-permute-start(bf16[80,488]{1,0:T(8,128)(2,1)S(1)} %gather_fusion), channel_id=1, source_target_pairs={{0,4},{4,0},{8,12},{12,8},{16,20},{20,16},{24,28},{28,24},{32,36},... | collective-permute-start | bytes 234248 | tf_op jit(solution)/shard_map/ppermute | solution.py:18
  12.3 4.9 %collective-permute-start.1 = (bf16[80,488]{1,0:T(8,128)(2,1)S(1)}, bf16[80,488]{1,0:T(8,128)(2,1)S(1)}, u32[]{:S(2)}, u32[]{:S(2)}) collective-permute-start(bf16[80,488]{1,0:T(8,128)(2,1)S(1)} %gather_fusion.1), channel_id=1, source_target_pairs={{0,8},{8,0},{4,12},{12,4},{16,24},{24,16},{20,28},{28,20},{32,40},... | collective-permute-start | bytes 234248 | tf_op jit(solution)/shard_map/ppermute | solution.py:18
  18.1 6.0 %collective-permute-start.2 = (bf16[80,488]{1,0:T(8,128)(2,1)S(1)}, bf16[80,488]{1,0:T(8,128)(2,1)S(1)}, u32[]{:S(2)}, u32[]{:S(2)}) collective-permute-start(bf16[80,488]{1,0:T(8,128)(2,1)S(1)} %gather_fusion.2), channel_id=1, source_target_pairs={{0,16},{16,0},{4,20},{20,4},{8,24},{24,8},{12,28},{28,12},{32,48},... | collective-permute-start | bytes 234248 | tf_op jit(solution)/shard_map/ppermute | solution.py:18
  25.0 4.5 %collective-permute-start.3 = (bf16[80,488]{1,0:T(8,128)(2,1)S(1)}, bf16[80,488]{1,0:T(8,128)(2,1)S(1)}, u32[]{:S(2)}, u32[]{:S(2)}) collective-permute-start(bf16[80,488]{1,0:T(8,128)(2,1)S(1)} %gather_fusion.3), channel_id=1, source_target_pairs={{0,32},{32,0},{4,36},{36,4},{8,40},{40,8},{12,44},{44,12},{16,48},... | collective-permute-start | bytes 234248 | tf_op jit(solution)/shard_map/ppermute | solution.py:18
  30.5 5.8 %collective-permute-start.4 = (bf16[80,488]{1,0:T(8,128)(2,1)S(1)}, bf16[80,488]{1,0:T(8,128)(2,1)S(1)}, u32[]{:S(2)}, u32[]{:S(2)}) collective-permute-start(bf16[80,488]{1,0:T(8,128)(2,1)S(1)} %gather_fusion.4), channel_id=1, source_target_pairs={{0,64},{64,0},{4,68},{68,4},{8,72},{72,8},{12,76},{76,12},{16,80},... | collective-permute-start | bytes 234248 | tf_op jit(solution)/shard_map/ppermute | solution.py:18
  37.0 10.4 %collective-permute-start.5 = (bf16[80,488]{1,0:T(8,128)(2,1)S(1)}, bf16[80,488]{1,0:T(8,128)(2,1)S(1)}, u32[]{:S(2)}, u32[]{:S(2)}) collective-permute-start(bf16[80,488]{1,0:T(8,128)(2,1)S(1)} %gather_fusion.5), channel_id=1, source_target_pairs={{0,128},{128,0},{4,132},{132,4},{8,136},{136,8},{12,140},{140,12},... | collective-permute-start | bytes 234248 | tf_op jit(solution)/shard_map/ppermute | solution.py:18
  59.7 18.6 %collective-permute-start.6 = (f32[64,488]{1,0:T(8,128)S(1)}, f32[64,488]{1,0:T(8,128)S(1)}, u32[]{:S(2)}, u32[]{:S(2)}) collective-permute-start(f32[64,488]{1,0:T(8,128)S(1)} %get-tuple-element.80), channel_id=1, source_target_pairs={{0,1},{1,2},{2,3},{3,0},{4,5},{5,6},{6,7},{7,4},{8,9},{9,10},{10,1... | collective-permute-start | bytes 374792 | tf_op jit(solution)/shard_map/ppermute | solution.py:303
  61.2 17.0 %collective-permute-start.7 = (f32[64,488]{1,0:T(8,128)S(1)}, f32[64,488]{1,0:T(8,128)S(1)}, u32[]{:S(2)}, u32[]{:S(2)}) collective-permute-start(f32[64,488]{1,0:T(8,128)S(1)} %get-tuple-element.82), channel_id=1, source_target_pairs={{0,2},{1,3},{2,0},{3,1},{4,6},{5,7},{6,4},{7,5},{8,10},{9,11},{10,... | collective-permute-start | bytes 374792 | tf_op jit(solution)/shard_map/ppermute | solution.py:303
  64.0 14.3 %collective-permute-start.8 = (f32[64,488]{1,0:T(8,128)S(1)}, f32[64,488]{1,0:T(8,128)S(1)}, u32[]{:S(2)}, u32[]{:S(2)}) collective-permute-start(f32[64,488]{1,0:T(8,128)S(1)} %get-tuple-element.81), channel_id=1, source_target_pairs={{0,3},{1,0},{2,1},{3,2},{4,7},{5,4},{6,5},{7,6},{8,11},{9,8},{10,9... | collective-permute-start | bytes 374792 | tf_op jit(solution)/shard_map/ppermute | solution.py:303
  74.9 17.7 %collective-permute-start.10 = (f32[64,488]{1,0:T(8,128)S(1)}, f32[64,488]{1,0:T(8,128)S(1)}, u32[]{:S(2)}, u32[]{:S(2)}) collective-permute-start(f32[64,488]{1,0:T(8,128)S(1)} %get-tuple-element.88), channel_id=1, source_target_pairs={{0,2},{1,3},{2,0},{3,1},{4,6},{5,7},{6,4},{7,5},{8,10},{9,11},{10,... | collective-permute-start | bytes 374792 | tf_op jit(solution)/shard_map/ppermute | solution.py:303
  75.5 17.3 %collective-permute-start.11 = (f32[64,488]{1,0:T(8,128)S(1)}, f32[64,488]{1,0:T(8,128)S(1)}, u32[]{:S(2)}, u32[]{:S(2)}) collective-permute-start(f32[64,488]{1,0:T(8,128)S(1)} %get-tuple-element.87), channel_id=1, source_target_pairs={{0,3},{1,0},{2,1},{3,2},{4,7},{5,4},{6,5},{7,6},{8,11},{9,8},{10,9... | collective-permute-start | bytes 374792 | tf_op jit(solution)/shard_map/ppermute | solution.py:303
  78.3 14.5 %collective-permute-start.9 = (f32[64,488]{1,0:T(8,128)S(1)}, f32[64,488]{1,0:T(8,128)S(1)}, u32[]{:S(2)}, u32[]{:S(2)}) collective-permute-start(f32[64,488]{1,0:T(8,128)S(1)} %get-tuple-element.86), channel_id=1, source_target_pairs={{0,1},{1,2},{2,3},{3,0},{4,5},{5,6},{6,7},{7,4},{8,9},{9,10},{10,1... | collective-permute-start | bytes 374792 | tf_op jit(solution)/shard_map/ppermute | solution.py:303
  87.8 16.4 %collective-permute-start.12 = (f32[64,488]{1,0:T(8,128)S(1)}, f32[64,488]{1,0:T(8,128)S(1)}, u32[]{:S(2)}, u32[]{:S(2)}) collective-permute-start(f32[64,488]{1,0:T(8,128)S(1)} %get-tuple-element.77), channel_id=1, source_target_pairs={{0,1},{1,2},{2,3},{3,0},{4,5},{5,6},{6,7},{7,4},{8,9},{9,10},{10,1... | collective-permute-start | bytes 374792 | tf_op jit(solution)/shard_map/ppermute | solution.py:303
  88.1 19.0 %collective-permute-start.13 = (f32[64,488]{1,0:T(8,128)S(1)}, f32[64,488]{1,0:T(8,128)S(1)}, u32[]{:S(2)}, u32[]{:S(2)}) collective-permute-start(f32[64,488]{1,0:T(8,128)S(1)} %get-tuple-element.79), channel_id=1, source_target_pairs={{0,2},{1,3},{2,0},{3,1},{4,6},{5,7},{6,4},{7,5},{8,10},{9,11},{10,... | collective-permute-start | bytes 374792 | tf_op jit(solution)/shard_map/ppermute | solution.py:303
  92.6 14.4 %collective-permute-start.14 = (f32[64,488]{1,0:T(8,128)S(1)}, f32[64,488]{1,0:T(8,128)S(1)}, u32[]{:S(2)}, u32[]{:S(2)}) collective-permute-start(f32[64,488]{1,0:T(8,128)S(1)} %get-tuple-element.78), channel_id=1, source_target_pairs={{0,3},{1,0},{2,1},{3,2},{4,7},{5,4},{6,5},{7,6},{8,11},{9,8},{10,9... | collective-permute-start | bytes 374792 | tf_op jit(solution)/shard_map/ppermute | solution.py:303
  102.3 6.3 %collective-permute-start.15 = (f32[64,488]{1,0:T(8,128)S(1)}, f32[64,488]{1,0:T(8,128)S(1)}, u32[]{:S(2)}, u32[]{:S(2)}) collective-permute-start(f32[64,488]{1,0:T(8,128)S(1)} %get-tuple-element.83), channel_id=1, source_target_pairs={{0,1},{1,2},{2,3},{3,0},{4,5},{5,6},{6,7},{7,4},{8,9},{9,10},{10,1... | collective-permute-start | bytes 374792 | tf_op jit(solution)/shard_map/ppermute | solution.py:303
  104.2 6.5 %collective-permute-start.16 = (f32[64,488]{1,0:T(8,128)S(1)}, f32[64,488]{1,0:T(8,128)S(1)}, u32[]{:S(2)}, u32[]{:S(2)}) collective-permute-start(f32[64,488]{1,0:T(8,128)S(1)} %get-tuple-element.85), channel_id=1, source_target_pairs={{0,2},{1,3},{2,0},{3,1},{4,6},{5,7},{6,4},{7,5},{8,10},{9,11},{10,... | collective-permute-start | bytes 374792 | tf_op jit(solution)/shard_map/ppermute | solution.py:303
  104.2 6.6 %collective-permute-start.17 = (f32[64,488]{1,0:T(8,128)S(1)}, f32[64,488]{1,0:T(8,128)S(1)}, u32[]{:S(2)}, u32[]{:S(2)}) collective-permute-start(f32[64,488]{1,0:T(8,128)S(1)} %get-tuple-element.84), channel_id=1, source_target_pairs={{0,3},{1,0},{2,1},{3,2},{4,7},{5,4},{6,5},{7,6},{8,11},{9,8},{10,9... | collective-permute-start | bytes 374792 | tf_op jit(solution)/shard_map/ppermute | solution.py:303

commit v9 on v8

--- a/solution.py
+++ b/solution.py
@@ -302,8 +302,11 @@
             route = [(k, (k + shift) % devices) for k in range(devices)]
             total = total + lax.ppermute(sent, "off", route)
         mine.append(total)
-    mine = jnp.stack(mine).reshape(8, span, width)
-    return mine.transpose(1, 0, 2).reshape(-1, width)
+    result = jnp.zeros((span, 8, width), jnp.float32)
+    for chunk, total in enumerate(mine):
+        placed = total.reshape(per, span, width).transpose(1, 0, 2)
+        result = lax.dynamic_update_slice(result, placed, (0, chunk * per, 0))
+    return result.reshape(-1, width)
 
 
 def solution(mesh):

time: 112 us -> 117 us (1.045)
  waiting for transfers between devices: 13.2 us -> 16.2 us
    ppermute x12, waiting for transfers between devices: 3.79 us -> 6.8 us  [on_device(): total = total + lax.ppermute(sent, 'off', route)]
  transfers between devices with their start and end apart: 18 -> 18, of which waited for: 8 -> 9; matrix products, arithmetic and copies ran while one was open for 2% -> 3% of each run, Pallas kernels for 30% -> 21%
where the time goes in v9:
time: 117 us; the launch traced here: 116 us
  Pallas kernels  48.9 us (42%)
  starting transfers between devices  34.8 us (30%)
  waiting for transfers between devices  16.2 us (14%)
  local copies, waits for them, and re-layouts  12.7 us (11%)
  other arithmetic  2.97 us (3%)
    pallas_call x4, Pallas kernels, translate(): pl.pallas_call(functools.partial(translate_kernel, spread is not None, de...  31.6 us
    ppermute x12, starting transfers between devices, on_device(): total = total + lax.ppermute(sent, 'off', route)  17.9 us
    ppermute x6, starting transfers between devices, partner(): return lax.ppermute(block, axis, route)  17 us
    pallas_call x1, Pallas kernels, first_chunk(): pl.pallas_call(functools.partial(first_kernel, devices, classes), grid=(2...  12.2 us
    ppermute x6, waiting for transfers between devices, partner(): return lax.ppermute(block, axis, route)  9.37 us
    ppermute x12, waiting for transfers between devices, on_device(): total = total + lax.ppermute(sent, 'off', route)  6.8 us
    pallas_call x6, Pallas kernels, slot_table(): pl.pallas_call(invert_kernel, out_shape=jax.ShapeDtypeStruct((classes, pa...  5.2 us
    gather x6, local copies, waits for them, and re-layouts, on_device(): outgoing = rows_all[picks]  4.43 us
  transfers between devices with their start and end apart: 18, of which 9 were waited for; matrix products, arithmetic and copies ran while one was open for 3% of the time, Pallas kernels for 21%

profile of v9, /device:TPU:16, one launch (start us, length us, event | category | flops | bytes accessed | tf_op | source)
XLA Modules:
  0.0 116.3 jit_solution(1554460746732562164)
XLA Ops:
  0.0 0.7 slice_bitcast_fusion
  0.7 0.7 add_bitcast_fusion
  1.6 1.5 %copy.259 = bf16[1024,488]{1,0:T(8,128)(2,1)S(1)} copy(bf16[1024,488]{0,1:T(8,128)(2,1)} %param.11) | data formatting | bytes 1998848 | tf_op args[0]
  3.3 2.1 %copy-done = bf16[8,488,488]{2,1,0:T(8,128)(2,1)S(1)} copy-done((bf16[8,488,488]{2,1,0:T(8,128)(2,1)S(1)}, bf16[8,488,488]{2,1,0:T(8,128)(2,1)}, u32[]{:S(2)}) %copy-start) | copy-done | bytes 3810328
  5.4 3.2 %shard_map.109 = f32[128,488]{1,0:T(8,128)S(1)} custom-call(s32[16,128]{1,0:T(8,128)S(1)} %fusion.18.slot_ref, bf16[1792,488]{1,0:T(8,128)(2,1)S(1)} %dynamic_update_slice.54.buf_ref, bf16[8,488,488]{2,1,0:T(8,128)(2,1)S(1)} %copy-done), custom_call_target="tpu_custom_call" | custom-call | flops 1511129088 | bytes 5559296 | tf_op jit(solution)/shard_map/pallas_call | solution.py:113
  8.9 0.7 gather_fusion
  10.3 0.9 shard_map.110
  11.4 0.7 gather_fusion.1
  12.3 1.4 %collective-permute-start.1 = (bf16[80,488]{1,0:T(8,128)(2,1)S(1)}, bf16[80,488]{1,0:T(8,128)(2,1)S(1)}, u32[]{:S(2)}, u32[]{:S(2)}) collective-permute-start(bf16[80,488]{1,0:T(8,128)(2,1)S(1)} %gather_fusion.1), channel_id=1, source_target_pairs={{0,8},{8,0},{4,12},{12,4},{16,24},{24,16},{20,28},{28,20},{32,40},... | collective-permute-start | bytes 234248 | tf_op jit(solution)/shard_map/ppermute | solution.py:18
  13.7 0.9 shard_map.111
  14.6 2.6 %collective-permute-done.1 = bf16[80,488]{1,0:T(8,128)(2,1)S(1)} collective-permute-done((bf16[80,488]{1,0:T(8,128)(2,1)S(1)}, bf16[80,488]{1,0:T(8,128)(2,1)S(1)}, u32[]{:S(2)}, u32[]{:S(2)}) %collective-permute-start.1) | collective-permute-done | bytes 78112 | tf_op jit(solution)/shard_map/ppermute | solution.py:18
  17.2 0.7 gather_fusion.2
  18.1 2.2 %collective-permute-start.2 = (bf16[80,488]{1,0:T(8,128)(2,1)S(1)}, bf16[80,488]{1,0:T(8,128)(2,1)S(1)}, u32[]{:S(2)}, u32[]{:S(2)}) collective-permute-start(bf16[80,488]{1,0:T(8,128)(2,1)S(1)} %gather_fusion.2), channel_id=1, source_target_pairs={{0,16},{16,0},{4,20},{20,4},{8,24},{24,8},{12,28},{28,12},{32,48},... | collective-permute-start | bytes 234248 | tf_op jit(solution)/shard_map/ppermute | solution.py:18
  20.3 0.9 shard_map.112
  21.2 2.9 %collective-permute-done.2 = bf16[80,488]{1,0:T(8,128)(2,1)S(1)} collective-permute-done((bf16[80,488]{1,0:T(8,128)(2,1)S(1)}, bf16[80,488]{1,0:T(8,128)(2,1)S(1)}, u32[]{:S(2)}, u32[]{:S(2)}) %collective-permute-start.2) | collective-permute-done | bytes 78112 | tf_op jit(solution)/shard_map/ppermute | solution.py:18
  24.1 0.7 gather_fusion.3
  25.0 2.0 %collective-permute-start.3 = (bf16[80,488]{1,0:T(8,128)(2,1)S(1)}, bf16[80,488]{1,0:T(8,128)(2,1)S(1)}, u32[]{:S(2)}, u32[]{:S(2)}) collective-permute-start(bf16[80,488]{1,0:T(8,128)(2,1)S(1)} %gather_fusion.3), channel_id=1, source_target_pairs={{0,32},{32,0},{4,36},{36,4},{8,40},{40,8},{12,44},{44,12},{16,48},... | collective-permute-start | bytes 234248 | tf_op jit(solution)/shard_map/ppermute | solution.py:18
  27.1 0.9 shard_map.113
  28.0 1.6 %collective-permute-done.3 = bf16[80,488]{1,0:T(8,128)(2,1)S(1)} collective-permute-done((bf16[80,488]{1,0:T(8,128)(2,1)S(1)}, bf16[80,488]{1,0:T(8,128)(2,1)S(1)}, u32[]{:S(2)}, u32[]{:S(2)}) %collective-permute-start.3) | collective-permute-done | bytes 78112 | tf_op jit(solution)/shard_map/ppermute | solution.py:18
  29.6 0.7 gather_fusion.4
  30.5 3.4 %collective-permute-start.4 = (bf16[80,488]{1,0:T(8,128)(2,1)S(1)}, bf16[80,488]{1,0:T(8,128)(2,1)S(1)}, u32[]{:S(2)}, u32[]{:S(2)}) collective-permute-start(bf16[80,488]{1,0:T(8,128)(2,1)S(1)} %gather_fusion.4), channel_id=1, source_target_pairs={{0,64},{64,0},{4,68},{68,4},{8,72},{72,8},{12,76},{76,12},{16,80},... | collective-permute-start | bytes 234248 | tf_op jit(solution)/shard_map/ppermute | solution.py:18
  33.9 0.9 shard_map.114
  34.8 1.5 %collective-permute-done.4 = bf16[80,488]{1,0:T(8,128)(2,1)S(1)} collective-permute-done((bf16[80,488]{1,0:T(8,128)(2,1)S(1)}, bf16[80,488]{1,0:T(8,128)(2,1)S(1)}, u32[]{:S(2)}, u32[]{:S(2)}) %collective-permute-start.4) | collective-permute-done | bytes 78112 | tf_op jit(solution)/shard_map/ppermute | solution.py:18
  36.3 0.7 gather_fusion.5
  37.0 8.0 %collective-permute-start.5 = (bf16[80,488]{1,0:T(8,128)(2,1)S(1)}, bf16[80,488]{1,0:T(8,128)(2,1)S(1)}, u32[]{:S(2)}, u32[]{:S(2)}) collective-permute-start(bf16[80,488]{1,0:T(8,128)(2,1)S(1)} %gather_fusion.5), channel_id=1, source_target_pairs={{0,128},{128,0},{4,132},{132,4},{8,136},{136,8},{12,140},{140,12},... | collective-permute-start | bytes 234248 | tf_op jit(solution)/shard_map/ppermute | solution.py:18
  45.0 0.5 shard_map.115
  46.5 0.9 collective-permute-done.5
  47.4 12.2 %shard_map.116 = (f32[256,488]{1,0:T(8,128)S(1)}, bf16[128,488]{1,0:T(8,128)(2,1)S(1)}, bf16[128,488]{1,0:T(8,128)(2,1)S(1)}) custom-call(s32[16,1024]{1,0:T(8,128)S(1)} %pad.59.slot_ref, bf16[1792,488]{1,0:T(8,128)(2,1)S(1)} %slice_dynamic-update-slice_fusion.6.buf_ref, bf16[10,488,488]{2,1,0:T(8,128)(2,1)} %k_ref.9, s32[16,128]{1,0:T(8,128)S(1)} %pad.62.cslot_ref, ...), custom_call_target="tpu_custom_call" | custom-call | flops 4737269760 | bytes 4762880 | tf_op jit(solution)/shard_map/pallas_call | solution.py:180
  59.6 9.4 %shard_map.117 = f32[256,488]{1,0:T(8,128)S(1)} custom-call(s32[16,1024]{1,0:T(8,128)S(1)} %pad.59.slot_ref, bf16[1792,488]{1,0:T(8,128)(2,1)S(1)} %slice_dynamic-update-slice_fusion.6.buf_ref, bf16[10,488,488]{2,1,0:T(8,128)(2,1)} %k_ref.9, bf16[128,488]{1,0:T(8,128)(2,1)S(1)} %get-tuple-element.71.rest_0_, bf16[128,488]{1,0:T(8,128)(2,1)S(1)} %get-tuple-element.72.rest_1_, ...), custom_call_target="tpu_custom_call" | custom-call | flops 4737269760 | bytes 6511872 | tf_op jit(solution)/shard_map/pallas_call | solution.py:113
  69.1 0.7 constant_dynamic-slice_fusion.8
  69.8 3.0 %collective-permute-start.10 = (f32[64,488]{1,0:T(8,128)}, f32[64,488]{1,0:T(8,128)S(1)}, u32[]{:S(2)}, u32[]{:S(2)}) collective-permute-start(f32[64,488]{1,0:T(8,128)} %get-tuple-element.85), channel_id=1, source_target_pairs={{0,2},{1,3},{2,0},{3,1},{4,6},{5,7},{6,4},{7,5},{8,10},{9,11},{10,... | collective-permute-start | bytes 374792 | tf_op jit(solution)/shard_map/ppermute | solution.py:303
  72.8 1.1 collective-permute-start.11
  74.0 0.9 collective-permute-start.9
  74.9 0.7 collective-permute-start.6
  75.6 3.2 %collective-permute-start.7 = (f32[64,488]{1,0:T(8,128)S(1)}, f32[64,488]{1,0:T(8,128)S(1)}, u32[]{:S(2)}, u32[]{:S(2)}) collective-permute-start(f32[64,488]{1,0:T(8,128)S(1)} %get-tuple-element.88), channel_id=1, source_target_pairs={{0,2},{1,3},{2,0},{3,1},{4,6},{5,7},{6,4},{7,5},{8,10},{9,11},{10,... | collective-permute-start | bytes 374792 | tf_op jit(solution)/shard_map/ppermute | solution.py:303
  78.8 1.9 %collective-permute-start.8 = (f32[64,488]{1,0:T(8,128)S(1)}, f32[64,488]{1,0:T(8,128)S(1)}, u32[]{:S(2)}, u32[]{:S(2)}) collective-permute-start(f32[64,488]{1,0:T(8,128)S(1)} %get-tuple-element.87), channel_id=1, source_target_pairs={{0,3},{1,0},{2,1},{3,2},{4,7},{5,4},{6,5},{7,6},{8,11},{9,8},{10,9... | collective-permute-start | bytes 374792 | tf_op jit(solution)/shard_map/ppermute | solution.py:303
  80.7 1.0 add_add_fusion.2
  81.7 9.4 %shard_map.119 = f32[256,488]{1,0:T(8,128)S(1)} custom-call(s32[16,1024]{1,0:T(8,128)S(1)} %pad.59.slot_ref, bf16[1792,488]{1,0:T(8,128)(2,1)S(1)} %slice_dynamic-update-slice_fusion.6.buf_ref, bf16[10,488,488]{2,1,0:T(8,128)(2,1)} %k_ref.9, bf16[128,488]{1,0:T(8,128)(2,1)S(1)} %get-tuple-element.71.rest_0_, bf16[128,488]{1,0:T(8,128)(2,1)S(1)} %get-tuple-element.72.rest_1_, ...), custom_call_target="tpu_custom_call" | custom-call | flops 4737269760 | bytes 6511872 | tf_op jit(solution)/shard_map/pallas_call | solution.py:113
  91.4 2.9 %collective-permute-start.16 = (f32[64,488]{1,0:T(8,128)S(1)}, f32[64,488]{1,0:T(8,128)S(1)}, u32[]{:S(2)}, u32[]{:S(2)}) collective-permute-start(f32[64,488]{1,0:T(8,128)S(1)} %get-tuple-element.79), channel_id=1, source_target_pairs={{0,2},{1,3},{2,0},{3,1},{4,6},{5,7},{6,4},{7,5},{8,10},{9,11},{10,... | collective-permute-start | bytes 374792 | tf_op jit(solution)/shard_map/ppermute | solution.py:303
  94.4 9.4 %shard_map.118 = f32[256,488]{1,0:T(8,128)S(1)} custom-call(s32[16,1024]{1,0:T(8,128)S(1)} %pad.59.slot_ref, bf16[1792,488]{1,0:T(8,128)(2,1)S(1)} %slice_dynamic-update-slice_fusion.6.buf_ref, bf16[10,488,488]{2,1,0:T(8,128)(2,1)} %k_ref.9, bf16[128,488]{1,0:T(8,128)(2,1)S(1)} %get-tuple-element.71.rest_0_, bf16[128,488]{1,0:T(8,128)(2,1)S(1)} %get-tuple-element.72.rest_1_, ...), custom_call_target="tpu_custom_call" | custom-call | flops 4737269760 | bytes 6511872 | tf_op jit(solution)/shard_map/pallas_call | solution.py:113
  103.8 1.1 collective-permute-start.12
  105.0 0.7 collective-permute-start.13
  105.7 2.0 %collective-permute-start.14 = (f32[64,488]{1,0:T(8,128)S(1)}, f32[64,488]{1,0:T(8,128)S(1)}, u32[]{:S(2)}, u32[]{:S(2)}) collective-permute-start(f32[64,488]{1,0:T(8,128)S(1)} %get-tuple-element.81), channel_id=1, source_target_pairs={{0,3},{1,0},{2,1},{3,2},{4,7},{5,4},{6,5},{7,6},{8,11},{9,8},{10,9... | collective-permute-start | bytes 374792 | tf_op jit(solution)/shard_map/ppermute | solution.py:303
  108.1 2.0 %collective-permute-done.12 = f32[64,488]{1,0:T(8,128)S(1)} collective-permute-done((f32[64,488]{1,0:T(8,128)S(1)}, f32[64,488]{1,0:T(8,128)S(1)}, u32[]{:S(2)}, u32[]{:S(2)}) %collective-permute-start.12) | collective-permute-done | bytes 124960 | tf_op jit(solution)/shard_map/ppermute | solution.py:303
  110.1 1.4 %collective-permute-done.13 = f32[64,488]{1,0:T(8,128)S(1)} collective-permute-done((f32[64,488]{1,0:T(8,128)S(1)}, f32[64,488]{1,0:T(8,128)S(1)}, u32[]{:S(2)}, u32[]{:S(2)}) %collective-permute-start.13) | collective-permute-done | bytes 124960 | tf_op jit(solution)/shard_map/ppermute | solution.py:303
  111.5 0.9 collective-permute-done.14
  112.6 2.5 %collective-permute-done.17 = f32[64,488]{1,0:T(8,128)S(1)} collective-permute-done((f32[64,488]{1,0:T(8,128)S(1)}, f32[64,488]{1,0:T(8,128)S(1)}, u32[]{:S(2)}, u32[]{:S(2)}) %collective-permute-start.17) | collective-permute-done | bytes 124960 | tf_op jit(solution)/shard_map/ppermute | solution.py:303
  115.3 1.0 copy.283
  (107 shorter events, 3.8 us)
Async XLA Ops:
  3.3 2.1 %copy-start = (bf16[8,488,488]{2,1,0:T(8,128)(2,1)S(1)}, bf16[8,488,488]{2,1,0:T(8,128)(2,1)}, u32[]{:S(2)}) copy-start(bf16[8,488,488]{2,1,0:T(8,128)(2,1)} %rest_2_.5) | copy-start | bytes 11430916
  5.4 3.3 %copy-start.1 = (s32[1,10,1024]{2,0,1:T(1,128)S(1)}, s32[1,10,1024]{2,0,1:T(1,128)}, u32[]{:S(2)}) copy-start(s32[1,10,1024]{2,0,1:T(1,128)} %param.15) | copy-start | bytes 122884
  5.4 3.3 %copy-start.2 = (s32[1,10,1024]{2,0,1:T(1,128)S(1)}, s32[1,10,1024]{2,0,1:T(1,128)}, u32[]{:S(2)}) copy-start(s32[1,10,1024]{2,0,1:T(1,128)} %param.14) | copy-start | bytes 122884
  5.4 3.4 %copy-start.3 = (s32[1,10]{1,0:T(1,128)S(1)}, s32[1,10]{1,0:T(1,128)}, u32[]{:S(2)}) copy-start(s32[1,10]{1,0:T(1,128)} %param.16) | copy-start | bytes 124
  5.4 4.7 %copy-start.4 = (s32[1,10,128]{2,0,1:T(1,128)S(1)}, s32[1,10,128]{2,0,1:T(1,128)}, u32[]{:S(2)}) copy-start(s32[1,10,128]{2,0,1:T(1,128)} %param.18) | copy-start | bytes 15364
  5.4 4.7 %copy-start.6 = (s32[1,10]{1,0:T(1,128)S(1)}, s32[1,10]{1,0:T(1,128)}, u32[]{:S(2)}) copy-start(s32[1,10]{1,0:T(1,128)} %param.19) | copy-start | bytes 124
  5.4 4.8 %copy-start.5 = (s32[1,10,128]{2,0,1:T(1,128)S(1)}, s32[1,10,128]{2,0,1:T(1,128)}, u32[]{:S(2)}) copy-start(s32[1,10,128]{2,0,1:T(1,128)} %param.17) | copy-start | bytes 15364
  9.6 1.7 %collective-permute-start = (bf16[80,488]{1,0:T(8,128)(2,1)S(1)}, bf16[80,488]{1,0:T(8,128)(2,1)S(1)}, u32[]{:S(2)}, u32[]{:S(2)}) collective-permute-start(bf16[80,488]{1,0:T(8,128)(2,1)S(1)} %gather_fusion), channel_id=1, source_target_pairs={{0,4},{4,0},{8,12},{12,8},{16,20},{20,16},{24,28},{28,24},{32,36},... | collective-permute-start | bytes 234248 | tf_op jit(solution)/shard_map/ppermute | solution.py:18
  12.3 4.9 %collective-permute-start.1 = (bf16[80,488]{1,0:T(8,128)(2,1)S(1)}, bf16[80,488]{1,0:T(8,128)(2,1)S(1)}, u32[]{:S(2)}, u32[]{:S(2)}) collective-permute-start(bf16[80,488]{1,0:T(8,128)(2,1)S(1)} %gather_fusion.1), channel_id=1, source_target_pairs={{0,8},{8,0},{4,12},{12,4},{16,24},{24,16},{20,28},{28,20},{32,40},... | collective-permute-start | bytes 234248 | tf_op jit(solution)/shard_map/ppermute | solution.py:18
  18.1 6.0 %collective-permute-start.2 = (bf16[80,488]{1,0:T(8,128)(2,1)S(1)}, bf16[80,488]{1,0:T(8,128)(2,1)S(1)}, u32[]{:S(2)}, u32[]{:S(2)}) collective-permute-start(bf16[80,488]{1,0:T(8,128)(2,1)S(1)} %gather_fusion.2), channel_id=1, source_target_pairs={{0,16},{16,0},{4,20},{20,4},{8,24},{24,8},{12,28},{28,12},{32,48},... | collective-permute-start | bytes 234248 | tf_op jit(solution)/shard_map/ppermute | solution.py:18
  25.0 4.5 %collective-permute-start.3 = (bf16[80,488]{1,0:T(8,128)(2,1)S(1)}, bf16[80,488]{1,0:T(8,128)(2,1)S(1)}, u32[]{:S(2)}, u32[]{:S(2)}) collective-permute-start(bf16[80,488]{1,0:T(8,128)(2,1)S(1)} %gather_fusion.3), channel_id=1, source_target_pairs={{0,32},{32,0},{4,36},{36,4},{8,40},{40,8},{12,44},{44,12},{16,48},... | collective-permute-start | bytes 234248 | tf_op jit(solution)/shard_map/ppermute | solution.py:18
  30.5 5.8 %collective-permute-start.4 = (bf16[80,488]{1,0:T(8,128)(2,1)S(1)}, bf16[80,488]{1,0:T(8,128)(2,1)S(1)}, u32[]{:S(2)}, u32[]{:S(2)}) collective-permute-start(bf16[80,488]{1,0:T(8,128)(2,1)S(1)} %gather_fusion.4), channel_id=1, source_target_pairs={{0,64},{64,0},{4,68},{68,4},{8,72},{72,8},{12,76},{76,12},{16,80},... | collective-permute-start | bytes 234248 | tf_op jit(solution)/shard_map/ppermute | solution.py:18
  37.0 10.4 %collective-permute-start.5 = (bf16[80,488]{1,0:T(8,128)(2,1)S(1)}, bf16[80,488]{1,0:T(8,128)(2,1)S(1)}, u32[]{:S(2)}, u32[]{:S(2)}) collective-permute-start(bf16[80,488]{1,0:T(8,128)(2,1)S(1)} %gather_fusion.5), channel_id=1, source_target_pairs={{0,128},{128,0},{4,132},{132,4},{8,136},{136,8},{12,140},{140,12},... | collective-permute-start | bytes 234248 | tf_op jit(solution)/shard_map/ppermute | solution.py:18
  69.8 9.0 %collective-permute-start.10 = (f32[64,488]{1,0:T(8,128)}, f32[64,488]{1,0:T(8,128)S(1)}, u32[]{:S(2)}, u32[]{:S(2)}) collective-permute-start(f32[64,488]{1,0:T(8,128)} %get-tuple-element.85), channel_id=1, source_target_pairs={{0,2},{1,3},{2,0},{3,1},{4,6},{5,7},{6,4},{7,5},{8,10},{9,11},{10,... | collective-permute-start | bytes 374792 | tf_op jit(solution)/shard_map/ppermute | solution.py:303
  72.8 7.8 %collective-permute-start.11 = (f32[64,488]{1,0:T(8,128)}, f32[64,488]{1,0:T(8,128)}, u32[]{:S(2)}, u32[]{:S(2)}) collective-permute-start(f32[64,488]{1,0:T(8,128)} %get-tuple-element.84), channel_id=1, source_target_pairs={{0,3},{1,0},{2,1},{3,2},{4,7},{5,4},{6,5},{7,6},{8,11},{9,8},{10,9... | collective-permute-start | bytes 374792 | tf_op jit(solution)/shard_map/ppermute | solution.py:303
  74.0 6.7 %collective-permute-start.9 = (f32[64,488]{1,0:T(8,128)S(1)}, f32[64,488]{1,0:T(8,128)}, u32[]{:S(2)}, u32[]{:S(2)}) collective-permute-start(f32[64,488]{1,0:T(8,128)S(1)} %get-tuple-element.83), channel_id=1, source_target_pairs={{0,1},{1,2},{2,3},{3,0},{4,5},{5,6},{6,7},{7,4},{8,9},{9,10},{10,1... | collective-permute-start | bytes 374792 | tf_op jit(solution)/shard_map/ppermute | solution.py:303
  74.9 19.4 %collective-permute-start.6 = (f32[64,488]{1,0:T(8,128)S(1)}, f32[64,488]{1,0:T(8,128)S(1)}, u32[]{:S(2)}, u32[]{:S(2)}) collective-permute-start(f32[64,488]{1,0:T(8,128)S(1)} %get-tuple-element.86), channel_id=1, source_target_pairs={{0,1},{1,2},{2,3},{3,0},{4,5},{5,6},{6,7},{7,4},{8,9},{9,10},{10,1... | collective-permute-start | bytes 374792 | tf_op jit(solution)/shard_map/ppermute | solution.py:303
  75.6 18.7 %collective-permute-start.7 = (f32[64,488]{1,0:T(8,128)S(1)}, f32[64,488]{1,0:T(8,128)S(1)}, u32[]{:S(2)}, u32[]{:S(2)}) collective-permute-start(f32[64,488]{1,0:T(8,128)S(1)} %get-tuple-element.88), channel_id=1, source_target_pairs={{0,2},{1,3},{2,0},{3,1},{4,6},{5,7},{6,4},{7,5},{8,10},{9,11},{10,... | collective-permute-start | bytes 374792 | tf_op jit(solution)/shard_map/ppermute | solution.py:303
  78.8 15.5 %collective-permute-start.8 = (f32[64,488]{1,0:T(8,128)S(1)}, f32[64,488]{1,0:T(8,128)S(1)}, u32[]{:S(2)}, u32[]{:S(2)}) collective-permute-start(f32[64,488]{1,0:T(8,128)S(1)} %get-tuple-element.87), channel_id=1, source_target_pairs={{0,3},{1,0},{2,1},{3,2},{4,7},{5,4},{6,5},{7,6},{8,11},{9,8},{10,9... | collective-permute-start | bytes 374792 | tf_op jit(solution)/shard_map/ppermute | solution.py:303
  91.2 21.4 %collective-permute-start.15 = (f32[64,488]{1,0:T(8,128)S(1)}, f32[64,488]{1,0:T(8,128)S(1)}, u32[]{:S(2)}, u32[]{:S(2)}) collective-permute-start(f32[64,488]{1,0:T(8,128)S(1)} %get-tuple-element.77), channel_id=1, source_target_pairs={{0,1},{1,2},{2,3},{3,0},{4,5},{5,6},{6,7},{7,4},{8,9},{9,10},{10,1... | collective-permute-start | bytes 374792 | tf_op jit(solution)/shard_map/ppermute | solution.py:303
  91.4 21.2 %collective-permute-start.16 = (f32[64,488]{1,0:T(8,128)S(1)}, f32[64,488]{1,0:T(8,128)S(1)}, u32[]{:S(2)}, u32[]{:S(2)}) collective-permute-start(f32[64,488]{1,0:T(8,128)S(1)} %get-tuple-element.79), channel_id=1, source_target_pairs={{0,2},{1,3},{2,0},{3,1},{4,6},{5,7},{6,4},{7,5},{8,10},{9,11},{10,... | collective-permute-start | bytes 374792 | tf_op jit(solution)/shard_map/ppermute | solution.py:303
  103.8 6.3 %collective-permute-start.12 = (f32[64,488]{1,0:T(8,128)S(1)}, f32[64,488]{1,0:T(8,128)S(1)}, u32[]{:S(2)}, u32[]{:S(2)}) collective-permute-start(f32[64,488]{1,0:T(8,128)S(1)} %get-tuple-element.80), channel_id=1, source_target_pairs={{0,1},{1,2},{2,3},{3,0},{4,5},{5,6},{6,7},{7,4},{8,9},{9,10},{10,1... | collective-permute-start | bytes 374792 | tf_op jit(solution)/shard_map/ppermute | solution.py:303
  105.0 6.5 %collective-permute-start.13 = (f32[64,488]{1,0:T(8,128)S(1)}, f32[64,488]{1,0:T(8,128)S(1)}, u32[]{:S(2)}, u32[]{:S(2)}) collective-permute-start(f32[64,488]{1,0:T(8,128)S(1)} %get-tuple-element.82), channel_id=1, source_target_pairs={{0,2},{1,3},{2,0},{3,1},{4,6},{5,7},{6,4},{7,5},{8,10},{9,11},{10,... | collective-permute-start | bytes 374792 | tf_op jit(solution)/shard_map/ppermute | solution.py:303
  105.7 6.6 %collective-permute-start.14 = (f32[64,488]{1,0:T(8,128)S(1)}, f32[64,488]{1,0:T(8,128)S(1)}, u32[]{:S(2)}, u32[]{:S(2)}) collective-permute-start(f32[64,488]{1,0:T(8,128)S(1)} %get-tuple-element.81), channel_id=1, source_target_pairs={{0,3},{1,0},{2,1},{3,2},{4,7},{5,4},{6,5},{7,6},{8,11},{9,8},{10,9... | collective-permute-start | bytes 374792 | tf_op jit(solution)/shard_map/ppermute | solution.py:303
  110.1 5.0 %collective-permute-start.17 = (f32[64,488]{1,0:T(8,128)S(1)}, f32[64,488]{1,0:T(8,128)S(1)}, u32[]{:S(2)}, u32[]{:S(2)}) collective-permute-start(f32[64,488]{1,0:T(8,128)S(1)} %get-tuple-element.78), channel_id=1, source_target_pairs={{0,3},{1,0},{2,1},{3,2},{4,7},{5,4},{6,5},{7,6},{8,11},{9,8},{10,9... | collective-permute-start | bytes 374792 | tf_op jit(solution)/shard_map/ppermute | solution.py:303

commit v10 on v8

--- a/solution.py
+++ b/solution.py
@@ -283,8 +283,8 @@
     mine = []
     for chunk in range(chunks):
         slot_in = leaf_slot
-        if chunk >= 2:
-            slot_in, _ = lax.optimization_barrier((leaf_slot, mine[chunk - 2]))
+        if chunk >= 3:
+            slot_in, _ = lax.optimization_barrier((leaf_slot, mine[chunk - 3]))
         if chunk == 0:
             partial_sum, coarse_high, coarse_low = first_chunk(
                 slot_in, rows_all, leaf_rows, kernels, coarse_slot, rows_all[leaf_region:],

time: 112 us -> 114 us (1.018); the launches traced: 112 us -> 113 us
  waiting for transfers between devices: 13.2 us -> 14.5 us
    ppermute x12, waiting for transfers between devices: 3.79 us -> 5.09 us  [on_device(): total = total + lax.ppermute(sent, 'off', route)]
  transfers between devices with their start and end apart: 18 -> 18, of which waited for: 8 -> 9; matrix products, arithmetic and copies ran while one was open for 2% -> 2% of each run, Pallas kernels for 30% -> 13%
where the time goes in v10:
time: 114 us; the launch traced here: 113 us
  Pallas kernels  48.9 us (43%)
  starting transfers between devices  35.1 us (31%)
  waiting for transfers between devices  14.5 us (13%)
  local copies, waits for them, and re-layouts  11.7 us (10%)
  other arithmetic  2.04 us (2%)
    pallas_call x4, Pallas kernels, translate(): pl.pallas_call(functools.partial(translate_kernel, spread is not None, de...  31.6 us
    ppermute x12, starting transfers between devices, on_device(): total = total + lax.ppermute(sent, 'off', route)  18.1 us
    ppermute x6, starting transfers between devices, partner(): return lax.ppermute(block, axis, route)  17 us
    pallas_call x1, Pallas kernels, first_chunk(): pl.pallas_call(functools.partial(first_kernel, devices, classes), grid=(2...  12.2 us
    ppermute x6, waiting for transfers between devices, partner(): return lax.ppermute(block, axis, route)  9.37 us
    pallas_call x6, Pallas kernels, slot_table(): pl.pallas_call(invert_kernel, out_shape=jax.ShapeDtypeStruct((classes, pa...  5.2 us
    ppermute x12, waiting for transfers between devices, on_device(): total = total + lax.ppermute(sent, 'off', route)  5.09 us
    gather x6, local copies, waits for them, and re-layouts, on_device(): outgoing = rows_all[picks]  4.43 us
  transfers between devices with their start and end apart: 18, of which 9 were waited for; matrix products, arithmetic and copies ran while one was open for 2% of the time, Pallas kernels for 13%

profile of v10, /device:TPU:16, one launch (start us, length us, event | category | flops | bytes accessed | tf_op | source)
XLA Modules:
  0.0 112.9 jit_solution(9676286834557453434)
XLA Ops:
  0.0 0.7 slice_bitcast_fusion
  0.7 0.7 add_bitcast_fusion.3
  1.6 1.5 %copy.232 = bf16[1024,488]{1,0:T(8,128)(2,1)S(1)} copy(bf16[1024,488]{0,1:T(8,128)(2,1)} %param.11) | data formatting | bytes 1998848 | tf_op args[0]
  3.3 2.1 %copy-done = bf16[8,488,488]{2,1,0:T(8,128)(2,1)S(1)} copy-done((bf16[8,488,488]{2,1,0:T(8,128)(2,1)S(1)}, bf16[8,488,488]{2,1,0:T(8,128)(2,1)}, u32[]{:S(2)}) %copy-start) | copy-done | bytes 3810328
  5.4 3.2 %shard_map.109 = f32[128,488]{1,0:T(8,128)S(1)} custom-call(s32[16,128]{1,0:T(8,128)S(1)} %fusion.18.slot_ref, bf16[1792,488]{1,0:T(8,128)(2,1)S(1)} %dynamic_update_slice.42.buf_ref, bf16[8,488,488]{2,1,0:T(8,128)(2,1)S(1)} %copy-done), custom_call_target="tpu_custom_call" | custom-call | flops 1511129088 | bytes 5559296 | tf_op jit(solution)/shard_map/pallas_call | solution.py:113
  8.9 0.7 gather_fusion
  10.3 0.9 shard_map.110
  11.4 0.7 gather_fusion.1
  12.3 1.4 %collective-permute-start.1 = (bf16[80,488]{1,0:T(8,128)(2,1)S(1)}, bf16[80,488]{1,0:T(8,128)(2,1)S(1)}, u32[]{:S(2)}, u32[]{:S(2)}) collective-permute-start(bf16[80,488]{1,0:T(8,128)(2,1)S(1)} %gather_fusion.1), channel_id=1, source_target_pairs={{0,8},{8,0},{4,12},{12,4},{16,24},{24,16},{20,28},{28,20},{32,40},... | collective-permute-start | bytes 234248 | tf_op jit(solution)/shard_map/ppermute | solution.py:18
  13.7 0.9 shard_map.111
  14.6 2.6 %collective-permute-done.1 = bf16[80,488]{1,0:T(8,128)(2,1)S(1)} collective-permute-done((bf16[80,488]{1,0:T(8,128)(2,1)S(1)}, bf16[80,488]{1,0:T(8,128)(2,1)S(1)}, u32[]{:S(2)}, u32[]{:S(2)}) %collective-permute-start.1) | collective-permute-done | bytes 78112 | tf_op jit(solution)/shard_map/ppermute | solution.py:18
  17.2 0.7 gather_fusion.2
  18.1 2.2 %collective-permute-start.2 = (bf16[80,488]{1,0:T(8,128)(2,1)S(1)}, bf16[80,488]{1,0:T(8,128)(2,1)S(1)}, u32[]{:S(2)}, u32[]{:S(2)}) collective-permute-start(bf16[80,488]{1,0:T(8,128)(2,1)S(1)} %gather_fusion.2), channel_id=1, source_target_pairs={{0,16},{16,0},{4,20},{20,4},{8,24},{24,8},{12,28},{28,12},{32,48},... | collective-permute-start | bytes 234248 | tf_op jit(solution)/shard_map/ppermute | solution.py:18
  20.3 0.9 shard_map.112
  21.2 2.9 %collective-permute-done.2 = bf16[80,488]{1,0:T(8,128)(2,1)S(1)} collective-permute-done((bf16[80,488]{1,0:T(8,128)(2,1)S(1)}, bf16[80,488]{1,0:T(8,128)(2,1)S(1)}, u32[]{:S(2)}, u32[]{:S(2)}) %collective-permute-start.2) | collective-permute-done | bytes 78112 | tf_op jit(solution)/shard_map/ppermute | solution.py:18
  24.1 0.7 gather_fusion.3
  25.0 2.0 %collective-permute-start.3 = (bf16[80,488]{1,0:T(8,128)(2,1)S(1)}, bf16[80,488]{1,0:T(8,128)(2,1)S(1)}, u32[]{:S(2)}, u32[]{:S(2)}) collective-permute-start(bf16[80,488]{1,0:T(8,128)(2,1)S(1)} %gather_fusion.3), channel_id=1, source_target_pairs={{0,32},{32,0},{4,36},{36,4},{8,40},{40,8},{12,44},{44,12},{16,48},... | collective-permute-start | bytes 234248 | tf_op jit(solution)/shard_map/ppermute | solution.py:18
  27.1 0.9 shard_map.113
  28.0 1.6 %collective-permute-done.3 = bf16[80,488]{1,0:T(8,128)(2,1)S(1)} collective-permute-done((bf16[80,488]{1,0:T(8,128)(2,1)S(1)}, bf16[80,488]{1,0:T(8,128)(2,1)S(1)}, u32[]{:S(2)}, u32[]{:S(2)}) %collective-permute-start.3) | collective-permute-done | bytes 78112 | tf_op jit(solution)/shard_map/ppermute | solution.py:18
  29.6 0.7 gather_fusion.4
  30.5 3.4 %collective-permute-start.4 = (bf16[80,488]{1,0:T(8,128)(2,1)S(1)}, bf16[80,488]{1,0:T(8,128)(2,1)S(1)}, u32[]{:S(2)}, u32[]{:S(2)}) collective-permute-start(bf16[80,488]{1,0:T(8,128)(2,1)S(1)} %gather_fusion.4), channel_id=1, source_target_pairs={{0,64},{64,0},{4,68},{68,4},{8,72},{72,8},{12,76},{76,12},{16,80},... | collective-permute-start | bytes 234248 | tf_op jit(solution)/shard_map/ppermute | solution.py:18
  33.9 0.9 shard_map.114
  34.8 1.5 %collective-permute-done.4 = bf16[80,488]{1,0:T(8,128)(2,1)S(1)} collective-permute-done((bf16[80,488]{1,0:T(8,128)(2,1)S(1)}, bf16[80,488]{1,0:T(8,128)(2,1)S(1)}, u32[]{:S(2)}, u32[]{:S(2)}) %collective-permute-start.4) | collective-permute-done | bytes 78112 | tf_op jit(solution)/shard_map/ppermute | solution.py:18
  36.3 0.7 gather_fusion.5
  37.0 8.0 %collective-permute-start.5 = (bf16[80,488]{1,0:T(8,128)(2,1)S(1)}, bf16[80,488]{1,0:T(8,128)(2,1)S(1)}, u32[]{:S(2)}, u32[]{:S(2)}) collective-permute-start(bf16[80,488]{1,0:T(8,128)(2,1)S(1)} %gather_fusion.5), channel_id=1, source_target_pairs={{0,128},{128,0},{4,132},{132,4},{8,136},{136,8},{12,140},{140,12},... | collective-permute-start | bytes 234248 | tf_op jit(solution)/shard_map/ppermute | solution.py:18
  45.0 0.5 shard_map.115
  45.8 0.5 copy.251
  46.5 0.9 collective-permute-done.5
  47.4 12.2 %shard_map.116 = (f32[256,488]{1,0:T(8,128)S(1)}, bf16[128,488]{1,0:T(8,128)(2,1)S(1)}, bf16[128,488]{1,0:T(8,128)(2,1)S(1)}) custom-call(s32[16,1024]{1,0:T(8,128)S(1)} %pad.58.slot_ref, bf16[1792,488]{1,0:T(8,128)(2,1)S(1)} %slice_dynamic-update-slice_fusion.6.buf_ref, bf16[10,488,488]{2,1,0:T(8,128)(2,1)} %k_ref.9, s32[16,128]{1,0:T(8,128)S(1)} %pad.61.cslot_ref, ...), custom_call_target="tpu_custom_call" | custom-call | flops 4737269760 | bytes 4762880 | tf_op jit(solution)/shard_map/pallas_call | solution.py:180
  59.6 9.4 %shard_map.117 = f32[256,488]{1,0:T(8,128)S(1)} custom-call(s32[16,1024]{1,0:T(8,128)S(1)} %pad.58.slot_ref, bf16[1792,488]{1,0:T(8,128)(2,1)S(1)} %slice_dynamic-update-slice_fusion.6.buf_ref, bf16[10,488,488]{2,1,0:T(8,128)(2,1)} %k_ref.9, bf16[128,488]{1,0:T(8,128)(2,1)S(1)} %get-tuple-element.70.rest_0_, bf16[128,488]{1,0:T(8,128)(2,1)S(1)} %get-tuple-element.71.rest_1_, ...), custom_call_target="tpu_custom_call" | custom-call | flops 4737269760 | bytes 6511872 | tf_op jit(solution)/shard_map/pallas_call | solution.py:113
  69.1 9.4 %shard_map.118 = f32[256,488]{1,0:T(8,128)S(1)} custom-call(s32[16,1024]{1,0:T(8,128)S(1)} %pad.58.slot_ref, bf16[1792,488]{1,0:T(8,128)(2,1)S(1)} %slice_dynamic-update-slice_fusion.6.buf_ref, bf16[10,488,488]{2,1,0:T(8,128)(2,1)} %k_ref.9, bf16[128,488]{1,0:T(8,128)(2,1)S(1)} %get-tuple-element.70.rest_0_, bf16[128,488]{1,0:T(8,128)(2,1)S(1)} %get-tuple-element.71.rest_1_, ...), custom_call_target="tpu_custom_call" | custom-call | flops 4737269760 | bytes 6511872 | tf_op jit(solution)/shard_map/pallas_call | solution.py:113
  78.6 1.6 %collective-permute-start.6 = (f32[64,488]{1,0:T(8,128)S(1)}, f32[64,488]{1,0:T(8,128)S(1)}, u32[]{:S(2)}, u32[]{:S(2)}) collective-permute-start(f32[64,488]{1,0:T(8,128)S(1)} %get-tuple-element.84), channel_id=1, source_target_pairs={{0,1},{1,2},{2,3},{3,0},{4,5},{5,6},{6,7},{7,4},{8,9},{9,10},{10,1... | collective-permute-start | bytes 374792 | tf_op jit(solution)/shard_map/ppermute | solution.py:303
  80.1 2.8 %collective-permute-start.7 = (f32[64,488]{1,0:T(8,128)S(1)}, f32[64,488]{1,0:T(8,128)S(1)}, u32[]{:S(2)}, u32[]{:S(2)}) collective-permute-start(f32[64,488]{1,0:T(8,128)S(1)} %get-tuple-element.86), channel_id=1, source_target_pairs={{0,2},{1,3},{2,0},{3,1},{4,6},{5,7},{6,4},{7,5},{8,10},{9,11},{10,... | collective-permute-start | bytes 374792 | tf_op jit(solution)/shard_map/ppermute | solution.py:303
  82.9 1.4 %collective-permute-start.8 = (f32[64,488]{1,0:T(8,128)S(1)}, f32[64,488]{1,0:T(8,128)S(1)}, u32[]{:S(2)}, u32[]{:S(2)}) collective-permute-start(f32[64,488]{1,0:T(8,128)S(1)} %get-tuple-element.85), channel_id=1, source_target_pairs={{0,3},{1,0},{2,1},{3,2},{4,7},{5,4},{6,5},{7,6},{8,11},{9,8},{10,9... | collective-permute-start | bytes 374792 | tf_op jit(solution)/shard_map/ppermute | solution.py:303
  84.3 0.6 collective-permute-start.10
  84.9 2.8 %collective-permute-start.11 = (f32[64,488]{1,0:T(8,128)S(1)}, f32[64,488]{1,0:T(8,128)S(1)}, u32[]{:S(2)}, u32[]{:S(2)}) collective-permute-start(f32[64,488]{1,0:T(8,128)S(1)} %get-tuple-element.76), channel_id=1, source_target_pairs={{0,3},{1,0},{2,1},{3,2},{4,7},{5,4},{6,5},{7,6},{8,11},{9,8},{10,9... | collective-permute-start | bytes 374792 | tf_op jit(solution)/shard_map/ppermute | solution.py:303
  87.8 2.0 %collective-permute-done.7 = f32[64,488]{1,0:T(8,128)S(1)} collective-permute-done((f32[64,488]{1,0:T(8,128)S(1)}, f32[64,488]{1,0:T(8,128)S(1)}, u32[]{:S(2)}, u32[]{:S(2)}) %collective-permute-start.7) | collective-permute-done | bytes 124960 | tf_op jit(solution)/shard_map/ppermute | solution.py:303
  89.9 2.7 %collective-permute-start.13 = (f32[64,488]{1,0:T(8,128)S(1)}, f32[64,488]{1,0:T(8,128)S(1)}, u32[]{:S(2)}, u32[]{:S(2)}) collective-permute-start(f32[64,488]{1,0:T(8,128)S(1)} %get-tuple-element.80), channel_id=1, source_target_pairs={{0,2},{1,3},{2,0},{3,1},{4,6},{5,7},{6,4},{7,5},{8,10},{9,11},{10,... | collective-permute-start | bytes 374792 | tf_op jit(solution)/shard_map/ppermute | solution.py:303
  92.6 9.4 %shard_map.119 = f32[256,488]{1,0:T(8,128)S(1)} custom-call(s32[16,1024]{1,0:T(8,128)S(1)} %pad.58.slot_ref, bf16[1792,488]{1,0:T(8,128)(2,1)S(1)} %slice_dynamic-update-slice_fusion.6.buf_ref, bf16[10,488,488]{2,1,0:T(8,128)(2,1)} %k_ref.9, bf16[128,488]{1,0:T(8,128)(2,1)S(1)} %get-tuple-element.70.rest_0_, bf16[128,488]{1,0:T(8,128)(2,1)S(1)} %get-tuple-element.71.rest_1_, ...), custom_call_target="tpu_custom_call" | custom-call | flops 4737269760 | bytes 6511872 | tf_op jit(solution)/shard_map/pallas_call | solution.py:113
  102.1 1.0 collective-permute-start.14
  103.1 1.1 collective-permute-start.15
  104.2 1.6 %collective-permute-start.16 = (f32[64,488]{1,0:T(8,128)S(1)}, f32[64,488]{1,0:T(8,128)S(1)}, u32[]{:S(2)}, u32[]{:S(2)}) collective-permute-start(f32[64,488]{1,0:T(8,128)S(1)} %get-tuple-element.83), channel_id=1, source_target_pairs={{0,2},{1,3},{2,0},{3,1},{4,6},{5,7},{6,4},{7,5},{8,10},{9,11},{10,... | collective-permute-start | bytes 374792 | tf_op jit(solution)/shard_map/ppermute | solution.py:303
  105.8 2.6 %collective-permute-start.17 = (f32[64,488]{1,0:T(8,128)S(1)}, f32[64,488]{1,0:T(8,128)S(1)}, u32[]{:S(2)}, u32[]{:S(2)}) collective-permute-start(f32[64,488]{1,0:T(8,128)S(1)} %get-tuple-element.82), channel_id=1, source_target_pairs={{0,3},{1,0},{2,1},{3,2},{4,7},{5,4},{6,5},{7,6},{8,11},{9,8},{10,9... | collective-permute-start | bytes 374792 | tf_op jit(solution)/shard_map/ppermute | solution.py:303
  108.5 0.8 collective-permute-done.15
  109.3 1.4 %collective-permute-done.16 = f32[64,488]{1,0:T(8,128)S(1)} collective-permute-done((f32[64,488]{1,0:T(8,128)S(1)}, f32[64,488]{1,0:T(8,128)S(1)}, u32[]{:S(2)}, u32[]{:S(2)}) %collective-permute-start.16) | collective-permute-done | bytes 124960 | tf_op jit(solution)/shard_map/ppermute | solution.py:303
  110.7 0.9 collective-permute-done.17
  111.6 0.3 copy.277
  111.9 1.0 copy.253
  (104 shorter events, 2.7 us)
Async XLA Ops:
  3.3 2.1 %copy-start = (bf16[8,488,488]{2,1,0:T(8,128)(2,1)S(1)}, bf16[8,488,488]{2,1,0:T(8,128)(2,1)}, u32[]{:S(2)}) copy-start(bf16[8,488,488]{2,1,0:T(8,128)(2,1)} %rest_2_.5) | copy-start | bytes 11430916
  5.4 3.3 %copy-start.1 = (s32[1,10,1024]{2,0,1:T(1,128)S(1)}, s32[1,10,1024]{2,0,1:T(1,128)}, u32[]{:S(2)}) copy-start(s32[1,10,1024]{2,0,1:T(1,128)} %param.15) | copy-start | bytes 122884
  5.4 3.3 %copy-start.2 = (s32[1,10,1024]{2,0,1:T(1,128)S(1)}, s32[1,10,1024]{2,0,1:T(1,128)}, u32[]{:S(2)}) copy-start(s32[1,10,1024]{2,0,1:T(1,128)} %param.14) | copy-start | bytes 122884
  5.4 3.4 %copy-start.3 = (s32[1,10]{1,0:T(1,128)S(1)}, s32[1,10]{1,0:T(1,128)}, u32[]{:S(2)}) copy-start(s32[1,10]{1,0:T(1,128)} %param.16) | copy-start | bytes 124
  5.4 4.7 %copy-start.4 = (s32[1,10,128]{2,0,1:T(1,128)S(1)}, s32[1,10,128]{2,0,1:T(1,128)}, u32[]{:S(2)}) copy-start(s32[1,10,128]{2,0,1:T(1,128)} %param.18) | copy-start | bytes 15364
  5.4 4.7 %copy-start.6 = (s32[1,10]{1,0:T(1,128)S(1)}, s32[1,10]{1,0:T(1,128)}, u32[]{:S(2)}) copy-start(s32[1,10]{1,0:T(1,128)} %param.19) | copy-start | bytes 124
  5.4 4.8 %copy-start.5 = (s32[1,10,128]{2,0,1:T(1,128)S(1)}, s32[1,10,128]{2,0,1:T(1,128)}, u32[]{:S(2)}) copy-start(s32[1,10,128]{2,0,1:T(1,128)} %param.17) | copy-start | bytes 15364
  9.6 1.7 %collective-permute-start = (bf16[80,488]{1,0:T(8,128)(2,1)S(1)}, bf16[80,488]{1,0:T(8,128)(2,1)S(1)}, u32[]{:S(2)}, u32[]{:S(2)}) collective-permute-start(bf16[80,488]{1,0:T(8,128)(2,1)S(1)} %gather_fusion), channel_id=1, source_target_pairs={{0,4},{4,0},{8,12},{12,8},{16,20},{20,16},{24,28},{28,24},{32,36},... | collective-permute-start | bytes 234248 | tf_op jit(solution)/shard_map/ppermute | solution.py:18
  12.3 4.9 %collective-permute-start.1 = (bf16[80,488]{1,0:T(8,128)(2,1)S(1)}, bf16[80,488]{1,0:T(8,128)(2,1)S(1)}, u32[]{:S(2)}, u32[]{:S(2)}) collective-permute-start(bf16[80,488]{1,0:T(8,128)(2,1)S(1)} %gather_fusion.1), channel_id=1, source_target_pairs={{0,8},{8,0},{4,12},{12,4},{16,24},{24,16},{20,28},{28,20},{32,40},... | collective-permute-start | bytes 234248 | tf_op jit(solution)/shard_map/ppermute | solution.py:18
  18.1 6.0 %collective-permute-start.2 = (bf16[80,488]{1,0:T(8,128)(2,1)S(1)}, bf16[80,488]{1,0:T(8,128)(2,1)S(1)}, u32[]{:S(2)}, u32[]{:S(2)}) collective-permute-start(bf16[80,488]{1,0:T(8,128)(2,1)S(1)} %gather_fusion.2), channel_id=1, source_target_pairs={{0,16},{16,0},{4,20},{20,4},{8,24},{24,8},{12,28},{28,12},{32,48},... | collective-permute-start | bytes 234248 | tf_op jit(solution)/shard_map/ppermute | solution.py:18
  25.0 4.5 %collective-permute-start.3 = (bf16[80,488]{1,0:T(8,128)(2,1)S(1)}, bf16[80,488]{1,0:T(8,128)(2,1)S(1)}, u32[]{:S(2)}, u32[]{:S(2)}) collective-permute-start(bf16[80,488]{1,0:T(8,128)(2,1)S(1)} %gather_fusion.3), channel_id=1, source_target_pairs={{0,32},{32,0},{4,36},{36,4},{8,40},{40,8},{12,44},{44,12},{16,48},... | collective-permute-start | bytes 234248 | tf_op jit(solution)/shard_map/ppermute | solution.py:18
  30.5 5.8 %collective-permute-start.4 = (bf16[80,488]{1,0:T(8,128)(2,1)S(1)}, bf16[80,488]{1,0:T(8,128)(2,1)S(1)}, u32[]{:S(2)}, u32[]{:S(2)}) collective-permute-start(bf16[80,488]{1,0:T(8,128)(2,1)S(1)} %gather_fusion.4), channel_id=1, source_target_pairs={{0,64},{64,0},{4,68},{68,4},{8,72},{72,8},{12,76},{76,12},{16,80},... | collective-permute-start | bytes 234248 | tf_op jit(solution)/shard_map/ppermute | solution.py:18
  37.0 10.4 %collective-permute-start.5 = (bf16[80,488]{1,0:T(8,128)(2,1)S(1)}, bf16[80,488]{1,0:T(8,128)(2,1)S(1)}, u32[]{:S(2)}, u32[]{:S(2)}) collective-permute-start(bf16[80,488]{1,0:T(8,128)(2,1)S(1)} %gather_fusion.5), channel_id=1, source_target_pairs={{0,128},{128,0},{4,132},{132,4},{8,136},{136,8},{12,140},{140,12},... | collective-permute-start | bytes 234248 | tf_op jit(solution)/shard_map/ppermute | solution.py:18
  78.6 9.2 %collective-permute-start.6 = (f32[64,488]{1,0:T(8,128)S(1)}, f32[64,488]{1,0:T(8,128)S(1)}, u32[]{:S(2)}, u32[]{:S(2)}) collective-permute-start(f32[64,488]{1,0:T(8,128)S(1)} %get-tuple-element.84), channel_id=1, source_target_pairs={{0,1},{1,2},{2,3},{3,0},{4,5},{5,6},{6,7},{7,4},{8,9},{9,10},{10,1... | collective-permute-start | bytes 374792 | tf_op jit(solution)/shard_map/ppermute | solution.py:303
  80.1 9.7 %collective-permute-start.7 = (f32[64,488]{1,0:T(8,128)S(1)}, f32[64,488]{1,0:T(8,128)S(1)}, u32[]{:S(2)}, u32[]{:S(2)}) collective-permute-start(f32[64,488]{1,0:T(8,128)S(1)} %get-tuple-element.86), channel_id=1, source_target_pairs={{0,2},{1,3},{2,0},{3,1},{4,6},{5,7},{6,4},{7,5},{8,10},{9,11},{10,... | collective-permute-start | bytes 374792 | tf_op jit(solution)/shard_map/ppermute | solution.py:303
  82.9 7.0 %collective-permute-start.8 = (f32[64,488]{1,0:T(8,128)S(1)}, f32[64,488]{1,0:T(8,128)S(1)}, u32[]{:S(2)}, u32[]{:S(2)}) collective-permute-start(f32[64,488]{1,0:T(8,128)S(1)} %get-tuple-element.85), channel_id=1, source_target_pairs={{0,3},{1,0},{2,1},{3,2},{4,7},{5,4},{6,5},{7,6},{8,11},{9,8},{10,9... | collective-permute-start | bytes 374792 | tf_op jit(solution)/shard_map/ppermute | solution.py:303
  84.3 17.7 %collective-permute-start.10 = (f32[64,488]{1,0:T(8,128)S(1)}, f32[64,488]{1,0:T(8,128)S(1)}, u32[]{:S(2)}, u32[]{:S(2)}) collective-permute-start(f32[64,488]{1,0:T(8,128)S(1)} %get-tuple-element.77), channel_id=1, source_target_pairs={{0,2},{1,3},{2,0},{3,1},{4,6},{5,7},{6,4},{7,5},{8,10},{9,11},{10,... | collective-permute-start | bytes 374792 | tf_op jit(solution)/shard_map/ppermute | solution.py:303
  84.9 18.2 %collective-permute-start.11 = (f32[64,488]{1,0:T(8,128)S(1)}, f32[64,488]{1,0:T(8,128)S(1)}, u32[]{:S(2)}, u32[]{:S(2)}) collective-permute-start(f32[64,488]{1,0:T(8,128)S(1)} %get-tuple-element.76), channel_id=1, source_target_pairs={{0,3},{1,0},{2,1},{3,2},{4,7},{5,4},{6,5},{7,6},{8,11},{9,8},{10,9... | collective-permute-start | bytes 374792 | tf_op jit(solution)/shard_map/ppermute | solution.py:303
  87.7 16.4 %collective-permute-start.9 = (f32[64,488]{1,0:T(8,128)S(1)}, f32[64,488]{1,0:T(8,128)S(1)}, u32[]{:S(2)}, u32[]{:S(2)}) collective-permute-start(f32[64,488]{1,0:T(8,128)S(1)} %get-tuple-element.75), channel_id=1, source_target_pairs={{0,1},{1,2},{2,3},{3,0},{4,5},{5,6},{6,7},{7,4},{8,9},{9,10},{10,1... | collective-permute-start | bytes 374792 | tf_op jit(solution)/shard_map/ppermute | solution.py:303
  89.9 15.9 %collective-permute-start.12 = (f32[64,488]{1,0:T(8,128)S(1)}, f32[64,488]{1,0:T(8,128)S(1)}, u32[]{:S(2)}, u32[]{:S(2)}) collective-permute-start(f32[64,488]{1,0:T(8,128)S(1)} %get-tuple-element.78), channel_id=1, source_target_pairs={{0,1},{1,2},{2,3},{3,0},{4,5},{5,6},{6,7},{7,4},{8,9},{9,10},{10,1... | collective-permute-start | bytes 374792 | tf_op jit(solution)/shard_map/ppermute | solution.py:303
  89.9 18.6 %collective-permute-start.13 = (f32[64,488]{1,0:T(8,128)S(1)}, f32[64,488]{1,0:T(8,128)S(1)}, u32[]{:S(2)}, u32[]{:S(2)}) collective-permute-start(f32[64,488]{1,0:T(8,128)S(1)} %get-tuple-element.80), channel_id=1, source_target_pairs={{0,2},{1,3},{2,0},{3,1},{4,6},{5,7},{6,4},{7,5},{8,10},{9,11},{10,... | collective-permute-start | bytes 374792 | tf_op jit(solution)/shard_map/ppermute | solution.py:303
  102.1 6.4 %collective-permute-start.14 = (f32[64,488]{1,0:T(8,128)S(1)}, f32[64,488]{1,0:T(8,128)S(1)}, u32[]{:S(2)}, u32[]{:S(2)}) collective-permute-start(f32[64,488]{1,0:T(8,128)S(1)} %get-tuple-element.79), channel_id=1, source_target_pairs={{0,3},{1,0},{2,1},{3,2},{4,7},{5,4},{6,5},{7,6},{8,11},{9,8},{10,9... | collective-permute-start | bytes 374792 | tf_op jit(solution)/shard_map/ppermute | solution.py:303
  103.1 6.2 %collective-permute-start.15 = (f32[64,488]{1,0:T(8,128)S(1)}, f32[64,488]{1,0:T(8,128)S(1)}, u32[]{:S(2)}, u32[]{:S(2)}) collective-permute-start(f32[64,488]{1,0:T(8,128)S(1)} %get-tuple-element.81), channel_id=1, source_target_pairs={{0,1},{1,2},{2,3},{3,0},{4,5},{5,6},{6,7},{7,4},{8,9},{9,10},{10,1... | collective-permute-start | bytes 374792 | tf_op jit(solution)/shard_map/ppermute | solution.py:303
  104.2 6.5 %collective-permute-start.16 = (f32[64,488]{1,0:T(8,128)S(1)}, f32[64,488]{1,0:T(8,128)S(1)}, u32[]{:S(2)}, u32[]{:S(2)}) collective-permute-start(f32[64,488]{1,0:T(8,128)S(1)} %get-tuple-element.83), channel_id=1, source_target_pairs={{0,2},{1,3},{2,0},{3,1},{4,6},{5,7},{6,4},{7,5},{8,10},{9,11},{10,... | collective-permute-start | bytes 374792 | tf_op jit(solution)/shard_map/ppermute | solution.py:303
  105.8 5.7 %collective-permute-start.17 = (f32[64,488]{1,0:T(8,128)S(1)}, f32[64,488]{1,0:T(8,128)S(1)}, u32[]{:S(2)}, u32[]{:S(2)}) collective-permute-start(f32[64,488]{1,0:T(8,128)S(1)} %get-tuple-element.82), channel_id=1, source_target_pairs={{0,3},{1,0},{2,1},{3,2},{4,7},{5,4},{6,5},{7,6},{8,11},{9,8},{10,9... | collective-permute-start | bytes 374792 | tf_op jit(solution)/shard_map/ppermute | solution.py:303
